TPU v7x, 768 devices: a whole 4x8x12 slice. The times are simulated.
768 devices in a mesh: region: 24 (over z, core), aux: 32 (over x, y).
Axes of the slice: x: 4, y: 8, z: 12, core: 2. Of those that a mesh axis runs over, the one named last changes fastest.
Arguments:
- occ_tiles: bfloat16 [384, 128, 128], P('region'), may hold values from -0.5 to 0.5
- vir_tiles: bfloat16 [384, 128, 128], P('region'), may hold values from -0.5 to 0.5
- three_index: bfloat16 [48, 64, 128, 128], P('region', 'aux'), may hold values from -6 to 6
- send_lists: int32 [24, 2, 48], P('region'), may hold values from 0 to 15
- term_pairs: int32 [24, 128, 2], P('region'), may hold values from 0 to 1
- term_tiles: int32 [24, 128, 2], P('region'), may hold values from 0 to 47
- term_count: int32 [24], P('region'), may hold values from 1 to 128, 1536 in all
- z_pattern: int32 [32, 32], P('aux'), may hold values 0 or 1
- laplace_point: int32 [1], replicated, may hold values from 0 to 7
Outputs:
- z_block: float32 [64, 64], P('aux')
Inputs may be any that keep to these rules, and one draw needn't show every extreme that they name: `term_count`: the largest count is exactly 128; the counts sum to 1536.
All inputs are finite; a program needn't handle non-finite values. No bound on the sum of `term_count` or of `z_pattern` on one device may be relied on, other than what follows from the above.
Results may differ from a plain program's by a relative error of at most 0.0041.
Values may be sent and summed in bfloat16 or wider, within the bound.
No kernel may reach another device: no remote copies, remote signals or barrier semaphores. Data moves between devices by JAX's collectives and lax.ppermute only.
A program may use at most 32 MiB of HBM per device.

v0:
```python
import jax
import jax.numpy as jnp
from jax import lax
from jax.sharding import PartitionSpec as P


def per_device(
    occ_tiles,
    vir_tiles,
    three_index,
    send_lists,
    term_pairs,
    term_tiles,
    term_count,
    z_pattern,
    laplace_point,
):
    regions = lax.axis_size("region")
    width = occ_tiles.shape[1]
    per_aux = three_index.shape[1]
    npairs = three_index.shape[0]
    nterms = term_pairs.shape[1]
    picks = send_lists[0]
    outgoing = jnp.stack(
        [jnp.take(occ_tiles, picks[0], axis=0), jnp.take(vir_tiles, picks[1], axis=0)]
    )
    incoming = lax.all_to_all(outgoing, "region", split_axis=1, concat_axis=1, tiled=True)
    occ_recv = incoming[0]
    vir_recv = incoming[1]
    pairs = term_pairs[0]
    tiles = term_tiles[0]
    count = term_count[0]
    block_len = 8

    def step(index, acc):
        start = index * block_len
        pair_blk = lax.dynamic_slice_in_dim(pairs, start, block_len, 0)
        tile_blk = lax.dynamic_slice_in_dim(tiles, start, block_len, 0)
        live = start + jnp.arange(block_len, dtype=jnp.int32) < count
        occ = jnp.take(occ_recv, tile_blk[:, 0], axis=0)
        vir = jnp.take(vir_recv, tile_blk[:, 1], axis=0)
        source = jnp.take(three_index, pair_blk[:, 1], axis=0)
        half = jnp.einsum("tij,tpjk->tpik", occ, source, preferred_element_type=jnp.float32).astype(
            jnp.bfloat16
        )
        second = jnp.einsum("tpik,tkl->tpil", half, vir, preferred_element_type=jnp.float32)
        added = jnp.stack(
            [
                jnp.sum(
                    jnp.where(
                        ((pair_blk[:, 0] == target_pair) & live)[:, None, None, None], second, 0.0
                    ),
                    axis=0,
                )
                for target_pair in range(npairs)
            ]
        )
        return acc + added

    blocks_live = (count + block_len - 1) // block_len
    acc = lax.fori_loop(
        0, blocks_live, step, jnp.zeros((npairs, per_aux, width, width), jnp.float32)
    )
    wide = acc.astype(jnp.bfloat16)
    mask_row = jnp.repeat(z_pattern[0], per_aux).astype(jnp.float32)
    weight = 0.5 + 0.125 * laplace_point[0].astype(jnp.float32)
    scale = weight / (width * jnp.sqrt(jnp.float32(regions * nterms)))
    contrib = jnp.einsum(
        "npij,nqij->pq",
        three_index,
        lax.all_gather(wide, "aux", axis=1, tiled=True),
        preferred_element_type=jnp.float32,
    )
    summed = lax.psum(contrib, "region")
    return summed * mask_row[None, :] * scale


def solution(mesh):
    in_specs = (
        P("region", None, None),
        P("region", None, None),
        P("region", "aux", None, None),
        P("region", None, None),
        P("region", None, None),
        P("region", None, None),
        P("region"),
        P("aux", None),
        P(),
    )
    out_specs = P("aux", None)
    return jax.shard_map(
        per_device, mesh=mesh, in_specs=in_specs, out_specs=out_specs, check_vma=False
    )
```

profile of v0, /device:TPU:1, one launch (start us, length us, event | category | flops | bytes accessed | tf_op | source)
XLA Modules:
  0.0 419.7 jit_solution(6271171949738585449)
XLA Ops:
  6.5 0.0 copy-start
  6.5 0.8 compare_and_fusion.3
  7.3 0.3 copy-done
  7.6 0.0 copy-start.2
  7.6 0.8 gather_fusion.3
  8.5 0.2 copy-done.2
  8.7 1.9 gather_fusion.4
  10.6 1.8 select_bitcast_fusion
  12.4 2.0 pad_maximum_fusion
  14.3 16.7 %all-to-all-start = ((bf16[2,48,128,128]{3,2,0,1:T(8,128)(2,1)}), bf16[2,48,128,128]{3,2,0,1:T(8,128)(2,1)}, u32[]{:S(2)}, u32[]{:S(2)}) async-start(bf16[2,48,128,128]{3,2,0,1:T(8,128)(2,1)} %pad_maximum_fusion), calls=%async_computation | async-start | bytes 6291456 | tf_op jit(solution)/shard_map/all_to_all | solution.py:27
  31.1 0.0 all-gather.2.cloned.1.call-start
  31.8 0.0 copy-start.1
  31.8 0.0 copy-start.3
  31.8 0.0 copy-start.4
  31.8 106.2 %all-to-all-done = bf16[2,48,128,128]{3,2,0,1:T(8,128)(2,1)} async-done(((bf16[2,48,128,128]{3,2,0,1:T(8,128)(2,1)}), bf16[2,48,128,128]{3,2,0,1:T(8,128)(2,1)}, u32[]{:S(2)}, u32[]{:S(2)}) %all-to-all-start) | async-done | bytes 3145760 | tf_op jit(solution)/shard_map/all_to_all | solution.py:27
  138.1 3.4 slice_bitcast_fusion
  141.4 0.0 copy-done.1
  141.5 0.0 copy-done.3
  141.5 0.0 copy-done.4
  141.5 8.6 %while.10 = (s32[]{:T(128)}, f32[2,2,128,128]{3,2,1,0:T(8,128)S(1)}, s32[]{:T(128)}, s32[128,2]{0,1:T(2,128)S(1)}, s32[]{:T(128)}, /*index=5*/bf16[2,2,128,128]{...) while((s32[]{:T(128)}, ...), condition=%wide.region_3.6_spmd, body=%wide.region_0.5_spmd.sunk | while | flops 136121568 | bytes 4207559 | solution.py:61
  141.5 0.1 constant_dynamic-slice_fusion.3
  141.6 1.2 bitcast_and_fusion.3
  142.8 0.6 compare_and_fusion.5
  143.4 0.6 gather_fusion
  144.0 2.0 gather_fusion.2
  146.1 0.6 gather_fusion.1
  146.7 2.1 select_reduce_fusion.3
  148.8 1.0 maximum_add_fusion.2
  150.0 0.7 copy.31
  150.7 0.0 all-gather.2.cloned.1.call-update
  150.7 0.7 convert_bitcast_fusion
  151.4 0.1 broadcast_in_dim.56
  151.5 0.1 convert_element_type.30
  152.2 210.5 %all-gather.2.cloned.1.call-done = bf16[2,64,128,128]{3,2,0,1:T(8,128)(2,1)} async-done(((bf16[2,2,128,128]{3,2,0,1:T(8,128)(2,1)}), bf16[2,64,128,128]{3,2,0,1:T(8,128)(2,1)}) %all-gather.2.cloned.1.call-update) | async-done | bytes 4194320 | tf_op jit(solution)/shard_map/all_gather | solution.py:71
  362.7 10.6 %fusion.24 = f32[2,64]{1,0:T(2,128)S(1)} fusion(bf16[2,64,128,128]{3,2,0,1:T(8,128)(2,1)} %all-gather.2.cloned.1.call-done, bf16[2,2,128,128]{3,2,1,0:T(8,128)(2,1)S(1)} %get-tuple-element.212), kind=kOutput, calls=%fused_computation.44 | convolution fusion | flops 8388608 | bytes 4325888 | tf_op jit(solution)/shard_map/npij,nqij->pq/dot_general | solution.py:68
  373.3 39.0 %psum.7 = f32[2,64]{1,0:T(2,128)S(1)} all-reduce(f32[2,64]{1,0:T(2,128)S(1)} %fusion.24), channel_id=1, replica_groups=mesh['region'=24,'aux'=32] {'region'}, use_global_device_ids=true, to_apply=%region_4.7 | all-reduce | flops 128 | bytes 1024 | tf_op jit(solution)/shard_map/psum | solution.py:74
  412.3 0.6 multiply_multiply_fusion
  (8 shorter events, 0.1 us)
Async XLA Ops:
  6.5 1.1 copy-start
  7.6 1.0 copy-start.2
  14.3 123.7 %all-to-all-start = ((bf16[2,48,128,128]{3,2,0,1:T(8,128)(2,1)}), bf16[2,48,128,128]{3,2,0,1:T(8,128)(2,1)}, u32[]{:S(2)}, u32[]{:S(2)}) async-start(bf16[2,48,128,128]{3,2,0,1:T(8,128)(2,1)} %pad_maximum_fusion), calls=%async_computation | async-start | bytes 6291456 | tf_op jit(solution)/shard_map/all_to_all | solution.py:27
  31.1 331.6 %all-gather.2.cloned.1.call-start = ((), (), s32[]{:S(2)}) async-start(), calls=%async_computation.1 | async-start | bytes 4325376 | tf_op jit(solution)/shard_map/all_gather | solution.py:71
  31.8 109.7 %copy-start.1 = (bf16[2,2,128,128]{3,2,1,0:T(8,128)(2,1)S(1)}, bf16[2,2,128,128]{3,2,1,0:T(8,128)(2,1)}, u32[]{:S(2)}) copy-start(bf16[2,2,128,128]{3,2,1,0:T(8,128)(2,1)} %param.17) | copy-start | bytes 393220
  31.8 109.7 %copy-start.3 = (s32[1,128,2]{1,2,0:T(2,128)S(1)}, s32[1,128,2]{1,2,0:T(2,128)}, u32[]{:S(2)}) copy-start(s32[1,128,2]{1,2,0:T(2,128)} %param.19) | copy-start | bytes 3076
  31.8 109.7 %copy-start.4 = (s32[1,128,2]{1,2,0:T(2,128)S(1)}, s32[1,128,2]{1,2,0:T(2,128)}, u32[]{:S(2)}) copy-start(s32[1,128,2]{1,2,0:T(2,128)} %param.20) | copy-start | bytes 3076
Sparse Core Ops, SparseCore 0:
  150.8 211.8 all-gather.1
where the time goes:
time: 421 us; the launch traced here: 420 us
  waiting for transfers between devices  317 us (75%)
  blocking collectives  39 us (9%)
  starting transfers between devices  16.8 us (4%)
  between operations  14.8 us (4%)
  matrix products  12.6 us (3%)
  local copies, waits for them, and re-layouts  10.8 us (3%)
  other arithmetic  8.61 us (2%)
    all_gather x1, waiting for transfers between devices, per_device(): lax.all_gather(wide, 'aux', axis=1, tiled=True)  210 us
    all_to_all x1, waiting for transfers between devices, per_device(): lax.all_to_all(outgoing, 'region', split_axis=1, concat_axis=1, tiled=True)  106 us
    psum x1, blocking collectives, per_device(): summed = lax.psum(contrib, 'region')  39 us
    all_to_all x1, starting transfers between devices, per_device(): lax.all_to_all(outgoing, 'region', split_axis=1, concat_axis=1, tiled=True)  16.7 us
    dot_general x1, matrix products, per_device(): jnp.einsum('npij,nqij->pq', three_index, lax.all_gather(wide, 'aux', axis...  10.6 us
  transfers between devices with their start and end apart: 2, of which 2 were waited for; matrix products, arithmetic and copies ran while one was open for 0% of the time, Pallas kernels for 0%

commit v1 on v0

v1 whole, which is shorter than its diff:
```python
import jax
import jax.numpy as jnp
from jax import lax
from jax.experimental import pallas as pl
from jax.experimental.pallas import tpu as pltpu
from jax.sharding import PartitionSpec as P

NX = 4
NY = 8
NI = 4
NL = 2
WIDTH = 128
IB = WIDTH // NI
LB = WIDTH // NL
Y_GROUPS = [[x * NY + y for y in range(NY)] for x in range(NX)]
X_GROUPS = [[x * NY + y for x in range(NX)] for y in range(NY)]


def pick_kernel(spots, lists, occ, vir, out):
    row = spots[0] * IB
    col = spots[1] * LB
    r = lax.broadcasted_iota(jnp.int32, (2 * WIDTH, WIDTH), 0)
    c = lax.broadcasted_iota(jnp.int32, (2 * WIDTH, WIDTH), 1)
    wanted = jnp.where(c < LB, c + col, c - LB + WIDTH + col)
    select = jnp.where(r == wanted, 1.0, 0.0).astype(jnp.bfloat16)
    for d in range(out.shape[0]):
        for j in range(2):
            out[d, j * IB : (j + 1) * IB, :] = occ[lists[0, 2 * d + j], pl.ds(pl.multiple_of(row, IB), IB), :]
        pair = jnp.concatenate([vir[lists[1, 2 * d]], vir[lists[1, 2 * d + 1]]], axis=1)
        out[d, 2 * IB :, :] = jnp.dot(pair, select, preferred_element_type=jnp.float32).astype(
            jnp.bfloat16
        )


def pick(spots, lists, occ, vir, regions):
    smem = pl.BlockSpec(memory_space=pltpu.SMEM)
    vmem = pl.BlockSpec(memory_space=pltpu.VMEM)
    return pl.pallas_call(
        pick_kernel,
        out_shape=jax.ShapeDtypeStruct((regions, 2 * IB + WIDTH, WIDTH), jnp.bfloat16),
        in_specs=[smem, smem, vmem, vmem],
        out_specs=vmem,
        compiler_params=pltpu.CompilerParams(vmem_limit_bytes=16 << 20),
        cost_estimate=pl.CostEstimate(flops=2 * 24 * 128 * 256 * 128, bytes_accessed=3 << 20, transcendentals=0),
    )(spots, lists, occ, vir)


CHUNK = 4


def transform_kernel(pairs, tiles, count, recv, bq, bp, out, half, acc, wide, order, number):
    regions = recv.shape[0]
    nq = bq.shape[0] * bq.shape[2]
    rows = nq * IB
    number[0] = 0
    number[1] = 0

    def place(t, carry):
        p = pairs[t, 0]
        n = number[p]
        order[p, 0, n] = pairs[t, 1] * (2 * regions) + tiles[t, 0]
        order[p, 1, n] = tiles[t, 1]
        number[p] = n + 1
        return carry

    lax.fori_loop(0, count[0], place, 0)

    group = 4

    def first(step, carry):
        q = step // bq.shape[0]
        y = step % bq.shape[0]
        source = jnp.concatenate([bq[y, q, 0], bq[y, q, 1]], axis=1)
        for s in range(0, regions, group):
            occ = recv[s : s + group, 0 : 2 * IB, :].reshape(group * 2 * IB, WIDTH)
            res = jnp.dot(occ, source, preferred_element_type=jnp.float32).astype(jnp.bfloat16)
            for u in range(2 * group):
                for f in range(2):
                    start = pl.multiple_of((y * 2 + f) * IB, IB)
                    half[q * (2 * regions) + 2 * s + u, pl.ds(start, IB), :] = res[
                        u * IB : (u + 1) * IB, f * WIDTH : (f + 1) * WIDTH
                    ]
        return carry

    lax.fori_loop(0, 2 * bq.shape[0], first, 0)

    lane = lax.broadcasted_iota(jnp.int32, (WIDTH, WIDTH), 1)
    for p in range(2):
        acc[p] = jnp.zeros((rows, WIDTH), jnp.float32)
        live = number[p]

        def second(step, carry, p=p, live=live):
            lhs = []
            rhs = []
            for u in range(CHUNK):
                t = step * CHUNK + u
                at = jnp.minimum(t, live - 1)
                b = order[p, 1, at]
                side = jnp.where(t < live, b % 2, 2)
                lhs.append(half[order[p, 0, at]])
                tile = recv[b // 2, 2 * IB :, :]
                rhs.append(jnp.where(lane // LB == side, tile, jnp.zeros_like(tile)))
            acc[p] += jnp.dot(
                jnp.concatenate(lhs, axis=1),
                jnp.concatenate(rhs, axis=0),
                preferred_element_type=jnp.float32,
            )
            return carry

        lax.fori_loop(0, (live + CHUNK - 1) // CHUNK, second, 0)
    low = acc[0]
    high = acc[1]
    lanes = lax.broadcasted_iota(jnp.int32, (rows, WIDTH), 1)
    wide[...] = jnp.where(
        lanes < LB, low + pltpu.roll(low, LB, 1), high + pltpu.roll(high, LB, 1)
    )
    flat = jnp.concatenate(
        [wide[pl.ds(i, nq, stride=IB), :].astype(jnp.bfloat16) for i in range(IB)], axis=1
    )
    out[...] = lax.dot_general(
        bp[...], flat, (((1,), (1,)), ((), ())), preferred_element_type=jnp.float32
    )


def transform(pairs, tiles, count, recv, bq, bp):
    smem = pl.BlockSpec(memory_space=pltpu.SMEM)
    vmem = pl.BlockSpec(memory_space=pltpu.VMEM)
    regions = recv.shape[0]
    nterms = pairs.shape[0]
    nq = bq.shape[0] * bq.shape[2]
    return pl.pallas_call(
        transform_kernel,
        out_shape=jax.ShapeDtypeStruct((bp.shape[0], nq), jnp.float32),
        in_specs=[smem, smem, smem, vmem, vmem, vmem],
        out_specs=vmem,
        scratch_shapes=[
            pltpu.VMEM((4 * regions, nq * IB, WIDTH), jnp.bfloat16),
            pltpu.VMEM((2, nq * IB, WIDTH), jnp.float32),
            pltpu.VMEM((nq * IB, WIDTH), jnp.float32),
            pltpu.SMEM((2, 2, nterms), jnp.int32),
            pltpu.SMEM((2,), jnp.int32),
        ],
        compiler_params=pltpu.CompilerParams(vmem_limit_bytes=40 << 20),
        cost_estimate=pl.CostEstimate(flops=4 << 30, bytes_accessed=4 << 20, transcendentals=0),
    )(pairs, tiles, count, recv, bq, bp)


def per_device(
    occ_tiles,
    vir_tiles,
    three_index,
    send_lists,
    term_pairs,
    term_tiles,
    term_count,
    z_pattern,
    laplace_point,
):
    regions = lax.axis_size("region")
    naux = lax.axis_size("aux")
    width = occ_tiles.shape[1]
    per_aux = three_index.shape[1]
    nterms = term_pairs.shape[1]
    nall = naux * per_aux
    aux = lax.axis_index("aux")
    x = aux // NY
    y = aux % NY
    spots = jnp.stack([y // NL, y % NL]).astype(jnp.int32)

    outgoing = pick(spots, send_lists[0], occ_tiles, vir_tiles, regions)
    recv = lax.all_to_all(outgoing, "region", 0, 0, tiled=True)

    bq = lax.all_gather(three_index, "aux", axis=0, tiled=False, axis_index_groups=Y_GROUPS)
    rows = lax.dynamic_slice_in_dim(bq, (y // NL) * IB, IB, 3)
    part = lax.dynamic_slice_in_dim(rows, (y % NL) * LB, LB, 4)
    part = jnp.concatenate([part[:, 0], part[:, 1]], axis=3)
    part = part.reshape(NY * per_aux, IB * WIDTH)
    bp = lax.all_gather(part, "aux", axis=0, tiled=True, axis_index_groups=X_GROUPS)

    partial = transform(term_pairs[0], term_tiles[0], term_count, recv, bq, bp)

    outs = partial.reshape(naux, per_aux, -1)
    spread = lax.all_to_all(outs, "aux", 0, 0, tiled=True)
    mine = jnp.sum(spread.reshape(NX, NY, per_aux, -1), axis=1)
    mine = jnp.transpose(mine, (1, 0, 2)).reshape(per_aux, nall)
    every = lax.all_to_all(
        jnp.broadcast_to(mine[None], (regions, per_aux, nall)), "region", 0, 0, tiled=True
    )
    summed = jnp.sum(every, axis=0)
    mask_row = jnp.repeat(z_pattern[0], per_aux).astype(jnp.float32)
    weight = 0.5 + 0.125 * laplace_point[0].astype(jnp.float32)
    scale = weight / (width * jnp.sqrt(jnp.float32(regions * nterms)))
    return summed * mask_row[None, :] * scale


def solution(mesh):
    in_specs = (
        P("region", None, None),
        P("region", None, None),
        P("region", "aux", None, None),
        P("region", None, None),
        P("region", None, None),
        P("region", None, None),
        P("region"),
        P("aux", None),
        P(),
    )
    out_specs = P("aux", None)
    return jax.shard_map(
        per_device, mesh=mesh, in_specs=in_specs, out_specs=out_specs, check_vma=False
    )
```

time: 421 us -> 156 us (0.37)
  waiting for transfers between devices: 317 us -> 51.1 us
  starting transfers between devices: 16.8 us -> 44.5 us
  blocking collectives: 39 us -> 25.7 us
  matrix products: 12.6 us -> 0 us
  Pallas kernels: 0 us -> 11.9 us
  other arithmetic: 8.61 us -> 1.49 us
  local copies, waits for them, and re-layouts: 10.8 us -> 5.87 us
    all_gather x1, waiting for transfers between devices: 210 us -> 41.9 us  [per_device(): lax.all_gather(three_index, 'aux', axis=0, tiled=False, axis_index_groups...]
    all_to_all x1 -> x2, waiting for transfers between devices: 106 us -> 8.55 us  [the longest x1 8.55 us: per_device(): lax.all_to_all(jnp.broadcast_to(mine[None], (regions, per_aux, nall)), 'r...]
    psum x1 -> x0, blocking collectives: 39 us -> none  [per_device(): summed = lax.psum(contrib, 'region')]
    all_to_all x1 -> x2, starting transfers between devices: 16.7 us -> 44.4 us  [the longest x1 27.6 us: per_device(): lax.all_to_all(jnp.broadcast_to(mine[None], (regions, per_aux, nall)), 'r...]
    all_to_all x0 -> x1, blocking collectives: none -> 14.7 us  [per_device(): spread = lax.all_to_all(outs, 'aux', 0, 0, tiled=True)]
    dot_general x2 -> x0, matrix products: 12.6 us -> none  [the longest x1 10.6 us: per_device(): jnp.einsum('npij,nqij->pq', three_index, lax.all_gather(wide, 'aux', axis...]
    pallas_call x0 -> x2, Pallas kernels: none -> 11.9 us  [the longest x1 9.74 us: transform(): pl.pallas_call(transform_kernel, out_shape=jax.ShapeDtypeStruct((bp.shape...]
    all_gather x0 -> x1, blocking collectives: none -> 10.9 us  [per_device(): lax.all_gather(part, 'aux', axis=0, tiled=True, axis_index_groups=X_GROUPS)]
  transfers between devices with their start and end apart: 2 -> 3, of which waited for: 2 -> 2; matrix products, arithmetic and copies ran while one was open for 0% -> 1% of each run, Pallas kernels for 0% -> 0%
where the time goes in v1:
time: 156 us; the launch traced here: 155 us
  waiting for transfers between devices  51.1 us (33%)
  starting transfers between devices  44.5 us (29%)
  blocking collectives  25.7 us (16%)
  between operations  14.8 us (9%)
  Pallas kernels  11.9 us (8%)
  local copies, waits for them, and re-layouts  5.87 us (4%)
    all_gather x1, waiting for transfers between devices, per_device(): lax.all_gather(three_index, 'aux', axis=0, tiled=False, axis_index_groups...  41.9 us
    all_to_all x1, starting transfers between devices, per_device(): lax.all_to_all(jnp.broadcast_to(mine[None], (regions, per_aux, nall)), 'r...  27.6 us
    all_to_all x1, starting transfers between devices, per_device(): recv = lax.all_to_all(outgoing, 'region', 0, 0, tiled=True)  16.8 us
    all_to_all x1, blocking collectives, per_device(): spread = lax.all_to_all(outs, 'aux', 0, 0, tiled=True)  14.7 us
    all_gather x1, blocking collectives, per_device(): lax.all_gather(part, 'aux', axis=0, tiled=True, axis_index_groups=X_GROUPS)  10.9 us
    pallas_call x1, Pallas kernels, transform(): pl.pallas_call(transform_kernel, out_shape=jax.ShapeDtypeStruct((bp.shape...  9.74 us
    all_to_all x1, waiting for transfers between devices, per_device(): lax.all_to_all(jnp.broadcast_to(mine[None], (regions, per_aux, nall)), 'r...  8.55 us
    unnamed x19, local copies, waits for them, and re-layouts  3.84 us
  transfers between devices with their start and end apart: 3, of which 2 were waited for; matrix products, arithmetic and copies ran while one was open for 1% of the time, Pallas kernels for 0%

profile of v1, /device:TPU:1, one launch (start us, length us, event | category | flops | bytes accessed | tf_op | source)
XLA Modules:
  0.0 155.3 jit_solution(3304817308415600915)
XLA Ops:
  6.5 0.1 pad_add_fusion.spots
  6.6 0.0 copy-start
  6.6 1.0 copy-done
  7.7 0.0 copy-start.1
  7.7 1.0 copy-done.1
  8.7 0.0 copy-start.3
  8.7 0.7 copy-done.3
  9.4 2.1 %shard_map.91 = bf16[24,192,128]{2,1,0:T(8,128)(2,1)} custom-call(s32[2]{0:T(128)S(1)} %pad_add_fusion.spots, s32[2,48]{1,0:T(2,128)S(1)} %bitcast.29, bf16[16,128,128]{2,1,0:T(8,128)(2,1)S(1)} %copy-done, bf16[16,128,128]{2,1,0:T(8,128)(2,1)S(1)} %copy-done.1), custom_call_target="tpu_custom_call" | custom-call | flops 201326592 | bytes 3145728 | tf_op jit(solution)/shard_map/pallas_call | solution.py:38
  11.5 0.0 copy-start.4
  11.5 0.0 copy-start.5
  11.5 16.8 %all-to-all-start = ((bf16[24,192,128]{2,1,0:T(8,128)(2,1)}), bf16[24,192,128]{2,1,0:T(8,128)(2,1)S(1)}, u32[]{:S(2)}, u32[]{:S(2)}) async-start(bf16[24,192,128]{2,1,0:T(8,128)(2,1)} %shard_map.91), calls=%async_computation | async-start | bytes 2359296 | tf_op jit(solution)/shard_map/all_to_all | solution.py:171
  28.3 0.0 all-gather.3.cloned.1.call-start
  28.4 0.7 all-gather.3.cloned.1.call-update
  29.1 0.0 copy-done.4
  29.1 0.1 copy.24
  29.2 0.0 copy-done.5
  29.2 0.1 copy.25
  30.0 41.9 %all-gather.3.cloned.1.call-done = bf16[16,2,128,128]{3,2,1,0:T(8,128)(2,1)} async-done(((bf16[2,2,128,128]{3,2,1,0:T(8,128)(2,1)}), bf16[16,2,128,128]{3,2,1,0:T(8,128)(2,1)}) %all-gather.3.cloned.1.call-update) | async-done | bytes 1048592 | tf_op jit(solution)/shard_map/all_gather | solution.py:173
  71.9 0.0 copy-start.2
  71.9 1.2 dynamic-slice_bitcast_fusion.1
  73.2 0.1 pad_maximum_fusion
  73.3 0.1 copy.33
  73.3 10.9 %all_gather.11.bp = bf16[64,4096]{1,0:T(8,128)(2,1)S(1)} all-gather(bf16[16,4096]{1,0:T(8,128)(2,1)S(1)} %bitcast.31), channel_id=1, replica_groups={{0,8,16,24},{1,9,17,25},{2,10,18,26},{3,11,19,27},{4,12,20,28},{5,13,21..., dimensions={0}, use_global_device_ids=true | all-gather | bytes 655360 | tf_op jit(solution)/shard_map/all_gather | solution.py:178
  84.3 0.0 all-to-all-done.recv
  84.3 0.0 copy-done.2
  84.3 0.0 copy-start.6
  84.3 9.7 %shard_map.92 = f32[64,16]{1,0:T(8,128)S(1)} custom-call(s32[128,2]{1,0:T(8,128)S(1)} %bitcast.26, s32[128,2]{1,0:T(8,128)S(1)} %bitcast.27, s32[1]{0:T(128)S(6)} %copy.34.count, bf16[24,192,128]{2,1,0:T(8,128)(2,1)S(1)} %all-to-all-done.recv, bf16[8,2,2,128,128]{4,3,2,1,0:T(8,128)(2,1)S(1)} %bitcast.25, bf16[64,4096]{1,0:T(8,128)(2,1)S(1)} %all_gather.11.bp), custom_call_target="tpu_custom_call" | custom-call | flops 4294967296 | bytes 4194304 | tf_op jit(solution)/shard_map/pallas_call | solution.py:131
  94.0 14.7 %all_to_all.15 = f32[32,2,16]{2,1,0:T(2,128)S(1)} all-to-all(f32[32,2,16]{2,1,0:T(2,128)S(1)} %bitcast.28), channel_id=1, replica_groups=mesh['region'=24,'aux'=32] {'aux'}, dimensions={0} | all-to-all | bytes 8192 | tf_op jit(solution)/shard_map/all_to_all | solution.py:183
  108.8 0.1 broadcast_in_dim.11
  108.9 0.7 reshape.29
  109.6 27.6 %all-to-all-start.2 = ((f32[24,1,128]{2,1,0:T(1,128)}), f32[24,1,128]{2,1,0:T(1,128)S(1)}, u32[]{:S(2)}, u32[]{:S(2)}) async-start(f32[24,1,128]{2,1,0:T(1,128)} %reshape.29), calls=%async_computation.2 | async-start | bytes 24576 | tf_op jit(solution)/shard_map/all_to_all | solution.py:186
  137.2 0.0 copy-done.6
  137.8 0.1 broadcast_in_dim.13
  137.9 0.1 convert_element_type.20
  138.0 8.5 %all-to-all-done.2 = f32[24,1,128]{2,1,0:T(1,128)S(1)} async-done(((f32[24,1,128]{2,1,0:T(1,128)}), f32[24,1,128]{2,1,0:T(1,128)S(1)}, u32[]{:S(2)}, u32[]{:S(2)}) %all-to-all-start.2) | async-done | bytes 12320 | tf_op jit(solution)/shard_map/all_to_all | solution.py:186
  146.6 0.5 broadcast.4
  147.1 0.7 reduce
  147.8 0.1 reshape.30
  147.9 0.6 multiply_multiply_fusion
  (5 shorter events, 0.1 us)
Async XLA Ops:
  6.6 1.0 copy-start
  7.7 1.0 copy-start.1
  8.7 0.7 copy-start.3
  11.5 17.6 %copy-start.4 = (s32[1,128,2]{1,2,0:T(2,128)S(1)}, s32[1,128,2]{1,2,0:T(2,128)}, u32[]{:S(2)}) copy-start(s32[1,128,2]{1,2,0:T(2,128)} %param.13) | copy-start | bytes 3076
  11.5 17.7 %copy-start.5 = (s32[1,128,2]{1,2,0:T(2,128)S(1)}, s32[1,128,2]{1,2,0:T(2,128)}, u32[]{:S(2)}) copy-start(s32[1,128,2]{1,2,0:T(2,128)} %param.14) | copy-start | bytes 3076
  11.5 72.8 %all-to-all-start = ((bf16[24,192,128]{2,1,0:T(8,128)(2,1)}), bf16[24,192,128]{2,1,0:T(8,128)(2,1)S(1)}, u32[]{:S(2)}, u32[]{:S(2)}) async-start(bf16[24,192,128]{2,1,0:T(8,128)(2,1)} %shard_map.91), calls=%async_computation | async-start | bytes 2359296 | tf_op jit(solution)/shard_map/all_to_all | solution.py:171
  28.3 43.6 %all-gather.3.cloned.1.call-start = ((), (), s32[]{:S(2)}) async-start(), calls=%async_computation.3 | async-start | bytes 1179648 | tf_op jit(solution)/shard_map/all_gather | solution.py:173
  71.9 12.4 %copy-start.2 = (bf16[16,2,128,128]{3,2,1,0:T(8,128)(2,1)S(1)}, bf16[16,2,128,128]{3,2,1,0:T(8,128)(2,1)}, u32[]{:S(2)}) copy-start(bf16[16,2,128,128]{3,2,1,0:T(8,128)(2,1)} %all-gather.3.cloned.1.call-done) | copy-start | bytes 3145732
  84.3 52.9 %copy-start.6 = (s32[1,32]{1,0:T(1,128)S(1)}, s32[1,32]{1,0:T(1,128)}, u32[]{:S(2)}) copy-start(s32[1,32]{1,0:T(1,128)} %param.16) | copy-start | bytes 388
  109.6 37.0 %all-to-all-start.2 = ((f32[24,1,128]{2,1,0:T(1,128)}), f32[24,1,128]{2,1,0:T(1,128)S(1)}, u32[]{:S(2)}, u32[]{:S(2)}) async-start(f32[24,1,128]{2,1,0:T(1,128)} %reshape.29), calls=%async_computation.2 | async-start | bytes 24576 | tf_op jit(solution)/shard_map/all_to_all | solution.py:186
Sparse Core Ops, SparseCore 0:
  31.6 40.3 all-gather.2

commit v2 on v1

v2 whole, which is shorter than its diff:
```python
import jax
import jax.numpy as jnp
from jax import lax
from jax.experimental import pallas as pl
from jax.experimental.pallas import tpu as pltpu
from jax.sharding import PartitionSpec as P

NX = 4
NY = 8
NI = 4
NL = 2
NG = NY // NL
WIDTH = 128
IB = WIDTH // NI
LB = WIDTH // NL
X_GROUPS = [[x * NY + y for x in range(NX)] for y in range(NY)]
PAIR_GROUPS = [[x * NY + NL * g + h for g in range(NG)] for x in range(NX) for h in range(NL)]
OTHER = [(x * NY + y, x * NY + (y ^ 1)) for x in range(NX) for y in range(NY)]


def placed(body, ins, outs, space, **extra):
    return pl.pallas_call(
        body,
        out_shape=outs,
        in_specs=[pl.BlockSpec(memory_space=m) for m in ins],
        out_specs=pl.BlockSpec(memory_space=space),
        **extra,
    )


PARTS = 4


def pick_kernel(spots, lists, occ, vir, out, rows, tiles, staged, sems):
    row = pl.multiple_of(spots[0] * IB, IB)
    col = spots[1] * LB
    ntile = occ.shape[0]
    copies = [pltpu.make_async_copy(occ.at[:, pl.ds(row, IB), :], rows, sems.at[0])]
    step = ntile // PARTS
    for u in range(PARTS):
        at = pl.ds(u * step, step)
        copies.append(pltpu.make_async_copy(vir.at[at], tiles.at[at], sems.at[1 + u]))
    for c in copies:
        c.start()
    r = lax.broadcasted_iota(jnp.int32, (2 * WIDTH, WIDTH), 0)
    c = lax.broadcasted_iota(jnp.int32, (2 * WIDTH, WIDTH), 1)
    wanted = jnp.where(c < LB, c + col, c - LB + WIDTH + col)
    select = jnp.where(r == wanted, 1.0, 0.0).astype(jnp.bfloat16)
    for c in copies:
        c.wait()
    regions = staged.shape[0]
    step = regions // PARTS
    sent = []
    for u in range(PARTS):
        for d in range(u * step, (u + 1) * step):
            for j in range(2):
                staged[d, j * IB : (j + 1) * IB, :] = rows[lists[0, 2 * d + j]]
            pair = jnp.concatenate([tiles[lists[1, 2 * d]], tiles[lists[1, 2 * d + 1]]], axis=1)
            staged[d, 2 * IB :, :] = jnp.dot(
                pair, select, preferred_element_type=jnp.float32
            ).astype(jnp.bfloat16)
        at = pl.ds(u * step, step)
        sent.append(pltpu.make_async_copy(staged.at[at], out.at[at], sems.at[1 + PARTS + u]))
        sent[-1].start()
    for c in sent:
        c.wait()


def pick(spots, lists, occ, vir, regions):
    smem, hbm = pltpu.SMEM, pltpu.HBM
    shape = (regions, 2 * IB + WIDTH, WIDTH)
    return placed(
        pick_kernel,
        [smem, smem, hbm, hbm],
        jax.ShapeDtypeStruct(shape, jnp.bfloat16),
        hbm,
        scratch_shapes=[
            pltpu.VMEM((occ.shape[0], IB, WIDTH), jnp.bfloat16),
            pltpu.VMEM(vir.shape, jnp.bfloat16),
            pltpu.VMEM(shape, jnp.bfloat16),
            pltpu.SemaphoreType.DMA((1 + 2 * PARTS,)),
        ],
        compiler_params=pltpu.CompilerParams(vmem_limit_bytes=60 << 20),
        cost_estimate=pl.CostEstimate(flops=40 << 20, bytes_accessed=2 << 20, transcendentals=0),
    )(spots, lists, occ, vir)


CHUNK = 4


def transform_kernel(
    spots, pairs, tiles, count, recv, own, other, bp, out, half, acc, wide, order, number
):
    regions = recv.shape[0]
    nq = 2 * own.shape[0] * own.shape[2]
    rows = nq * IB
    parity = spots[1]
    group_at = spots[2]
    number[0] = 0
    number[1] = 0

    def place(t, carry):
        p = pairs[t, 0]
        n = number[p]
        order[p, 0, n] = pairs[t, 1] * (2 * regions) + tiles[t, 0]
        order[p, 1, n] = tiles[t, 1]
        number[p] = n + 1
        return carry

    lax.fori_loop(0, count[0], place, 0)

    group = 4
    for o, bq in enumerate((own, other)):

        def first(step, carry, o=o, bq=bq):
            q = step // NX
            x = step % NX
            source = jnp.concatenate([bq[x, q, 0], bq[x, q, 1]], axis=1)
            spot = ((parity ^ o) * NX + x) * 2
            for s in range(0, regions, group):
                occ = recv[s : s + group, 0 : 2 * IB, :].reshape(group * 2 * IB, WIDTH)
                res = jnp.dot(occ, source, preferred_element_type=jnp.float32).astype(jnp.bfloat16)
                for u in range(2 * group):
                    for f in range(2):
                        start = pl.multiple_of((spot + f) * IB, IB)
                        half[q * (2 * regions) + 2 * s + u, pl.ds(start, IB), :] = res[
                            u * IB : (u + 1) * IB, f * WIDTH : (f + 1) * WIDTH
                        ]
            return carry

        lax.fori_loop(0, 2 * NX, first, 0)

    lane = lax.broadcasted_iota(jnp.int32, (WIDTH, WIDTH), 1)
    for p in range(2):
        acc[p] = jnp.zeros((rows, WIDTH), jnp.float32)
        live = number[p]

        def second(step, carry, p=p, live=live):
            lhs = []
            rhs = []
            for u in range(CHUNK):
                t = step * CHUNK + u
                at = jnp.minimum(t, live - 1)
                b = order[p, 1, at]
                side = jnp.where(t < live, b % 2, 2)
                lhs.append(half[order[p, 0, at]])
                tile = recv[b // 2, 2 * IB :, :]
                rhs.append(jnp.where(lane // LB == side, tile, jnp.zeros_like(tile)))
            acc[p] += jnp.dot(
                jnp.concatenate(lhs, axis=1),
                jnp.concatenate(rhs, axis=0),
                preferred_element_type=jnp.float32,
            )
            return carry

        lax.fori_loop(0, (live + CHUNK - 1) // CHUNK, second, 0)
    low = acc[0]
    high = acc[1]
    lanes = lax.broadcasted_iota(jnp.int32, (rows, WIDTH), 1)
    wide[...] = jnp.where(
        lanes < LB, low + pltpu.roll(low, LB, 1), high + pltpu.roll(high, LB, 1)
    )
    flat = jnp.concatenate(
        [wide[pl.ds(i, nq, stride=IB), :].astype(jnp.bfloat16) for i in range(IB)], axis=1
    )
    partial = lax.dot_general(
        bp[...], flat, (((1,), (1,)), ((), ())), preferred_element_type=jnp.float32
    )
    n = lax.broadcasted_iota(jnp.int32, (nq, WIDTH), 0)
    c = lax.broadcasted_iota(jnp.int32, (nq, WIDTH), 1)
    at = ((n // 2) % NX) * nq + group_at * (nq // NX) + (n // (2 * NX)) * 2 + n % 2
    line = jnp.zeros((bp.shape[0] // 2, WIDTH), jnp.float32)
    split = partial.reshape(NG, 2, 2 * NX, nq)
    for f in range(2):
        spread = jnp.where(c == at + f * bp.shape[0], 1.0, 0.0)
        line += jnp.dot(
            split[:, f].reshape(NG * 2 * NX, nq),
            spread,
            preferred_element_type=jnp.float32,
            precision=lax.Precision.HIGHEST,
        )
    for g in range(NG):
        for h in range(NL):
            for x in range(NX):
                row = (g * NL + h) * NX + x
                out[x * NY + g * NL + h] = line[row : row + 1, :]


def transform(spots, pairs, tiles, count, recv, own, other, bp):
    smem, vmem = pltpu.SMEM, pltpu.VMEM
    regions = recv.shape[0]
    nterms = pairs.shape[0]
    nq = 2 * own.shape[0] * own.shape[2]
    return placed(
        transform_kernel,
        [smem] * 4 + [vmem] * 4,
        jax.ShapeDtypeStruct((bp.shape[0] // 2, 1, 2 * bp.shape[0]), jnp.float32),
        vmem,
        scratch_shapes=[
            pltpu.VMEM((4 * regions, nq * IB, WIDTH), jnp.bfloat16),
            pltpu.VMEM((2, nq * IB, WIDTH), jnp.float32),
            pltpu.VMEM((nq * IB, WIDTH), jnp.float32),
            pltpu.SMEM((2, 2, nterms), jnp.int32),
            pltpu.SMEM((2,), jnp.int32),
        ],
        compiler_params=pltpu.CompilerParams(vmem_limit_bytes=40 << 20),
        cost_estimate=pl.CostEstimate(flops=4 << 30, bytes_accessed=4 << 20, transcendentals=0),
    )(spots, pairs, tiles, count, recv, own, other, bp)


def total_kernel(parts, out):
    out[...] = jnp.broadcast_to(jnp.sum(parts[...], axis=0, keepdims=True), out.shape)


def total(parts, copies):
    return placed(
        total_kernel,
        [pltpu.VMEM],
        jax.ShapeDtypeStruct((copies,) + parts.shape[1:], parts.dtype),
        pltpu.VMEM,
        compiler_params=pltpu.CompilerParams(vmem_limit_bytes=1 << 20),
    )(parts)


def finish_kernel(parts, factor, out):
    line = jnp.sum(parts[...], axis=0) * factor[...]
    n = out.shape[1]
    out[0:1, :] = line[:, :n]
    out[1:2, :] = line[:, n:]


def finish(parts, factor):
    return placed(
        finish_kernel,
        [pltpu.VMEM, pltpu.VMEM],
        jax.ShapeDtypeStruct((2, parts.shape[2] // 2), parts.dtype),
        pltpu.VMEM,
        compiler_params=pltpu.CompilerParams(vmem_limit_bytes=1 << 20),
    )(parts, factor)


def per_device(
    occ_tiles,
    vir_tiles,
    three_index,
    send_lists,
    term_pairs,
    term_tiles,
    term_count,
    z_pattern,
    laplace_point,
):
    regions = lax.axis_size("region")
    width = occ_tiles.shape[1]
    per_aux = three_index.shape[1]
    nterms = term_pairs.shape[1]
    aux = lax.axis_index("aux").astype(jnp.int32)
    x = aux // NY
    y = aux % NY
    parity = y % NL
    spots = jnp.stack([x, parity, y // NL])

    outgoing = pick(spots, send_lists[0], occ_tiles, vir_tiles, regions)
    recv = lax.all_to_all(outgoing, "region", 0, 0, tiled=True)

    own = lax.all_gather(three_index, "aux", axis=0, tiled=False, axis_index_groups=X_GROUPS)
    other = lax.ppermute(own, "aux", OTHER)

    def sliced(b):
        b = lax.dynamic_slice_in_dim(b, x * IB, IB, 3)
        b = lax.dynamic_slice_in_dim(b, parity * LB, LB, 4)
        return jnp.concatenate([b[:, 0], b[:, 1]], axis=3)

    mine, theirs = sliced(own), sliced(other)
    even = parity == 0
    both = jnp.stack([jnp.where(even, mine, theirs), jnp.where(even, theirs, mine)])
    part = jnp.transpose(both, (2, 0, 1, 3, 4)).reshape(per_aux * NL * NX, IB * WIDTH)
    bp = lax.all_gather(part, "aux", axis=0, tiled=True, axis_index_groups=PAIR_GROUPS)

    partial = transform(
        spots, term_pairs[0], term_tiles[0], term_count, recv, own, other, bp
    )

    mask_row = jnp.repeat(z_pattern[0], per_aux).astype(jnp.float32)
    weight = 0.5 + 0.125 * laplace_point[0].astype(jnp.float32)
    scale = weight / (width * jnp.sqrt(jnp.float32(regions * nterms)))
    factor = jnp.concatenate([mask_row, mask_row])[None] * scale

    spread = lax.all_to_all(partial, "aux", 0, 0, tiled=True)
    every = lax.all_to_all(total(spread, regions), "region", 0, 0, tiled=True)
    return finish(every, factor)


def solution(mesh):
    in_specs = (
        P("region", None, None),
        P("region", None, None),
        P("region", "aux", None, None),
        P("region", None, None),
        P("region", None, None),
        P("region", None, None),
        P("region"),
        P("aux", None),
        P(),
    )
    out_specs = P("aux", None)
    return jax.shard_map(
        per_device, mesh=mesh, in_specs=in_specs, out_specs=out_specs, check_vma=False
    )
```

time: 156 us -> 123 us (0.79)
  waiting for transfers between devices: 51.1 us -> 26.3 us
  between operations: 14.8 us -> 1.49 us
  local copies, waits for them, and re-layouts: 5.87 us -> 0.73 us
  starting transfers between devices: 44.5 us -> 49.2 us
  Pallas kernels: 11.9 us -> 15.1 us
  blocking collectives: 25.7 us -> 28.7 us
    all_gather x1 -> x0, waiting for transfers between devices: 41.9 us -> none  [per_device(): lax.all_gather(three_index, 'aux', axis=0, tiled=False, axis_index_groups...]
    all_gather x1 -> x2, blocking collectives: 10.9 us -> 28.7 us  [the longest x1 17.4 us: per_device(): lax.all_gather(part, 'aux', axis=0, tiled=True, axis_index_groups=PAIR_GR...]
    all_to_all x1 -> x0, blocking collectives: 14.7 us -> none  [per_device(): spread = lax.all_to_all(outs, 'aux', 0, 0, tiled=True)]
    ppermute x0 -> x1, waiting for transfers between devices: none -> 8.9 us  [per_device(): other = lax.ppermute(own, 'aux', OTHER)]
    all_to_all x1 -> x2, waiting for transfers between devices: 8.55 us -> 17.1 us  [the longest x1 9.32 us: per_device(): every = lax.all_to_all(total(spread, regions), 'region', 0, 0, tiled=True)]
    unnamed x19 -> x13, local copies, waits for them, and re-layouts: 3.84 us -> 0.31 us
    pallas_call x2 -> x4, Pallas kernels: 11.9 us -> 15.1 us  [the longest x1 10.6 us: transform(): placed(transform_kernel, [smem] * 4 + [vmem] * 4, jax.ShapeDtypeStruct((b...]
    ppermute x0 -> x1, starting transfers between devices: none -> 3.19 us  [per_device(): other = lax.ppermute(own, 'aux', OTHER)]
  transfers between devices with their start and end apart: 3 -> 4, of which waited for: 2 -> 4; matrix products, arithmetic and copies ran while one was open for 1% -> 1% of each run, Pallas kernels for 0% -> 0%
where the time goes in v2:
time: 123 us; the launch traced here: 122 us
  starting transfers between devices  49.2 us (40%)
  blocking collectives  28.7 us (23%)
  waiting for transfers between devices  26.3 us (21%)
  Pallas kernels  15.1 us (12%)
  between operations  1.49 us (1%)
    all_to_all x1, starting transfers between devices, per_device(): every = lax.all_to_all(total(spread, regions), 'region', 0, 0, tiled=True)  19.6 us
    all_gather x1, blocking collectives, per_device(): lax.all_gather(part, 'aux', axis=0, tiled=True, axis_index_groups=PAIR_GR...  17.4 us
    all_to_all x1, starting transfers between devices, per_device(): recv = lax.all_to_all(outgoing, 'region', 0, 0, tiled=True)  16.8 us
    all_gather x1, blocking collectives, per_device(): lax.all_gather(three_index, 'aux', axis=0, tiled=False, axis_index_groups...  11.2 us
    pallas_call x1, Pallas kernels, transform(): placed(transform_kernel, [smem] * 4 + [vmem] * 4, jax.ShapeDtypeStruct((b...  10.6 us
    all_to_all x1, starting transfers between devices, per_device(): spread = lax.all_to_all(partial, 'aux', 0, 0, tiled=True)  9.66 us
    all_to_all x1, waiting for transfers between devices, per_device(): every = lax.all_to_all(total(spread, regions), 'region', 0, 0, tiled=True)  9.32 us
    ppermute x1, waiting for transfers between devices, per_device(): other = lax.ppermute(own, 'aux', OTHER)  8.9 us
  transfers between devices with their start and end apart: 4, of which 4 were waited for; matrix products, arithmetic and copies ran while one was open for 1% of the time, Pallas kernels for 0%

profile of v2, /device:TPU:1, one launch (start us, length us, event | category | flops | bytes accessed | tf_op | source)
XLA Modules:
  0.0 122.5 jit_solution(6092970824085362994)
XLA Ops:
  0.0 0.6 pad_add_fusion.spots
  0.6 3.2 %shard_map.91 = bf16[24,192,128]{2,1,0:T(8,128)(2,1)} custom-call(s32[3]{0:T(128)} %pad_add_fusion.spots, s32[2,48]{1,0:T(2,128)} %bitcast.38, bf16[16,128,128]{2,1,0:T(8,128)(2,1)} %occ.1, bf16[16,128,128]{2,1,0:T(8,128)(2,1)} %vir.1), custom_call_target="tpu_custom_call" | custom-call | flops 41943040 | bytes 2097152 | tf_op jit(solution)/shard_map/pallas_call | solution.py:72
  3.8 0.0 copy-start.1
  3.9 0.0 copy-start.2
  3.9 0.0 copy-start.3
  3.9 16.8 %all-to-all-start = ((bf16[24,192,128]{2,1,0:T(8,128)(2,1)}), bf16[24,192,128]{2,1,0:T(8,128)(2,1)S(1)}, u32[]{:S(2)}, u32[]{:S(2)}) async-start(bf16[24,192,128]{2,1,0:T(8,128)(2,1)} %shard_map.91), calls=%async_computation | async-start | bytes 2359296 | tf_op jit(solution)/shard_map/all_to_all | solution.py:264
  20.7 0.0 copy-done.1
  20.7 11.2 %all-gather = bf16[8,2,128,128]{3,2,1,0:T(8,128)(2,1)S(1)} all-gather(bf16[2,2,128,128]{3,2,1,0:T(8,128)(2,1)S(1)} %copy-done.1), channel_id=2, replica_groups={{0,8,16,24},{1,9,17,25},{2,10,18,26},{3,11,19,27},{4,12,20,28},{5,13,21..., dimensions={0}, use_global_device_ids=true | all-gather | bytes 655360 | tf_op jit(solution)/shard_map/all_gather | solution.py:266
  32.0 3.2 %collective-permute-start = (bf16[4,2,2,128,128]{4,3,2,1,0:T(8,128)(2,1)S(1)}, bf16[4,2,2,128,128]{4,3,2,1,0:T(8,128)(2,1)S(1)}, u32[]{:S(2)}, u32[]{:S(2)}) collective-permute-start(bf16[4,2,2,128,128]{4,3,2,1,0:T(8,128)(2,1)S(1)} %bitcast.31), channel_id=1, source_target_pairs={{0,1},{1,0},{2,3},{3,2},{4,5},{5,4},{6,7},{7,6},{8,9},{9,8},{10,11... | collective-permute-start | bytes 1572872 | tf_op jit(solution)/shard_map/ppermute | solution.py:267
  35.2 0.0 copy-done.2
  35.2 0.1 copy.21
  35.3 0.0 copy-done.3
  35.3 0.1 copy.22
  36.1 0.0 copy-start
  36.1 0.1 dynamic-slice_bitcast_fusion.3
  36.2 8.9 %collective-permute-done.other = bf16[4,2,2,128,128]{4,3,2,1,0:T(8,128)(2,1)S(1)} collective-permute-done((bf16[4,2,2,128,128]{4,3,2,1,0:T(8,128)(2,1)S(1)}, bf16[4,2,2,128,128]{4,3,2,1,0:T(8,128)(2,1)S(1)}, u32[]{:S(2)}, u32[]{:S(2)}) %collective-permute-start) | collective-permute-done | bytes 524320 | tf_op jit(solution)/shard_map/ppermute | solution.py:267
  45.1 0.1 dynamic-slice_bitcast_fusion.1
  45.3 0.1 broadcast_select_fusion.1
  45.4 0.1 copy.32
  45.5 17.4 %all_gather.11.bp = bf16[64,4096]{1,0:T(8,128)(2,1)S(1)} all-gather(bf16[16,4096]{1,0:T(8,128)(2,1)S(1)} %bitcast.36), channel_id=1, replica_groups={{0,2,4,6},{1,3,5,7},{8,10,12,14},{9,11,13,15},{16,18,20,22},{17,19,21,2..., dimensions={0}, use_global_device_ids=true | all-gather | bytes 655360 | tf_op jit(solution)/shard_map/all_gather | solution.py:278
  62.9 0.4 all-to-all-done.recv
  63.3 0.0 copy-done
  63.3 0.0 copy-start.4
  63.3 10.6 %shard_map.92 = f32[32,1,128]{2,1,0:T(1,128)} custom-call(s32[3]{0:T(128)S(1)} %copy-done, s32[128,2]{1,0:T(8,128)S(1)} %bitcast.34, s32[128,2]{1,0:T(8,128)S(1)} %bitcast.35, s32[1]{0:T(128)S(6)} %copy.33.count, bf16[24,192,128]{2,1,0:T(8,128)(2,1)S(1)} %all-to-all-done.recv, bf16[4,2,2,128,128]{4,3,2,1,0:T(8,128)(2,1)S(1)} %bitcast.33, ...), custom_call_target="tpu_custom_call" | custom-call | flops 4294967296 | bytes 4194304 | tf_op jit(solution)/shard_map/pallas_call | solution.py:194
  73.9 9.7 %all-to-all-start.1 = ((f32[32,1,128]{2,1,0:T(1,128)}), f32[32,1,128]{2,1,0:T(1,128)S(1)}, u32[]{:S(2)}, u32[]{:S(2)}) async-start(f32[32,1,128]{2,1,0:T(1,128)} %shard_map.92), calls=%async_computation.1 | async-start | bytes 32768 | tf_op jit(solution)/shard_map/all_to_all | solution.py:289
  83.6 0.0 copy-done.4
  83.6 0.1 broadcast_in_dim.4
  83.7 0.1 concatenate.60
  84.4 7.8 %all-to-all-done.1.parts = f32[32,1,128]{2,1,0:T(1,128)S(1)} async-done(((f32[32,1,128]{2,1,0:T(1,128)}), f32[32,1,128]{2,1,0:T(1,128)S(1)}, u32[]{:S(2)}, u32[]{:S(2)}) %all-to-all-start.1) | async-done | bytes 16416 | tf_op jit(solution)/shard_map/all_to_all | solution.py:289
  92.2 0.6 shard_map.93
  92.8 19.6 %all-to-all-start.2 = ((f32[24,1,128]{2,1,0:T(1,128)}), f32[24,1,128]{2,1,0:T(1,128)S(1)}, u32[]{:S(2)}, u32[]{:S(2)}) async-start(f32[24,1,128]{2,1,0:T(1,128)} %shard_map.93), calls=%async_computation.2 | async-start | bytes 24576 | tf_op jit(solution)/shard_map/all_to_all | solution.py:290
  112.4 0.1 maximum_multiply_fusion.factor
  112.5 9.3 %all-to-all-done.2.parts = f32[24,1,128]{2,1,0:T(1,128)S(1)} async-done(((f32[24,1,128]{2,1,0:T(1,128)}), f32[24,1,128]{2,1,0:T(1,128)S(1)}, u32[]{:S(2)}, u32[]{:S(2)}) %all-to-all-start.2) | async-done | bytes 12320 | tf_op jit(solution)/shard_map/all_to_all | solution.py:290
  121.8 0.7 shard_map.94
  (3 shorter events, 0.0 us)
Async XLA Ops:
  3.8 16.9 %copy-start.1 = (bf16[2,2,128,128]{3,2,1,0:T(8,128)(2,1)S(1)}, bf16[2,2,128,128]{3,2,1,0:T(8,128)(2,1)}, u32[]{:S(2)}) copy-start(bf16[2,2,128,128]{3,2,1,0:T(8,128)(2,1)} %param.11) | copy-start | bytes 393220
  3.9 31.3 %copy-start.2 = (s32[1,128,2]{1,2,0:T(2,128)S(1)}, s32[1,128,2]{1,2,0:T(2,128)}, u32[]{:S(2)}) copy-start(s32[1,128,2]{1,2,0:T(2,128)} %param.13) | copy-start | bytes 3076
  3.9 31.5 %copy-start.3 = (s32[1,128,2]{1,2,0:T(2,128)S(1)}, s32[1,128,2]{1,2,0:T(2,128)}, u32[]{:S(2)}) copy-start(s32[1,128,2]{1,2,0:T(2,128)} %param.14) | copy-start | bytes 3076
  3.9 59.4 %all-to-all-start = ((bf16[24,192,128]{2,1,0:T(8,128)(2,1)}), bf16[24,192,128]{2,1,0:T(8,128)(2,1)S(1)}, u32[]{:S(2)}, u32[]{:S(2)}) async-start(bf16[24,192,128]{2,1,0:T(8,128)(2,1)} %shard_map.91), calls=%async_computation | async-start | bytes 2359296 | tf_op jit(solution)/shard_map/all_to_all | solution.py:264
  32.0 13.2 %collective-permute-start = (bf16[4,2,2,128,128]{4,3,2,1,0:T(8,128)(2,1)S(1)}, bf16[4,2,2,128,128]{4,3,2,1,0:T(8,128)(2,1)S(1)}, u32[]{:S(2)}, u32[]{:S(2)}) collective-permute-start(bf16[4,2,2,128,128]{4,3,2,1,0:T(8,128)(2,1)S(1)} %bitcast.31), channel_id=1, source_target_pairs={{0,1},{1,0},{2,3},{3,2},{4,5},{5,4},{6,7},{7,6},{8,9},{9,8},{10,11... | collective-permute-start | bytes 1572872 | tf_op jit(solution)/shard_map/ppermute | solution.py:267
  36.1 27.2 %copy-start = (s32[3]{0:T(128)S(1)}, s32[3]{0:T(128)}, u32[]{:S(2)}) copy-start(s32[3]{0:T(128)} %pad_add_fusion.spots) | copy-start | bytes 40
  63.3 20.3 %copy-start.4 = (s32[1,32]{1,0:T(1,128)S(1)}, s32[1,32]{1,0:T(1,128)}, u32[]{:S(2)}) copy-start(s32[1,32]{1,0:T(1,128)} %param.16) | copy-start | bytes 388
  73.9 18.3 %all-to-all-start.1 = ((f32[32,1,128]{2,1,0:T(1,128)}), f32[32,1,128]{2,1,0:T(1,128)S(1)}, u32[]{:S(2)}, u32[]{:S(2)}) async-start(f32[32,1,128]{2,1,0:T(1,128)} %shard_map.92), calls=%async_computation.1 | async-start | bytes 32768 | tf_op jit(solution)/shard_map/all_to_all | solution.py:289
  92.8 29.0 %all-to-all-start.2 = ((f32[24,1,128]{2,1,0:T(1,128)}), f32[24,1,128]{2,1,0:T(1,128)S(1)}, u32[]{:S(2)}, u32[]{:S(2)}) async-start(f32[24,1,128]{2,1,0:T(1,128)} %shard_map.93), calls=%async_computation.2 | async-start | bytes 24576 | tf_op jit(solution)/shard_map/all_to_all | solution.py:290

commit v3 on v2

v3 whole, which is shorter than its diff:
```python
import jax
import jax.numpy as jnp
from jax import lax
from jax.experimental import pallas as pl
from jax.experimental.pallas import tpu as pltpu
from jax.sharding import PartitionSpec as P

NX = 4
NY = 8
NI = 4
NL = 2
NG = NY // NL
WIDTH = 128
IB = WIDTH // NI
LB = WIDTH // NL
X_GROUPS = [[x * NY + y for x in range(NX)] for y in range(NY)]
PAIR_GROUPS = [[x * NY + NL * g + h for g in range(NG)] for x in range(NX) for h in range(NL)]
OTHER = [(x * NY + y, x * NY + (y ^ 1)) for x in range(NX) for y in range(NY)]


def placed(body, ins, outs, space, **extra):
    return pl.pallas_call(
        body,
        out_shape=outs,
        in_specs=[pl.BlockSpec(memory_space=m) for m in ins],
        out_specs=pl.BlockSpec(memory_space=space),
        **extra,
    )


def member():
    aux = lax.axis_index("aux")
    return aux // NY, aux % NY


PARTS = 4


def pick_kernel(lists, occ, vir, out, rows, tiles, staged, sems):
    x, y = member()
    row = pl.multiple_of(x * IB, IB)
    col = (y % NL) * LB
    ntile = occ.shape[0]
    copies = [pltpu.make_async_copy(occ.at[:, pl.ds(row, IB), :], rows, sems.at[0])]
    step = ntile // PARTS
    for u in range(PARTS):
        at = pl.ds(u * step, step)
        copies.append(pltpu.make_async_copy(vir.at[at], tiles.at[at], sems.at[1 + u]))
    for c in copies:
        c.start()
    r = lax.broadcasted_iota(jnp.int32, (2 * WIDTH, WIDTH), 0)
    c = lax.broadcasted_iota(jnp.int32, (2 * WIDTH, WIDTH), 1)
    wanted = jnp.where(c < LB, c + col, c - LB + WIDTH + col)
    select = jnp.where(r == wanted, 1.0, 0.0).astype(jnp.bfloat16)
    for c in copies:
        c.wait()
    regions = staged.shape[0]
    step = regions // PARTS
    sent = []
    for u in range(PARTS):
        for d in range(u * step, (u + 1) * step):
            for j in range(2):
                staged[d, j * IB : (j + 1) * IB, :] = rows[lists[0, 2 * d + j]]
            pair = jnp.concatenate([tiles[lists[1, 2 * d]], tiles[lists[1, 2 * d + 1]]], axis=1)
            staged[d, 2 * IB :, :] = jnp.dot(
                pair, select, preferred_element_type=jnp.float32
            ).astype(jnp.bfloat16)
        at = pl.ds(u * step, step)
        sent.append(pltpu.make_async_copy(staged.at[at], out.at[at], sems.at[1 + PARTS + u]))
        sent[-1].start()
    for c in sent:
        c.wait()


def pick(lists, occ, vir, regions):
    smem, hbm = pltpu.SMEM, pltpu.HBM
    shape = (regions, 2 * IB + WIDTH, WIDTH)
    return placed(
        pick_kernel,
        [smem, hbm, hbm],
        jax.ShapeDtypeStruct(shape, jnp.bfloat16),
        hbm,
        scratch_shapes=[
            pltpu.VMEM((occ.shape[0], IB, WIDTH), jnp.bfloat16),
            pltpu.VMEM(vir.shape, jnp.bfloat16),
            pltpu.VMEM(shape, jnp.bfloat16),
            pltpu.SemaphoreType.DMA((1 + 2 * PARTS,)),
        ],
        compiler_params=pltpu.CompilerParams(vmem_limit_bytes=60 << 20),
        cost_estimate=pl.CostEstimate(flops=40 << 20, bytes_accessed=2 << 20, transcendentals=0),
    )(lists, occ, vir)


GROUP = 2
WIDE = 2
CHUNK = 32


def transform_kernel(
    pairs, tiles, count, recv, own, other, same, rest, out, half, acc, wide
):
    regions = recv.shape[0]
    nq = 2 * own.shape[0] * own.shape[2]
    rows = nq * IB
    y = member()[1]
    parity = y % NL

    def first(n, carry):
        q = n // (NX // WIDE)
        at = (n % (NX // WIDE)) * WIDE
        source = jnp.concatenate(
            [bq[at + v, q, f] for v in range(WIDE) for bq in (own, other) for f in range(2)], axis=1
        )
        for s in range(0, regions, GROUP):
            occ = recv[s : s + GROUP, 0 : 2 * IB, :].reshape(GROUP * 2 * IB, WIDTH)
            res = jnp.dot(occ, source, preferred_element_type=jnp.float32).astype(jnp.bfloat16)
            for v in range(WIDE):
                for o in range(2):
                    for f in range(2):
                        spot = ((parity ^ o) * NX + at + v) * 2 + f
                        start = pl.multiple_of(spot * IB, IB)
                        left = (v * 4 + o * 2 + f) * WIDTH
                        for u in range(2 * GROUP):
                            half[q * (2 * regions) + 2 * s + u, pl.ds(start, IB), :] = res[
                                u * IB : (u + 1) * IB, left : left + WIDTH
                            ]
        return carry

    lax.fori_loop(0, 2 * NX // WIDE, first, 0)

    acc[...] = jnp.zeros_like(acc)
    live = count[0]
    lane = lax.broadcasted_iota(jnp.int32, (WIDTH, 2 * WIDTH), 1) // LB

    def second(n, carry):
        lhs = []
        rhs = []
        for u in range(CHUNK):
            t = n * CHUNK + u
            at = jnp.minimum(t, live - 1)
            b = tiles[at, 1]
            side = jnp.where(t < live, pairs[at, 0] * NL + b % 2, -1)
            lhs.append(half[pairs[at, 1] * (2 * regions) + tiles[at, 0]])
            tile = recv[b // 2, 2 * IB :, :]
            tile = jnp.concatenate([tile, tile], axis=1)
            rhs.append(jnp.where(lane == side, tile, jnp.zeros_like(tile)))
        acc[...] += jnp.dot(
            jnp.concatenate(lhs, axis=1),
            jnp.concatenate(rhs, axis=0),
            preferred_element_type=jnp.float32,
        )
        return carry

    lax.fori_loop(0, (live + CHUNK - 1) // CHUNK, second, 0)
    low = acc[:, :WIDTH]
    high = acc[:, WIDTH:]
    lanes = lax.broadcasted_iota(jnp.int32, (rows, WIDTH), 1)
    wide[...] = jnp.where(
        lanes < LB, low + pltpu.roll(low, LB, 1), high + pltpu.roll(high, LB, 1)
    )
    flat = jnp.concatenate(
        [wide[pl.ds(i, nq, stride=IB), :].astype(jnp.bfloat16) for i in range(IB)], axis=1
    )
    nall = 2 * same.shape[0]
    n = lax.broadcasted_iota(jnp.int32, (nq, WIDTH), 0)
    c = lax.broadcasted_iota(jnp.int32, (nq, WIDTH), 1)
    at = ((n // 2) % NX) * nq + (y // NL) * (nq // NX) + (n // (2 * NX)) * 2 + n % 2
    places = [jnp.where(c == at + f * nall, 1.0, 0.0) for f in range(2)]
    for o, bp in enumerate((same, rest)):
        partial = lax.dot_general(
            bp[...], flat, (((1,), (1,)), ((), ())), preferred_element_type=jnp.float32
        )
        lines = [
            jnp.dot(
                partial,
                place,
                preferred_element_type=jnp.float32,
                precision=lax.Precision.HIGHEST,
            )
            for place in places
        ]
        for g in range(NG):
            for v in range(NX):
                row = 2 * (g * NX + v)
                out[v * NY + NL * g + (parity ^ o)] = (
                    lines[0][row : row + 1, :] + lines[1][row + 1 : row + 2, :]
                )


def transform(pairs, tiles, count, recv, own, other, same, rest):
    smem, vmem = pltpu.SMEM, pltpu.VMEM
    regions = recv.shape[0]
    nq = 2 * own.shape[0] * own.shape[2]
    return placed(
        transform_kernel,
        [smem] * 3 + [vmem] * 5,
        jax.ShapeDtypeStruct((same.shape[0], 1, 4 * same.shape[0]), jnp.float32),
        vmem,
        scratch_shapes=[
            pltpu.VMEM((4 * regions, nq * IB, WIDTH), jnp.bfloat16),
            pltpu.VMEM((nq * IB, 2 * WIDTH), jnp.float32),
            pltpu.VMEM((nq * IB, WIDTH), jnp.float32),
        ],
        compiler_params=pltpu.CompilerParams(vmem_limit_bytes=40 << 20),
        cost_estimate=pl.CostEstimate(flops=4 << 30, bytes_accessed=4 << 20, transcendentals=0),
    )(pairs, tiles, count, recv, own, other, same, rest)


def total_kernel(parts, out):
    out[...] = jnp.broadcast_to(jnp.sum(parts[...], axis=0, keepdims=True), out.shape)


def total(parts, copies):
    return placed(
        total_kernel,
        [pltpu.VMEM],
        jax.ShapeDtypeStruct((copies,) + parts.shape[1:], parts.dtype),
        pltpu.VMEM,
        compiler_params=pltpu.CompilerParams(vmem_limit_bytes=1 << 20),
    )(parts)


def finish_kernel(parts, factor, out):
    line = jnp.sum(parts[...], axis=0) * factor[...]
    n = out.shape[1]
    out[0:1, :] = line[:, :n]
    out[1:2, :] = line[:, n:]


def finish(parts, factor):
    return placed(
        finish_kernel,
        [pltpu.VMEM, pltpu.VMEM],
        jax.ShapeDtypeStruct((2, parts.shape[2] // 2), parts.dtype),
        pltpu.VMEM,
        compiler_params=pltpu.CompilerParams(vmem_limit_bytes=1 << 20),
    )(parts, factor)


def per_device(
    occ_tiles,
    vir_tiles,
    three_index,
    send_lists,
    term_pairs,
    term_tiles,
    term_count,
    z_pattern,
    laplace_point,
):
    regions = lax.axis_size("region")
    width = occ_tiles.shape[1]
    per_aux = three_index.shape[1]
    nterms = term_pairs.shape[1]
    x, y = member()

    outgoing = pick(send_lists[0], occ_tiles, vir_tiles, regions)
    recv = lax.all_to_all(outgoing, "region", 0, 0, tiled=True)

    own = lax.all_gather(three_index, "aux", axis=0, tiled=False, axis_index_groups=X_GROUPS)
    other = lax.ppermute(own, "aux", OTHER)

    def sliced(b):
        b = lax.dynamic_slice_in_dim(b, x * IB, IB, 3)
        b = lax.dynamic_slice_in_dim(b, (y % NL) * LB, LB, 4)
        b = jnp.concatenate([b[:, 0], b[:, 1]], axis=3)
        return b.reshape(NX * per_aux, IB * WIDTH)

    def spread(b):
        return lax.all_gather(b, "aux", axis=0, tiled=True, axis_index_groups=PAIR_GROUPS)

    same = spread(sliced(own))
    theirs, same = lax.optimization_barrier((sliced(other), same))
    rest = spread(theirs)

    partial = transform(
        term_pairs[0], term_tiles[0], term_count, recv, own, other, same, rest
    )

    mask_row = jnp.repeat(z_pattern[0], per_aux).astype(jnp.float32)
    weight = 0.5 + 0.125 * laplace_point[0].astype(jnp.float32)
    scale = weight / (width * jnp.sqrt(jnp.float32(regions * nterms)))
    factor = jnp.concatenate([mask_row, mask_row])[None] * scale

    spread = lax.all_to_all(partial, "aux", 0, 0, tiled=True)
    every = lax.all_to_all(total(spread, regions), "region", 0, 0, tiled=True)
    return finish(every, factor)


def solution(mesh):
    in_specs = (
        P("region", None, None),
        P("region", None, None),
        P("region", "aux", None, None),
        P("region", None, None),
        P("region", None, None),
        P("region", None, None),
        P("region"),
        P("aux", None),
        P(),
    )
    out_specs = P("aux", None)
    return jax.shard_map(
        per_device, mesh=mesh, in_specs=in_specs, out_specs=out_specs, check_vma=False
    )
```

time: 123 us -> 123 us (level)
  blocking collectives: 28.7 us -> 42.1 us
  waiting for transfers between devices: 26.3 us -> 17.1 us
  starting transfers between devices: 49.2 us -> 46.9 us
    all_gather x1 -> x2, blocking collectives: 17.4 us -> 30.8 us  [spread(): lax.all_gather(b, 'aux', axis=0, tiled=True, axis_index_groups=PAIR_GROUPS)]
    ppermute x1, waiting for transfers between devices: 8.9 us -> 0.01 us  [per_device(): other = lax.ppermute(own, 'aux', OTHER)]
    all_to_all x1, starting transfers between devices: 9.66 us -> 6.28 us  [per_device(): spread = lax.all_to_all(partial, 'aux', 0, 0, tiled=True)]
  transfers between devices with their start and end apart: 4 -> 4, of which waited for: 4 -> 2; matrix products, arithmetic and copies ran while one was open for 1% -> 1% of each run, Pallas kernels for 0% -> 0%
where the time goes in v3:
time: 123 us
  starting transfers between devices  46.9 us (38%)
  blocking collectives  42.1 us (34%)
  waiting for transfers between devices  17.1 us (14%)
  Pallas kernels  14 us (11%)
  between operations  1.51 us (1%)
    all_gather x2, blocking collectives, spread(): lax.all_gather(b, 'aux', axis=0, tiled=True, axis_index_groups=PAIR_GROUPS)  30.8 us
    all_to_all x1, starting transfers between devices, per_device(): every = lax.all_to_all(total(spread, regions), 'region', 0, 0, tiled=True)  20.6 us
    all_to_all x1, starting transfers between devices, per_device(): recv = lax.all_to_all(outgoing, 'region', 0, 0, tiled=True)  16.8 us
    all_gather x1, blocking collectives, per_device(): lax.all_gather(three_index, 'aux', axis=0, tiled=False, axis_index_groups...  11.2 us
    pallas_call x1, Pallas kernels, transform(): placed(transform_kernel, [smem] * 3 + [vmem] * 5, jax.ShapeDtypeStruct((s...  9.5 us
    all_to_all x1, waiting for transfers between devices, per_device(): every = lax.all_to_all(total(spread, regions), 'region', 0, 0, tiled=True)  9.34 us
    all_to_all x1, waiting for transfers between devices, per_device(): spread = lax.all_to_all(partial, 'aux', 0, 0, tiled=True)  7.77 us
    all_to_all x1, starting transfers between devices, per_device(): spread = lax.all_to_all(partial, 'aux', 0, 0, tiled=True)  6.28 us
  transfers between devices with their start and end apart: 4, of which 2 were waited for; matrix products, arithmetic and copies ran while one was open for 1% of the time, Pallas kernels for 0%

profile of v3, /device:TPU:1, one launch (start us, length us, event | category | flops | bytes accessed | tf_op | source)
XLA Modules:
  0.0 122.6 jit_solution(17862628899086053459)
XLA Ops:
  0.0 3.2 %shard_map.91 = bf16[24,192,128]{2,1,0:T(8,128)(2,1)} custom-call(s32[2,48]{1,0:T(2,128)} %bitcast.38, bf16[16,128,128]{2,1,0:T(8,128)(2,1)} %occ.1, bf16[16,128,128]{2,1,0:T(8,128)(2,1)} %vir.1), custom_call_target="tpu_custom_call" | custom-call | flops 41943040 | bytes 2097152 | tf_op jit(solution)/shard_map/pallas_call | solution.py:78
  3.2 0.0 copy-start
  3.2 0.0 copy-start.1
  3.3 0.0 copy-start.2
  3.3 16.8 %all-to-all-start = ((bf16[24,192,128]{2,1,0:T(8,128)(2,1)}), bf16[24,192,128]{2,1,0:T(8,128)(2,1)S(1)}, u32[]{:S(2)}, u32[]{:S(2)}) async-start(bf16[24,192,128]{2,1,0:T(8,128)(2,1)} %shard_map.91), calls=%async_computation | async-start | bytes 2359296 | tf_op jit(solution)/shard_map/all_to_all | solution.py:258
  20.1 0.0 copy-done
  20.1 11.2 %all-gather = bf16[8,2,128,128]{3,2,1,0:T(8,128)(2,1)S(1)} all-gather(bf16[2,2,128,128]{3,2,1,0:T(8,128)(2,1)S(1)} %copy-done), channel_id=2, replica_groups={{0,8,16,24},{1,9,17,25},{2,10,18,26},{3,11,19,27},{4,12,20,28},{5,13,21..., dimensions={0}, use_global_device_ids=true | all-gather | bytes 655360 | tf_op jit(solution)/shard_map/all_gather | solution.py:260
  31.4 3.2 %collective-permute-start = (bf16[4,2,2,128,128]{4,3,2,1,0:T(8,128)(2,1)S(1)}, bf16[4,2,2,128,128]{4,3,2,1,0:T(8,128)(2,1)S(1)}, u32[]{:S(2)}, u32[]{:S(2)}) collective-permute-start(bf16[4,2,2,128,128]{4,3,2,1,0:T(8,128)(2,1)S(1)} %bitcast.29), channel_id=1, source_target_pairs={{0,1},{1,0},{2,3},{3,2},{4,5},{5,4},{6,7},{7,6},{8,9},{9,8},{10,11... | collective-permute-start | bytes 1572872 | tf_op jit(solution)/shard_map/ppermute | solution.py:261
  34.6 0.0 copy-done.1
  34.6 0.1 copy.18
  34.7 0.0 copy-done.2
  34.7 0.1 copy.19
  35.5 0.1 dynamic-slice_bitcast_fusion.1
  35.6 0.1 pad_maximum_fusion.1
  35.8 18.7 %all_gather.14.same = bf16[32,4096]{1,0:T(8,128)(2,1)S(1)} all-gather(bf16[8,4096]{1,0:T(8,128)(2,1)S(1)} %bitcast.36), channel_id=1, replica_groups={{0,2,4,6},{1,3,5,7},{8,10,12,14},{9,11,13,15},{16,18,20,22},{17,19,21,2..., dimensions={0}, use_global_device_ids=true | all-gather | bytes 327680 | tf_op jit(solution)/shard_map/all_gather | solution.py:270
  54.5 0.0 collective-permute-done.other
  54.5 0.1 dynamic-slice_bitcast_fusion.3
  54.6 0.1 pad_maximum_fusion
  54.8 12.1 %all_gather.15.rest = bf16[32,4096]{1,0:T(8,128)(2,1)S(1)} all-gather(bf16[8,4096]{1,0:T(8,128)(2,1)S(1)} %bitcast.37), channel_id=1, replica_groups={{0,2,4,6},{1,3,5,7},{8,10,12,14},{9,11,13,15},{16,18,20,22},{17,19,21,2..., dimensions={0}, use_global_device_ids=true | all-gather | bytes 327680 | tf_op jit(solution)/shard_map/all_gather | solution.py:270
  66.9 0.0 all-to-all-done.recv
  66.9 0.0 copy-start.3
  66.9 9.5 %shard_map.92 = f32[32,1,128]{2,1,0:T(1,128)} custom-call(s32[128,2]{1,0:T(8,128)S(1)} %bitcast.32, s32[128,2]{1,0:T(8,128)S(1)} %bitcast.33, s32[1]{0:T(128)S(6)} %copy.30.count, bf16[24,192,128]{2,1,0:T(8,128)(2,1)S(1)} %all-to-all-done.recv, bf16[4,2,2,128,128]{4,3,2,1,0:T(8,128)(2,1)S(1)} %bitcast.31, ...), custom_call_target="tpu_custom_call" | custom-call | flops 4294967296 | bytes 4194304 | tf_op jit(solution)/shard_map/pallas_call | solution.py:194
  76.4 6.3 %all-to-all-start.1 = ((f32[32,1,128]{2,1,0:T(1,128)}), f32[32,1,128]{2,1,0:T(1,128)S(1)}, u32[]{:S(2)}, u32[]{:S(2)}) async-start(f32[32,1,128]{2,1,0:T(1,128)} %shard_map.92), calls=%async_computation.1 | async-start | bytes 32768 | tf_op jit(solution)/shard_map/all_to_all | solution.py:285
  82.7 0.0 copy-done.3
  82.7 0.1 broadcast_in_dim.4
  82.8 0.1 concatenate.20
  83.5 7.8 %all-to-all-done.1.parts = f32[32,1,128]{2,1,0:T(1,128)S(1)} async-done(((f32[32,1,128]{2,1,0:T(1,128)}), f32[32,1,128]{2,1,0:T(1,128)S(1)}, u32[]{:S(2)}, u32[]{:S(2)}) %all-to-all-start.1) | async-done | bytes 16416 | tf_op jit(solution)/shard_map/all_to_all | solution.py:285
  91.3 0.6 shard_map.93
  91.9 20.6 %all-to-all-start.2 = ((f32[24,1,128]{2,1,0:T(1,128)}), f32[24,1,128]{2,1,0:T(1,128)S(1)}, u32[]{:S(2)}, u32[]{:S(2)}) async-start(f32[24,1,128]{2,1,0:T(1,128)} %shard_map.93), calls=%async_computation.2 | async-start | bytes 24576 | tf_op jit(solution)/shard_map/all_to_all | solution.py:286
  112.5 0.1 maximum_multiply_fusion.factor
  112.6 9.3 %all-to-all-done.2.parts = f32[24,1,128]{2,1,0:T(1,128)S(1)} async-done(((f32[24,1,128]{2,1,0:T(1,128)}), f32[24,1,128]{2,1,0:T(1,128)S(1)}, u32[]{:S(2)}, u32[]{:S(2)}) %all-to-all-start.2) | async-done | bytes 12320 | tf_op jit(solution)/shard_map/all_to_all | solution.py:286
  122.0 0.7 shard_map.94
  (3 shorter events, 0.1 us)
Async XLA Ops:
  3.2 16.9 %copy-start = (bf16[2,2,128,128]{3,2,1,0:T(8,128)(2,1)S(1)}, bf16[2,2,128,128]{3,2,1,0:T(8,128)(2,1)}, u32[]{:S(2)}) copy-start(bf16[2,2,128,128]{3,2,1,0:T(8,128)(2,1)} %param.11) | copy-start | bytes 393220
  3.2 31.4 %copy-start.1 = (s32[1,128,2]{1,2,0:T(2,128)S(1)}, s32[1,128,2]{1,2,0:T(2,128)}, u32[]{:S(2)}) copy-start(s32[1,128,2]{1,2,0:T(2,128)} %param.13) | copy-start | bytes 3076
  3.3 31.5 %copy-start.2 = (s32[1,128,2]{1,2,0:T(2,128)S(1)}, s32[1,128,2]{1,2,0:T(2,128)}, u32[]{:S(2)}) copy-start(s32[1,128,2]{1,2,0:T(2,128)} %param.14) | copy-start | bytes 3076
  3.3 63.6 %all-to-all-start = ((bf16[24,192,128]{2,1,0:T(8,128)(2,1)}), bf16[24,192,128]{2,1,0:T(8,128)(2,1)S(1)}, u32[]{:S(2)}, u32[]{:S(2)}) async-start(bf16[24,192,128]{2,1,0:T(8,128)(2,1)} %shard_map.91), calls=%async_computation | async-start | bytes 2359296 | tf_op jit(solution)/shard_map/all_to_all | solution.py:258
  31.4 23.1 %collective-permute-start = (bf16[4,2,2,128,128]{4,3,2,1,0:T(8,128)(2,1)S(1)}, bf16[4,2,2,128,128]{4,3,2,1,0:T(8,128)(2,1)S(1)}, u32[]{:S(2)}, u32[]{:S(2)}) collective-permute-start(bf16[4,2,2,128,128]{4,3,2,1,0:T(8,128)(2,1)S(1)} %bitcast.29), channel_id=1, source_target_pairs={{0,1},{1,0},{2,3},{3,2},{4,5},{5,4},{6,7},{7,6},{8,9},{9,8},{10,11... | collective-permute-start | bytes 1572872 | tf_op jit(solution)/shard_map/ppermute | solution.py:261
  66.9 15.8 %copy-start.3 = (s32[1,32]{1,0:T(1,128)S(1)}, s32[1,32]{1,0:T(1,128)}, u32[]{:S(2)}) copy-start(s32[1,32]{1,0:T(1,128)} %param.16) | copy-start | bytes 388
  76.4 14.9 %all-to-all-start.1 = ((f32[32,1,128]{2,1,0:T(1,128)}), f32[32,1,128]{2,1,0:T(1,128)S(1)}, u32[]{:S(2)}, u32[]{:S(2)}) async-start(f32[32,1,128]{2,1,0:T(1,128)} %shard_map.92), calls=%async_computation.1 | async-start | bytes 32768 | tf_op jit(solution)/shard_map/all_to_all | solution.py:285
  91.9 30.0 %all-to-all-start.2 = ((f32[24,1,128]{2,1,0:T(1,128)}), f32[24,1,128]{2,1,0:T(1,128)S(1)}, u32[]{:S(2)}, u32[]{:S(2)}) async-start(f32[24,1,128]{2,1,0:T(1,128)} %shard_map.93), calls=%async_computation.2 | async-start | bytes 24576 | tf_op jit(solution)/shard_map/all_to_all | solution.py:286

commit v4 on v3

--- a/solution.py
+++ b/solution.py
@@ -14,8 +14,12 @@
 IB = WIDTH // NI
 LB = WIDTH // NL
 X_GROUPS = [[x * NY + y for x in range(NX)] for y in range(NY)]
-PAIR_GROUPS = [[x * NY + NL * g + h for g in range(NG)] for x in range(NX) for h in range(NL)]
 OTHER = [(x * NY + y, x * NY + (y ^ 1)) for x in range(NX) for y in range(NY)]
+HOPS = (2, 1, NG - 1)
+
+
+def onward(hop):
+    return [(x * NY + y, x * NY + (y + NL * hop) % NY) for x in range(NX) for y in range(NY)]
 
 
 def placed(body, ins, outs, space, **extra):
@@ -96,9 +100,7 @@
 CHUNK = 32
 
 
-def transform_kernel(
-    pairs, tiles, count, recv, own, other, same, rest, out, half, acc, wide
-):
+def transform_kernel(pairs, tiles, count, recv, own, other, out, half, acc, wide):
     regions = recv.shape[0]
     nq = 2 * own.shape[0] * own.shape[2]
     rows = nq * IB
@@ -158,43 +160,18 @@
     wide[...] = jnp.where(
         lanes < LB, low + pltpu.roll(low, LB, 1), high + pltpu.roll(high, LB, 1)
     )
-    flat = jnp.concatenate(
-        [wide[pl.ds(i, nq, stride=IB), :].astype(jnp.bfloat16) for i in range(IB)], axis=1
-    )
-    nall = 2 * same.shape[0]
-    n = lax.broadcasted_iota(jnp.int32, (nq, WIDTH), 0)
-    c = lax.broadcasted_iota(jnp.int32, (nq, WIDTH), 1)
-    at = ((n // 2) % NX) * nq + (y // NL) * (nq // NX) + (n // (2 * NX)) * 2 + n % 2
-    places = [jnp.where(c == at + f * nall, 1.0, 0.0) for f in range(2)]
-    for o, bp in enumerate((same, rest)):
-        partial = lax.dot_general(
-            bp[...], flat, (((1,), (1,)), ((), ())), preferred_element_type=jnp.float32
-        )
-        lines = [
-            jnp.dot(
-                partial,
-                place,
-                preferred_element_type=jnp.float32,
-                precision=lax.Precision.HIGHEST,
-            )
-            for place in places
-        ]
-        for g in range(NG):
-            for v in range(NX):
-                row = 2 * (g * NX + v)
-                out[v * NY + NL * g + (parity ^ o)] = (
-                    lines[0][row : row + 1, :] + lines[1][row + 1 : row + 2, :]
-                )
-
-
-def transform(pairs, tiles, count, recv, own, other, same, rest):
+    for i in range(IB):
+        out[:, i * WIDTH : (i + 1) * WIDTH] = wide[pl.ds(i, nq, stride=IB), :].astype(jnp.bfloat16)
+
+
+def transform(pairs, tiles, count, recv, own, other):
     smem, vmem = pltpu.SMEM, pltpu.VMEM
     regions = recv.shape[0]
     nq = 2 * own.shape[0] * own.shape[2]
     return placed(
         transform_kernel,
-        [smem] * 3 + [vmem] * 5,
-        jax.ShapeDtypeStruct((same.shape[0], 1, 4 * same.shape[0]), jnp.float32),
+        [smem] * 3 + [vmem] * 3,
+        jax.ShapeDtypeStruct((nq, IB * WIDTH), jnp.bfloat16),
         vmem,
         scratch_shapes=[
             pltpu.VMEM((4 * regions, nq * IB, WIDTH), jnp.bfloat16),
@@ -202,8 +179,53 @@
             pltpu.VMEM((nq * IB, WIDTH), jnp.float32),
         ],
         compiler_params=pltpu.CompilerParams(vmem_limit_bytes=40 << 20),
-        cost_estimate=pl.CostEstimate(flops=4 << 30, bytes_accessed=4 << 20, transcendentals=0),
-    )(pairs, tiles, count, recv, own, other, same, rest)
+        cost_estimate=pl.CostEstimate(flops=8 << 30, bytes_accessed=4 << 20, transcendentals=0),
+    )(pairs, tiles, count, recv, own, other)
+
+
+def contract_kernel(flat, *refs):
+    parts, out = refs[:-1], refs[-1]
+    y = member()[1]
+    group = y // NL
+    nq = flat.shape[0]
+    nall = nq * NG
+    partial = lax.dot_general(
+        jnp.concatenate([p[...] for p in parts], axis=0),
+        flat[...],
+        (((1,), (1,)), ((), ())),
+        preferred_element_type=jnp.float32,
+    )
+    n = lax.broadcasted_iota(jnp.int32, (nq, WIDTH), 0)
+    c = lax.broadcasted_iota(jnp.int32, (nq, WIDTH), 1)
+    at = ((n // 2) % NX) * nq + group * (nq // NX) + (n // (2 * NX)) * 2 + n % 2
+    lines = [
+        jnp.dot(
+            partial,
+            jnp.where(c == at + f * nall, 1.0, 0.0),
+            preferred_element_type=jnp.float32,
+            precision=lax.Precision.HIGHEST,
+        )
+        for f in range(2)
+    ]
+    for k, hop in enumerate((0,) + HOPS):
+        pair = (group + NG - hop) % NG
+        for o in range(NL):
+            for v in range(NX):
+                row = (k * NL + o) * 2 * NX + 2 * v
+                out[v * NY + NL * pair + ((y % NL) ^ o)] = (
+                    lines[0][row : row + 1, :] + lines[1][row + 1 : row + 2, :]
+                )
+
+
+def contract(flat, parts):
+    nall = flat.shape[0] * NG
+    return placed(
+        contract_kernel,
+        [pltpu.VMEM] * (1 + len(parts)),
+        jax.ShapeDtypeStruct((nall // 2, 1, 2 * nall), jnp.float32),
+        pltpu.VMEM,
+        compiler_params=pltpu.CompilerParams(vmem_limit_bytes=4 << 20),
+    )(flat, *parts)
 
 
 def total_kernel(parts, out):
@@ -266,16 +288,11 @@
         b = jnp.concatenate([b[:, 0], b[:, 1]], axis=3)
         return b.reshape(NX * per_aux, IB * WIDTH)
 
-    def spread(b):
-        return lax.all_gather(b, "aux", axis=0, tiled=True, axis_index_groups=PAIR_GROUPS)
-
-    same = spread(sliced(own))
-    theirs, same = lax.optimization_barrier((sliced(other), same))
-    rest = spread(theirs)
-
-    partial = transform(
-        term_pairs[0], term_tiles[0], term_count, recv, own, other, same, rest
-    )
+    part = jnp.concatenate([sliced(own), sliced(other)])
+    parts = [part] + [lax.ppermute(part, "aux", onward(hop)) for hop in HOPS]
+
+    flat = transform(term_pairs[0], term_tiles[0], term_count, recv, own, other)
+    partial = contract(flat, parts)
 
     mask_row = jnp.repeat(z_pattern[0], per_aux).astype(jnp.float32)
     weight = 0.5 + 0.125 * laplace_point[0].astype(jnp.float32)

time: 123 us -> 114 us (0.927)
  blocking collectives: 42.1 us -> 11.2 us
  waiting for transfers between devices: 17.1 us -> 28.9 us
  starting transfers between devices: 46.9 us -> 52.7 us
  Pallas kernels: 14 us -> 17.8 us
    all_gather x2 -> x0, blocking collectives: 30.8 us -> none  [spread(): lax.all_gather(b, 'aux', axis=0, tiled=True, axis_index_groups=PAIR_GROUPS)]
    ppermute x0 -> x3, starting transfers between devices: none -> 14.8 us  [per_device(): parts = [part] + [lax.ppermute(part, 'aux', onward(hop)) for hop in HOPS]]
    all_to_all x1, starting transfers between devices: 20.6 us -> 8.15 us  [per_device(): every = lax.all_to_all(total(spread, regions), 'region', 0, 0, tiled=True)]
    ppermute x1, waiting for transfers between devices: 0.01 us -> 8.76 us  [per_device(): other = lax.ppermute(own, 'aux', OTHER)]
    pallas_call x1 -> x2, Pallas kernels: 9.5 us -> 13.3 us  [the longest x1 12.1 us: transform(): placed(transform_kernel, [smem] * 3 + [vmem] * 3, jax.ShapeDtypeStruct((n...]
    all_to_all x1, starting transfers between devices: 6.28 us -> 9.66 us  [per_device(): spread = lax.all_to_all(partial, 'aux', 0, 0, tiled=True)]
    all_to_all x1, waiting for transfers between devices: 0.01 us -> 3.02 us  [per_device(): recv = lax.all_to_all(outgoing, 'region', 0, 0, tiled=True)]
  transfers between devices with their start and end apart: 4 -> 7, of which waited for: 2 -> 4; matrix products, arithmetic and copies ran while one was open for 1% -> 1% of each run, Pallas kernels for 0% -> 11%
where the time goes in v4:
time: 114 us; the launch traced here: 113 us
  starting transfers between devices  52.7 us (46%)
  waiting for transfers between devices  28.9 us (25%)
  Pallas kernels  17.8 us (16%)
  blocking collectives  11.2 us (10%)
  between operations  1.56 us (1%)
    all_to_all x1, starting transfers between devices, per_device(): recv = lax.all_to_all(outgoing, 'region', 0, 0, tiled=True)  16.8 us
    ppermute x3, starting transfers between devices, per_device(): parts = [part] + [lax.ppermute(part, 'aux', onward(hop)) for hop in HOPS]  14.8 us
    pallas_call x1, Pallas kernels, transform(): placed(transform_kernel, [smem] * 3 + [vmem] * 3, jax.ShapeDtypeStruct((n...  12.1 us
    all_gather x1, blocking collectives, per_device(): lax.all_gather(three_index, 'aux', axis=0, tiled=False, axis_index_groups...  11.2 us
    all_to_all x1, starting transfers between devices, per_device(): spread = lax.all_to_all(partial, 'aux', 0, 0, tiled=True)  9.66 us
    all_to_all x1, waiting for transfers between devices, per_device(): every = lax.all_to_all(total(spread, regions), 'region', 0, 0, tiled=True)  9.32 us
    ppermute x1, waiting for transfers between devices, per_device(): other = lax.ppermute(own, 'aux', OTHER)  8.76 us
    all_to_all x1, starting transfers between devices, per_device(): every = lax.all_to_all(total(spread, regions), 'region', 0, 0, tiled=True)  8.15 us
  transfers between devices with their start and end apart: 7, of which 4 were waited for; matrix products, arithmetic and copies ran while one was open for 1% of the time, Pallas kernels for 11%

profile of v4, /device:TPU:1, one launch (start us, length us, event | category | flops | bytes accessed | tf_op | source)
XLA Modules:
  0.0 113.1 jit_solution(4870762429807980020)
XLA Ops:
  0.0 3.2 %shard_map.91 = bf16[24,192,128]{2,1,0:T(8,128)(2,1)} custom-call(s32[2,48]{1,0:T(2,128)} %bitcast.34, bf16[16,128,128]{2,1,0:T(8,128)(2,1)} %occ.1, bf16[16,128,128]{2,1,0:T(8,128)(2,1)} %vir.1), custom_call_target="tpu_custom_call" | custom-call | flops 41943040 | bytes 2097152 | tf_op jit(solution)/shard_map/pallas_call | solution.py:82
  3.2 0.0 copy-start
  3.2 0.0 copy-start.1
  3.3 0.0 copy-start.2
  3.3 16.8 %all-to-all-start = ((bf16[24,192,128]{2,1,0:T(8,128)(2,1)}), bf16[24,192,128]{2,1,0:T(8,128)(2,1)S(1)}, u32[]{:S(2)}, u32[]{:S(2)}) async-start(bf16[24,192,128]{2,1,0:T(8,128)(2,1)} %shard_map.91), calls=%async_computation | async-start | bytes 2359296 | tf_op jit(solution)/shard_map/all_to_all | solution.py:280
  20.1 0.0 copy-done
  20.1 11.2 %all-gather = bf16[8,2,128,128]{3,2,1,0:T(8,128)(2,1)S(1)} all-gather(bf16[2,2,128,128]{3,2,1,0:T(8,128)(2,1)S(1)} %copy-done), channel_id=2, replica_groups={{0,8,16,24},{1,9,17,25},{2,10,18,26},{3,11,19,27},{4,12,20,28},{5,13,21..., dimensions={0}, use_global_device_ids=true | all-gather | bytes 655360 | tf_op jit(solution)/shard_map/all_gather | solution.py:282
  31.4 3.2 %collective-permute-start = (bf16[4,2,2,128,128]{4,3,2,1,0:T(8,128)(2,1)S(1)}, bf16[4,2,2,128,128]{4,3,2,1,0:T(8,128)(2,1)S(1)}, u32[]{:S(2)}, u32[]{:S(2)}) collective-permute-start(bf16[4,2,2,128,128]{4,3,2,1,0:T(8,128)(2,1)S(1)} %bitcast.27), channel_id=1, source_target_pairs={{0,1},{1,0},{2,3},{3,2},{4,5},{5,4},{6,7},{7,6},{8,9},{9,8},{10,11... | collective-permute-start | bytes 1572872 | tf_op jit(solution)/shard_map/ppermute | solution.py:283
  34.6 0.0 copy-done.1
  34.6 0.1 copy.18
  34.7 0.0 copy-done.2
  34.7 0.1 copy.19
  35.5 0.1 dynamic-slice_bitcast_fusion.3
  35.6 0.1 pad_maximum_fusion
  35.8 8.8 %collective-permute-done.other = bf16[4,2,2,128,128]{4,3,2,1,0:T(8,128)(2,1)S(1)} collective-permute-done((bf16[4,2,2,128,128]{4,3,2,1,0:T(8,128)(2,1)S(1)}, bf16[4,2,2,128,128]{4,3,2,1,0:T(8,128)(2,1)S(1)}, u32[]{:S(2)}, u32[]{:S(2)}) %collective-permute-start) | collective-permute-done | bytes 524320 | tf_op jit(solution)/shard_map/ppermute | solution.py:283
  44.5 0.1 dynamic-slice_bitcast_fusion.1
  44.7 0.1 pad_maximum_fusion.1
  44.8 7.5 %collective-permute-start.1 = (bf16[16,4096]{1,0:T(8,128)(2,1)S(1)}, bf16[16,4096]{1,0:T(8,128)(2,1)S(1)}, u32[]{:S(2)}, u32[]{:S(2)}) collective-permute-start(bf16[16,4096]{1,0:T(8,128)(2,1)S(1)} %bitcast_dynamic-update-slice_fusion.refs_0_), channel_id=1, source_target_pairs={{0,4},{1,5},{2,6},{3,7},{4,0},{5,1},{6,2},{7,3},{8,12},{9,13},{10,... | collective-permute-start | bytes 393224 | tf_op jit(solution)/shard_map/ppermute | solution.py:292
  52.2 2.4 %collective-permute-start.2 = (bf16[16,4096]{1,0:T(8,128)(2,1)S(1)}, bf16[16,4096]{1,0:T(8,128)(2,1)S(1)}, u32[]{:S(2)}, u32[]{:S(2)}) collective-permute-start(bf16[16,4096]{1,0:T(8,128)(2,1)S(1)} %bitcast_dynamic-update-slice_fusion.refs_0_), channel_id=1, source_target_pairs={{0,2},{1,3},{2,4},{3,5},{4,6},{5,7},{6,0},{7,1},{8,10},{9,11},{10,... | collective-permute-start | bytes 393224 | tf_op jit(solution)/shard_map/ppermute | solution.py:292
  54.7 5.0 %collective-permute-start.3 = (bf16[16,4096]{1,0:T(8,128)(2,1)S(1)}, bf16[16,4096]{1,0:T(8,128)(2,1)S(1)}, u32[]{:S(2)}, u32[]{:S(2)}) collective-permute-start(bf16[16,4096]{1,0:T(8,128)(2,1)S(1)} %bitcast_dynamic-update-slice_fusion.refs_0_), channel_id=1, source_target_pairs={{0,6},{1,7},{2,0},{3,1},{4,2},{5,3},{6,4},{7,5},{8,14},{9,15},{10,... | collective-permute-start | bytes 393224 | tf_op jit(solution)/shard_map/ppermute | solution.py:292
  59.7 3.0 %all-to-all-done.recv = bf16[24,192,128]{2,1,0:T(8,128)(2,1)S(1)} async-done(((bf16[24,192,128]{2,1,0:T(8,128)(2,1)}), bf16[24,192,128]{2,1,0:T(8,128)(2,1)S(1)}, u32[]{:S(2)}, u32[]{:S(2)}) %all-to-all-start) | async-done | bytes 1179680 | tf_op jit(solution)/shard_map/all_to_all | solution.py:280
  62.7 0.0 copy-start.3
  62.7 12.1 %shard_map.92.flat = bf16[16,4096]{1,0:T(8,128)(2,1)S(1)} custom-call(s32[128,2]{1,0:T(8,128)S(1)} %bitcast.30, s32[128,2]{1,0:T(8,128)S(1)} %bitcast.31, s32[1]{0:T(128)S(6)} %copy.29.count, bf16[24,192,128]{2,1,0:T(8,128)(2,1)S(1)} %all-to-all-done.recv, bf16[4,2,2,128,128]{4,3,2,1,0:T(8,128)(2,1)S(1)} %bitcast.29, ...), custom_call_target="tpu_custom_call" | custom-call | flops 8589934592 | bytes 4194304 | tf_op jit(solution)/shard_map/pallas_call | solution.py:171
  74.8 0.0 collective-permute-done.1.refs_1_
  74.8 0.0 collective-permute-done.2.refs_2_
  74.8 0.0 collective-permute-done.3.refs_3_
  74.8 1.1 %shard_map.93 = f32[32,1,128]{2,1,0:T(1,128)} custom-call(bf16[16,4096]{1,0:T(8,128)(2,1)S(1)} %shard_map.92.flat, bf16[16,4096]{1,0:T(8,128)(2,1)S(1)} %bitcast_dynamic-update-slice_fusion.refs_0_, bf16[16,4096]{1,0:T(8,128)(2,1)S(1)} %collective-permute-done.1.refs_1_, bf16[16,4096]{1,0:T(8,128)(2,1)S(1)} %collective-permute-done.2.refs_2_, ...), custom_call_target="tpu_custom_call" | custom-call | tf_op jit(solution)/shard_map/pallas_call | solution.py:222
  76.0 9.7 %all-to-all-start.1 = ((f32[32,1,128]{2,1,0:T(1,128)}), f32[32,1,128]{2,1,0:T(1,128)S(1)}, u32[]{:S(2)}, u32[]{:S(2)}) async-start(f32[32,1,128]{2,1,0:T(1,128)} %shard_map.93), calls=%async_computation.1 | async-start | bytes 32768 | tf_op jit(solution)/shard_map/all_to_all | solution.py:302
  85.6 0.0 copy-done.3
  85.7 0.1 broadcast_in_dim.4
  85.7 0.1 concatenate.24
  86.5 7.8 %all-to-all-done.1.parts = f32[32,1,128]{2,1,0:T(1,128)S(1)} async-done(((f32[32,1,128]{2,1,0:T(1,128)}), f32[32,1,128]{2,1,0:T(1,128)S(1)}, u32[]{:S(2)}, u32[]{:S(2)}) %all-to-all-start.1) | async-done | bytes 16416 | tf_op jit(solution)/shard_map/all_to_all | solution.py:302
  94.3 0.6 shard_map.94
  94.9 8.2 %all-to-all-start.2 = ((f32[24,1,128]{2,1,0:T(1,128)}), f32[24,1,128]{2,1,0:T(1,128)S(1)}, u32[]{:S(2)}, u32[]{:S(2)}) async-start(f32[24,1,128]{2,1,0:T(1,128)} %shard_map.94), calls=%async_computation.2 | async-start | bytes 24576 | tf_op jit(solution)/shard_map/all_to_all | solution.py:303
  103.1 0.1 maximum_multiply_fusion.factor
  103.1 9.3 %all-to-all-done.2.parts = f32[24,1,128]{2,1,0:T(1,128)S(1)} async-done(((f32[24,1,128]{2,1,0:T(1,128)}), f32[24,1,128]{2,1,0:T(1,128)S(1)}, u32[]{:S(2)}, u32[]{:S(2)}) %all-to-all-start.2) | async-done | bytes 12320 | tf_op jit(solution)/shard_map/all_to_all | solution.py:303
  112.5 0.7 shard_map.95
  (3 shorter events, 0.1 us)
Async XLA Ops:
  3.2 16.9 %copy-start = (bf16[2,2,128,128]{3,2,1,0:T(8,128)(2,1)S(1)}, bf16[2,2,128,128]{3,2,1,0:T(8,128)(2,1)}, u32[]{:S(2)}) copy-start(bf16[2,2,128,128]{3,2,1,0:T(8,128)(2,1)} %param.11) | copy-start | bytes 393220
  3.2 31.4 %copy-start.1 = (s32[1,128,2]{1,2,0:T(2,128)S(1)}, s32[1,128,2]{1,2,0:T(2,128)}, u32[]{:S(2)}) copy-start(s32[1,128,2]{1,2,0:T(2,128)} %param.13) | copy-start | bytes 3076
  3.3 31.5 %copy-start.2 = (s32[1,128,2]{1,2,0:T(2,128)S(1)}, s32[1,128,2]{1,2,0:T(2,128)}, u32[]{:S(2)}) copy-start(s32[1,128,2]{1,2,0:T(2,128)} %param.14) | copy-start | bytes 3076
  3.3 59.4 %all-to-all-start = ((bf16[24,192,128]{2,1,0:T(8,128)(2,1)}), bf16[24,192,128]{2,1,0:T(8,128)(2,1)S(1)}, u32[]{:S(2)}, u32[]{:S(2)}) async-start(bf16[24,192,128]{2,1,0:T(8,128)(2,1)} %shard_map.91), calls=%async_computation | async-start | bytes 2359296 | tf_op jit(solution)/shard_map/all_to_all | solution.py:280
  31.4 13.2 %collective-permute-start = (bf16[4,2,2,128,128]{4,3,2,1,0:T(8,128)(2,1)S(1)}, bf16[4,2,2,128,128]{4,3,2,1,0:T(8,128)(2,1)S(1)}, u32[]{:S(2)}, u32[]{:S(2)}) collective-permute-start(bf16[4,2,2,128,128]{4,3,2,1,0:T(8,128)(2,1)S(1)} %bitcast.27), channel_id=1, source_target_pairs={{0,1},{1,0},{2,3},{3,2},{4,5},{5,4},{6,7},{7,6},{8,9},{9,8},{10,11... | collective-permute-start | bytes 1572872 | tf_op jit(solution)/shard_map/ppermute | solution.py:283
  44.8 30.0 %collective-permute-start.1 = (bf16[16,4096]{1,0:T(8,128)(2,1)S(1)}, bf16[16,4096]{1,0:T(8,128)(2,1)S(1)}, u32[]{:S(2)}, u32[]{:S(2)}) collective-permute-start(bf16[16,4096]{1,0:T(8,128)(2,1)S(1)} %bitcast_dynamic-update-slice_fusion.refs_0_), channel_id=1, source_target_pairs={{0,4},{1,5},{2,6},{3,7},{4,0},{5,1},{6,2},{7,3},{8,12},{9,13},{10,... | collective-permute-start | bytes 393224 | tf_op jit(solution)/shard_map/ppermute | solution.py:292
  52.2 22.6 %collective-permute-start.2 = (bf16[16,4096]{1,0:T(8,128)(2,1)S(1)}, bf16[16,4096]{1,0:T(8,128)(2,1)S(1)}, u32[]{:S(2)}, u32[]{:S(2)}) collective-permute-start(bf16[16,4096]{1,0:T(8,128)(2,1)S(1)} %bitcast_dynamic-update-slice_fusion.refs_0_), channel_id=1, source_target_pairs={{0,2},{1,3},{2,4},{3,5},{4,6},{5,7},{6,0},{7,1},{8,10},{9,11},{10,... | collective-permute-start | bytes 393224 | tf_op jit(solution)/shard_map/ppermute | solution.py:292
  54.7 20.2 %collective-permute-start.3 = (bf16[16,4096]{1,0:T(8,128)(2,1)S(1)}, bf16[16,4096]{1,0:T(8,128)(2,1)S(1)}, u32[]{:S(2)}, u32[]{:S(2)}) collective-permute-start(bf16[16,4096]{1,0:T(8,128)(2,1)S(1)} %bitcast_dynamic-update-slice_fusion.refs_0_), channel_id=1, source_target_pairs={{0,6},{1,7},{2,0},{3,1},{4,2},{5,3},{6,4},{7,5},{8,14},{9,15},{10,... | collective-permute-start | bytes 393224 | tf_op jit(solution)/shard_map/ppermute | solution.py:292
  62.7 23.0 %copy-start.3 = (s32[1,32]{1,0:T(1,128)S(1)}, s32[1,32]{1,0:T(1,128)}, u32[]{:S(2)}) copy-start(s32[1,32]{1,0:T(1,128)} %param.16) | copy-start | bytes 388
  76.0 18.3 %all-to-all-start.1 = ((f32[32,1,128]{2,1,0:T(1,128)}), f32[32,1,128]{2,1,0:T(1,128)S(1)}, u32[]{:S(2)}, u32[]{:S(2)}) async-start(f32[32,1,128]{2,1,0:T(1,128)} %shard_map.93), calls=%async_computation.1 | async-start | bytes 32768 | tf_op jit(solution)/shard_map/all_to_all | solution.py:302
  94.9 17.6 %all-to-all-start.2 = ((f32[24,1,128]{2,1,0:T(1,128)}), f32[24,1,128]{2,1,0:T(1,128)S(1)}, u32[]{:S(2)}, u32[]{:S(2)}) async-start(f32[24,1,128]{2,1,0:T(1,128)} %shard_map.94), calls=%async_computation.2 | async-start | bytes 24576 | tf_op jit(solution)/shard_map/all_to_all | solution.py:303

commit v5 on v4

--- a/solution.py
+++ b/solution.py
@@ -13,8 +13,10 @@
 WIDTH = 128
 IB = WIDTH // NI
 LB = WIDTH // NL
+KB = WIDTH // 2
 X_GROUPS = [[x * NY + y for x in range(NX)] for y in range(NY)]
 OTHER = [(x * NY + y, x * NY + (y ^ 1)) for x in range(NX) for y in range(NY)]
+X_OTHER = [(x * NY + y, (x ^ 1) * NY + y) for x in range(NX) for y in range(NY)]
 HOPS = (2, 1, NG - 1)
 
 
@@ -44,12 +46,13 @@
     x, y = member()
     row = pl.multiple_of(x * IB, IB)
     col = (y % NL) * LB
+    depth = pl.multiple_of((x % 2) * KB, KB)
     ntile = occ.shape[0]
     copies = [pltpu.make_async_copy(occ.at[:, pl.ds(row, IB), :], rows, sems.at[0])]
     step = ntile // PARTS
     for u in range(PARTS):
         at = pl.ds(u * step, step)
-        copies.append(pltpu.make_async_copy(vir.at[at], tiles.at[at], sems.at[1 + u]))
+        copies.append(pltpu.make_async_copy(vir.at[at, pl.ds(depth, KB), :], tiles.at[at], sems.at[1 + u]))
     for c in copies:
         c.start()
     r = lax.broadcasted_iota(jnp.int32, (2 * WIDTH, WIDTH), 0)
@@ -78,7 +81,7 @@
 
 def pick(lists, occ, vir, regions):
     smem, hbm = pltpu.SMEM, pltpu.HBM
-    shape = (regions, 2 * IB + WIDTH, WIDTH)
+    shape = (regions, 2 * IB + KB, WIDTH)
     return placed(
         pick_kernel,
         [smem, hbm, hbm],
@@ -86,7 +89,7 @@
         hbm,
         scratch_shapes=[
             pltpu.VMEM((occ.shape[0], IB, WIDTH), jnp.bfloat16),
-            pltpu.VMEM(vir.shape, jnp.bfloat16),
+            pltpu.VMEM((vir.shape[0], KB, WIDTH), jnp.bfloat16),
             pltpu.VMEM(shape, jnp.bfloat16),
             pltpu.SemaphoreType.DMA((1 + 2 * PARTS,)),
         ],
@@ -100,14 +103,11 @@
 CHUNK = 32
 
 
-def transform_kernel(pairs, tiles, count, recv, own, other, out, half, acc, wide):
+def first_kernel(recv, own, other, half):
     regions = recv.shape[0]
-    nq = 2 * own.shape[0] * own.shape[2]
-    rows = nq * IB
-    y = member()[1]
-    parity = y % NL
-
-    def first(n, carry):
+    parity = member()[1] % NL
+
+    def step(n, carry):
         q = n // (NX // WIDE)
         at = (n % (NX // WIDE)) * WIDE
         source = jnp.concatenate(
@@ -128,13 +128,34 @@
                             ]
         return carry
 
-    lax.fori_loop(0, 2 * NX // WIDE, first, 0)
+    lax.fori_loop(0, 2 * NX // WIDE, step, 0)
+
+
+def first(recv, own, other):
+    nq = 2 * own.shape[0] * own.shape[2]
+    return placed(
+        first_kernel,
+        [pltpu.VMEM] * 3,
+        jax.ShapeDtypeStruct((4 * recv.shape[0], nq * IB, WIDTH), jnp.bfloat16),
+        pltpu.VMEM,
+        compiler_params=pltpu.CompilerParams(vmem_limit_bytes=4 << 20),
+        cost_estimate=pl.CostEstimate(flops=4 << 30, bytes_accessed=4 << 20, transcendentals=0),
+    )(recv, own, other)
+
+
+def second_kernel(pairs, tiles, count, half, kept, came, out, vir, acc, wide):
+    regions = kept.shape[0]
+    rows = half.shape[1]
+    nq = rows // IB
+    depth = pl.multiple_of((member()[0] % 2) * KB, KB)
+    vir[:, pl.ds(depth, KB), :] = kept[:, 2 * IB :, :]
+    vir[:, pl.ds(KB - depth, KB), :] = came[...]
 
     acc[...] = jnp.zeros_like(acc)
     live = count[0]
     lane = lax.broadcasted_iota(jnp.int32, (WIDTH, 2 * WIDTH), 1) // LB
 
-    def second(n, carry):
+    def step(n, carry):
         lhs = []
         rhs = []
         for u in range(CHUNK):
@@ -143,7 +164,7 @@
             b = tiles[at, 1]
             side = jnp.where(t < live, pairs[at, 0] * NL + b % 2, -1)
             lhs.append(half[pairs[at, 1] * (2 * regions) + tiles[at, 0]])
-            tile = recv[b // 2, 2 * IB :, :]
+            tile = vir[b // 2]
             tile = jnp.concatenate([tile, tile], axis=1)
             rhs.append(jnp.where(lane == side, tile, jnp.zeros_like(tile)))
         acc[...] += jnp.dot(
@@ -153,7 +174,7 @@
         )
         return carry
 
-    lax.fori_loop(0, (live + CHUNK - 1) // CHUNK, second, 0)
+    lax.fori_loop(0, (live + CHUNK - 1) // CHUNK, step, 0)
     low = acc[:, :WIDTH]
     high = acc[:, WIDTH:]
     lanes = lax.broadcasted_iota(jnp.int32, (rows, WIDTH), 1)
@@ -164,23 +185,22 @@
         out[:, i * WIDTH : (i + 1) * WIDTH] = wide[pl.ds(i, nq, stride=IB), :].astype(jnp.bfloat16)
 
 
-def transform(pairs, tiles, count, recv, own, other):
+def second(pairs, tiles, count, half, kept, came):
     smem, vmem = pltpu.SMEM, pltpu.VMEM
-    regions = recv.shape[0]
-    nq = 2 * own.shape[0] * own.shape[2]
-    return placed(
-        transform_kernel,
+    rows = half.shape[1]
+    return placed(
+        second_kernel,
         [smem] * 3 + [vmem] * 3,
-        jax.ShapeDtypeStruct((nq, IB * WIDTH), jnp.bfloat16),
+        jax.ShapeDtypeStruct((rows // IB, IB * WIDTH), jnp.bfloat16),
         vmem,
         scratch_shapes=[
-            pltpu.VMEM((4 * regions, nq * IB, WIDTH), jnp.bfloat16),
-            pltpu.VMEM((nq * IB, 2 * WIDTH), jnp.float32),
-            pltpu.VMEM((nq * IB, WIDTH), jnp.float32),
+            pltpu.VMEM((kept.shape[0], WIDTH, WIDTH), jnp.bfloat16),
+            pltpu.VMEM((rows, 2 * WIDTH), jnp.float32),
+            pltpu.VMEM((rows, WIDTH), jnp.float32),
         ],
-        compiler_params=pltpu.CompilerParams(vmem_limit_bytes=40 << 20),
-        cost_estimate=pl.CostEstimate(flops=8 << 30, bytes_accessed=4 << 20, transcendentals=0),
-    )(pairs, tiles, count, recv, own, other)
+        compiler_params=pltpu.CompilerParams(vmem_limit_bytes=16 << 20),
+        cost_estimate=pl.CostEstimate(flops=4 << 30, bytes_accessed=4 << 20, transcendentals=0),
+    )(pairs, tiles, count, half, kept, came)
 
 
 def contract_kernel(flat, *refs):
@@ -280,25 +300,29 @@
     recv = lax.all_to_all(outgoing, "region", 0, 0, tiled=True)
 
     own = lax.all_gather(three_index, "aux", axis=0, tiled=False, axis_index_groups=X_GROUPS)
-    other = lax.ppermute(own, "aux", OTHER)
-
-    def sliced(b):
+    def sliced(b, side):
         b = lax.dynamic_slice_in_dim(b, x * IB, IB, 3)
-        b = lax.dynamic_slice_in_dim(b, (y % NL) * LB, LB, 4)
+        b = lax.dynamic_slice_in_dim(b, side * LB, LB, 4)
         b = jnp.concatenate([b[:, 0], b[:, 1]], axis=3)
         return b.reshape(NX * per_aux, IB * WIDTH)
 
-    part = jnp.concatenate([sliced(own), sliced(other)])
+    theirs = lax.ppermute(sliced(own, 1 - y % NL), "aux", OTHER)
+    late, theirs = lax.optimization_barrier((own, theirs))
+    other = lax.ppermute(late, "aux", OTHER)
+    part = jnp.concatenate([sliced(own, y % NL), theirs])
     parts = [part] + [lax.ppermute(part, "aux", onward(hop)) for hop in HOPS]
-
-    flat = transform(term_pairs[0], term_tiles[0], term_count, recv, own, other)
-    partial = contract(flat, parts)
 
     mask_row = jnp.repeat(z_pattern[0], per_aux).astype(jnp.float32)
     weight = 0.5 + 0.125 * laplace_point[0].astype(jnp.float32)
     scale = weight / (width * jnp.sqrt(jnp.float32(regions * nterms)))
     factor = jnp.concatenate([mask_row, mask_row])[None] * scale
 
+    came = lax.ppermute(recv[:, 2 * IB :, :], "aux", X_OTHER)
+    half = first(recv, own, other)
+    half, factor = lax.optimization_barrier((half, factor))
+    flat = second(term_pairs[0], term_tiles[0], term_count, half, recv, came)
+    partial = contract(flat, parts)
+
     spread = lax.all_to_all(partial, "aux", 0, 0, tiled=True)
     every = lax.all_to_all(total(spread, regions), "region", 0, 0, tiled=True)
     return finish(every, factor)

time: 114 us -> 113 us (level)
  blocking collectives: 11.2 us -> 53.5 us
  waiting for transfers between devices: 28.9 us -> 2.18 us
  starting transfers between devices: 52.7 us -> 39.6 us
  Pallas kernels: 17.8 us -> 12.5 us
  local copies, waits for them, and re-layouts: 0.72 us -> 2.04 us
    all_to_all x0 -> x2, blocking collectives: none -> 42 us  [the longest x1 28.3 us: per_device(): every = lax.all_to_all(total(spread, regions), 'region', 0, 0, tiled=True)]
    all_to_all x2 -> x0, starting transfers between devices: 17.8 us -> none  [the longest x1 9.66 us: per_device(): spread = lax.all_to_all(partial, 'aux', 0, 0, tiled=True)]
    all_to_all x2 -> x0, waiting for transfers between devices: 17.1 us -> none  [the longest x1 9.32 us: per_device(): every = lax.all_to_all(total(spread, regions), 'region', 0, 0, tiled=True)]
    ppermute x1 -> x3, waiting for transfers between devices: 8.76 us -> 2.17 us  [the longest x1 2.17 us: per_device(): came = lax.ppermute(recv[:, 2 * IB:, :], 'aux', X_OTHER)]
    ppermute x1 -> x3, starting transfers between devices: 3.19 us -> 8.11 us  [the longest x1 3.2 us: per_device(): theirs = lax.ppermute(sliced(own, 1 - y % NL), 'aux', OTHER)]
    pallas_call x1 -> x2, Pallas kernels: 12.1 us -> 8.39 us  [the longest x1 4.43 us: second(): placed(second_kernel, [smem] * 3 + [vmem] * 3, jax.ShapeDtypeStruct((rows...]
    all_to_all x1, waiting for transfers between devices: 3.02 us -> 0.01 us  [per_device(): recv = lax.all_to_all(outgoing, 'region', 0, 0, tiled=True)]
    unnamed x11 -> x4, local copies, waits for them, and re-layouts: 0.27 us -> 1.63 us
  transfers between devices with their start and end apart: 7 -> 7, of which waited for: 4 -> 1; matrix products, arithmetic and copies ran while one was open for 1% -> 3% of each run, Pallas kernels for 11% -> 7%
where the time goes in v5:
time: 113 us; the launch traced here: 112 us
  blocking collectives  53.5 us (47%)
  starting transfers between devices  39.6 us (35%)
  Pallas kernels  12.5 us (11%)
  waiting for transfers between devices  2.18 us (2%)
  local copies, waits for them, and re-layouts  2.04 us (2%)
  between operations  1.55 us (1%)
    all_to_all x1, blocking collectives, per_device(): every = lax.all_to_all(total(spread, regions), 'region', 0, 0, tiled=True)  28.3 us
    all_to_all x1, starting transfers between devices, per_device(): recv = lax.all_to_all(outgoing, 'region', 0, 0, tiled=True)  16.7 us
    ppermute x3, starting transfers between devices, per_device(): parts = [part] + [lax.ppermute(part, 'aux', onward(hop)) for hop in HOPS]  14.8 us
    all_to_all x1, blocking collectives, per_device(): spread = lax.all_to_all(partial, 'aux', 0, 0, tiled=True)  13.8 us
    all_gather x1, blocking collectives, per_device(): lax.all_gather(three_index, 'aux', axis=0, tiled=False, axis_index_groups...  11.5 us
    pallas_call x1, Pallas kernels, second(): placed(second_kernel, [smem] * 3 + [vmem] * 3, jax.ShapeDtypeStruct((rows...  4.43 us
    pallas_call x1, Pallas kernels, first(): placed(first_kernel, [pltpu.VMEM] * 3, jax.ShapeDtypeStruct((4 * recv.sha...  3.95 us
    ppermute x1, starting transfers between devices, per_device(): theirs = lax.ppermute(sliced(own, 1 - y % NL), 'aux', OTHER)  3.2 us
  transfers between devices with their start and end apart: 7, of which 1 were waited for; matrix products, arithmetic and copies ran while one was open for 3% of the time, Pallas kernels for 7%

profile of v5, /device:TPU:1, one launch (start us, length us, event | category | flops | bytes accessed | tf_op | source)
XLA Modules:
  0.0 112.2 jit_solution(10856530048370327165)
XLA Ops:
  0.0 2.9 %shard_map.91 = bf16[24,128,128]{2,1,0:T(8,128)(2,1)} custom-call(s32[2,48]{1,0:T(2,128)} %bitcast.36, bf16[16,128,128]{2,1,0:T(8,128)(2,1)} %occ.1, bf16[16,128,128]{2,1,0:T(8,128)(2,1)} %vir.1), custom_call_target="tpu_custom_call" | custom-call | flops 41943040 | bytes 2097152 | tf_op jit(solution)/shard_map/pallas_call | solution.py:85
  2.9 16.7 %all-to-all-start = ((bf16[24,128,128]{2,1,0:T(8,128)(2,1)}), bf16[24,128,128]{2,1,0:T(8,128)(2,1)S(1)}, u32[]{:S(2)}, u32[]{:S(2)}) async-start(bf16[24,128,128]{2,1,0:T(8,128)(2,1)} %shard_map.91), calls=%async_computation | async-start | bytes 1572864 | tf_op jit(solution)/shard_map/all_to_all | solution.py:300
  19.6 11.5 %all-gather = bf16[8,2,128,128]{3,2,1,0:T(8,128)(2,1)S(1)} all-gather(bf16[2,2,128,128]{3,2,1,0:T(8,128)(2,1)} %param.11), channel_id=2, replica_groups={{0,8,16,24},{1,9,17,25},{2,10,18,26},{3,11,19,27},{4,12,20,28},{5,13,21..., dimensions={0}, use_global_device_ids=true | all-gather | bytes 655360 | tf_op jit(solution)/shard_map/all_gather | solution.py:302
  31.1 0.2 dynamic-slice_bitcast_fusion.1
  31.3 0.1 pad_maximum_fusion
  31.5 3.2 %collective-permute-start = (bf16[8,4096]{1,0:T(8,128)(2,1)S(1)}, bf16[8,4096]{1,0:T(8,128)(2,1)S(1)}, u32[]{:S(2)}, u32[]{:S(2)}) collective-permute-start(bf16[8,4096]{1,0:T(8,128)(2,1)S(1)} %bitcast.35), channel_id=1, source_target_pairs={{0,1},{1,0},{2,3},{3,2},{4,5},{5,4},{6,7},{7,6},{8,9},{9,8},{10,11... | collective-permute-start | bytes 196616 | tf_op jit(solution)/shard_map/ppermute | solution.py:309
  34.7 0.7 convert_bitcast_fusion
  35.4 0.1 broadcast_in_dim.4
  35.4 0.1 concatenate.22
  36.2 0.8 copy.18
  37.0 0.8 copy.19
  38.4 0.0 collective-permute-done
  38.4 2.1 %collective-permute-start.1 = (bf16[4,2,2,128,128]{4,3,2,1,0:T(8,128)(2,1)S(1)}, bf16[4,2,2,128,128]{4,3,2,1,0:T(8,128)(2,1)S(1)}, u32[]{:S(2)}, u32[]{:S(2)}) collective-permute-start(bf16[4,2,2,128,128]{4,3,2,1,0:T(8,128)(2,1)S(1)} %bitcast.29), channel_id=1, source_target_pairs={{0,1},{1,0},{2,3},{3,2},{4,5},{5,4},{6,7},{7,6},{8,9},{9,8},{10,11... | collective-permute-start | bytes 1572872 | tf_op jit(solution)/shard_map/ppermute | solution.py:311
  40.5 0.1 maximum_multiply_fusion.factor
  40.6 7.4 %collective-permute-start.3 = (bf16[16,4096]{1,0:T(8,128)(2,1)S(1)}, bf16[16,4096]{1,0:T(8,128)(2,1)S(1)}, u32[]{:S(2)}, u32[]{:S(2)}) collective-permute-start(bf16[16,4096]{1,0:T(8,128)(2,1)S(1)} %constant_dynamic-update-slice_fusion.refs_0_), channel_id=1, source_target_pairs={{0,4},{1,5},{2,6},{3,7},{4,0},{5,1},{6,2},{7,3},{8,12},{9,13},{10,... | collective-permute-start | bytes 393224 | tf_op jit(solution)/shard_map/ppermute | solution.py:313
  48.1 2.4 %collective-permute-start.4 = (bf16[16,4096]{1,0:T(8,128)(2,1)S(1)}, bf16[16,4096]{1,0:T(8,128)(2,1)S(1)}, u32[]{:S(2)}, u32[]{:S(2)}) collective-permute-start(bf16[16,4096]{1,0:T(8,128)(2,1)S(1)} %constant_dynamic-update-slice_fusion.refs_0_), channel_id=1, source_target_pairs={{0,2},{1,3},{2,4},{3,5},{4,6},{5,7},{6,0},{7,1},{8,10},{9,11},{10,... | collective-permute-start | bytes 393224 | tf_op jit(solution)/shard_map/ppermute | solution.py:313
  50.5 5.0 %collective-permute-start.5 = (bf16[16,4096]{1,0:T(8,128)(2,1)S(1)}, bf16[16,4096]{1,0:T(8,128)(2,1)S(1)}, u32[]{:S(2)}, u32[]{:S(2)}) collective-permute-start(bf16[16,4096]{1,0:T(8,128)(2,1)S(1)} %constant_dynamic-update-slice_fusion.refs_0_), channel_id=1, source_target_pairs={{0,6},{1,7},{2,0},{3,1},{4,2},{5,3},{6,4},{7,5},{8,14},{9,15},{10,... | collective-permute-start | bytes 393224 | tf_op jit(solution)/shard_map/ppermute | solution.py:313
  55.5 0.0 all-to-all-done.recv.kept
  55.5 2.8 %collective-permute-start.2 = (bf16[24,64,128]{2,1,0:T(8,128)(2,1)S(1)}, bf16[24,64,128]{2,1,0:T(8,128)(2,1)S(1)}, u32[]{:S(2)}, u32[]{:S(2)}) collective-permute-start(bf16[24,64,128]{2,1,0:T(8,128)(2,1)S(1)} %slice.20), channel_id=1, source_target_pairs={{0,8},{1,9},{2,10},{3,11},{4,12},{5,13},{6,14},{7,15},{8,0},{9,1},... | collective-permute-start | bytes 1179656 | tf_op jit(solution)/shard_map/ppermute | solution.py:320
  58.3 0.0 collective-permute-done.1.other
  58.4 4.0 %shard_map.92.half = bf16[96,512,128]{2,1,0:T(8,128)(2,1)S(1)} custom-call(bf16[24,128,128]{2,1,0:T(8,128)(2,1)S(1)} %all-to-all-done.recv.kept, bf16[4,2,2,128,128]{4,3,2,1,0:T(8,128)(2,1)S(1)} %bitcast.30, bf16[4,2,2,128,128]{4,3,2,1,0:T(8,128)(2,1)S(1)} %collective-permute-done.1.other), custom_call_target="tpu_custom_call" | custom-call | flops 4294967296 | bytes 4194304 | tf_op jit(solution)/shard_map/pallas_call | solution.py:136
  62.3 2.2 %collective-permute-done.2.came = bf16[24,64,128]{2,1,0:T(8,128)(2,1)S(1)} collective-permute-done((bf16[24,64,128]{2,1,0:T(8,128)(2,1)S(1)}, bf16[24,64,128]{2,1,0:T(8,128)(2,1)S(1)}, u32[]{:S(2)}, u32[]{:S(2)}) %collective-permute-start.2) | collective-permute-done | bytes 393248 | tf_op jit(solution)/shard_map/ppermute | solution.py:320
  64.5 4.4 %shard_map.93.flat = bf16[16,4096]{1,0:T(8,128)(2,1)S(1)} custom-call(s32[128,2]{1,0:T(8,128)S(1)} %bitcast.31, s32[128,2]{1,0:T(8,128)S(1)} %bitcast.32, s32[1]{0:T(128)S(6)} %copy.30.count, bf16[96,512,128]{2,1,0:T(8,128)(2,1)S(1)} %shard_map.92.half, bf16[24,128,128]{2,1,0:T(8,128)(2,1)S(1)} %all-to-all-done.recv.kept, ...), custom_call_target="tpu_custom_call" | custom-call | flops 4294967296 | bytes 4194304 | tf_op jit(solution)/shard_map/pallas_call | solution.py:191
  68.9 0.0 collective-permute-done.3.refs_1_
  68.9 0.0 collective-permute-done.4.refs_2_
  68.9 0.0 collective-permute-done.5.refs_3_
  69.0 0.5 shard_map.94
  69.5 13.8 %all_to_all.15.parts = f32[32,1,128]{2,1,0:T(1,128)S(1)} all-to-all(f32[32,1,128]{2,1,0:T(1,128)S(1)} %shard_map.94), channel_id=1, replica_groups=mesh['region'=24,'aux'=32] {'aux'}, dimensions={0} | all-to-all | bytes 32768 | tf_op jit(solution)/shard_map/all_to_all | solution.py:326
  83.3 28.3 %all_to_all.16.parts = f32[24,1,128]{2,1,0:T(1,128)S(1)} all-to-all(f32[24,1,128]{2,1,0:T(1,128)S(1)} %shard_map.95), channel_id=1, replica_groups=mesh['region'=24,'aux'=32] {'region'}, dimensions={0} | all-to-all | bytes 24576 | tf_op jit(solution)/shard_map/all_to_all | solution.py:327
  111.6 0.7 shard_map.96
  (5 shorter events, 0.1 us)
Async XLA Ops:
  2.9 52.6 %all-to-all-start = ((bf16[24,128,128]{2,1,0:T(8,128)(2,1)}), bf16[24,128,128]{2,1,0:T(8,128)(2,1)S(1)}, u32[]{:S(2)}, u32[]{:S(2)}) async-start(bf16[24,128,128]{2,1,0:T(8,128)(2,1)} %shard_map.91), calls=%async_computation | async-start | bytes 1572864 | tf_op jit(solution)/shard_map/all_to_all | solution.py:300
  31.5 7.0 %collective-permute-start = (bf16[8,4096]{1,0:T(8,128)(2,1)S(1)}, bf16[8,4096]{1,0:T(8,128)(2,1)S(1)}, u32[]{:S(2)}, u32[]{:S(2)}) collective-permute-start(bf16[8,4096]{1,0:T(8,128)(2,1)S(1)} %bitcast.35), channel_id=1, source_target_pairs={{0,1},{1,0},{2,3},{3,2},{4,5},{5,4},{6,7},{7,6},{8,9},{9,8},{10,11... | collective-permute-start | bytes 196616 | tf_op jit(solution)/shard_map/ppermute | solution.py:309
  38.4 19.9 %collective-permute-start.1 = (bf16[4,2,2,128,128]{4,3,2,1,0:T(8,128)(2,1)S(1)}, bf16[4,2,2,128,128]{4,3,2,1,0:T(8,128)(2,1)S(1)}, u32[]{:S(2)}, u32[]{:S(2)}) collective-permute-start(bf16[4,2,2,128,128]{4,3,2,1,0:T(8,128)(2,1)S(1)} %bitcast.29), channel_id=1, source_target_pairs={{0,1},{1,0},{2,3},{3,2},{4,5},{5,4},{6,7},{7,6},{8,9},{9,8},{10,11... | collective-permute-start | bytes 1572872 | tf_op jit(solution)/shard_map/ppermute | solution.py:311
  40.6 28.3 %collective-permute-start.3 = (bf16[16,4096]{1,0:T(8,128)(2,1)S(1)}, bf16[16,4096]{1,0:T(8,128)(2,1)S(1)}, u32[]{:S(2)}, u32[]{:S(2)}) collective-permute-start(bf16[16,4096]{1,0:T(8,128)(2,1)S(1)} %constant_dynamic-update-slice_fusion.refs_0_), channel_id=1, source_target_pairs={{0,4},{1,5},{2,6},{3,7},{4,0},{5,1},{6,2},{7,3},{8,12},{9,13},{10,... | collective-permute-start | bytes 393224 | tf_op jit(solution)/shard_map/ppermute | solution.py:313
  48.1 20.9 %collective-permute-start.4 = (bf16[16,4096]{1,0:T(8,128)(2,1)S(1)}, bf16[16,4096]{1,0:T(8,128)(2,1)S(1)}, u32[]{:S(2)}, u32[]{:S(2)}) collective-permute-start(bf16[16,4096]{1,0:T(8,128)(2,1)S(1)} %constant_dynamic-update-slice_fusion.refs_0_), channel_id=1, source_target_pairs={{0,2},{1,3},{2,4},{3,5},{4,6},{5,7},{6,0},{7,1},{8,10},{9,11},{10,... | collective-permute-start | bytes 393224 | tf_op jit(solution)/shard_map/ppermute | solution.py:313
  50.5 18.5 %collective-permute-start.5 = (bf16[16,4096]{1,0:T(8,128)(2,1)S(1)}, bf16[16,4096]{1,0:T(8,128)(2,1)S(1)}, u32[]{:S(2)}, u32[]{:S(2)}) collective-permute-start(bf16[16,4096]{1,0:T(8,128)(2,1)S(1)} %constant_dynamic-update-slice_fusion.refs_0_), channel_id=1, source_target_pairs={{0,6},{1,7},{2,0},{3,1},{4,2},{5,3},{6,4},{7,5},{8,14},{9,15},{10,... | collective-permute-start | bytes 393224 | tf_op jit(solution)/shard_map/ppermute | solution.py:313
  55.5 9.0 %collective-permute-start.2 = (bf16[24,64,128]{2,1,0:T(8,128)(2,1)S(1)}, bf16[24,64,128]{2,1,0:T(8,128)(2,1)S(1)}, u32[]{:S(2)}, u32[]{:S(2)}) collective-permute-start(bf16[24,64,128]{2,1,0:T(8,128)(2,1)S(1)} %slice.20), channel_id=1, source_target_pairs={{0,8},{1,9},{2,10},{3,11},{4,12},{5,13},{6,14},{7,15},{8,0},{9,1},... | collective-permute-start | bytes 1179656 | tf_op jit(solution)/shard_map/ppermute | solution.py:320

commit v6 on v5

--- a/solution.py
+++ b/solution.py
@@ -17,11 +17,7 @@
 X_GROUPS = [[x * NY + y for x in range(NX)] for y in range(NY)]
 OTHER = [(x * NY + y, x * NY + (y ^ 1)) for x in range(NX) for y in range(NY)]
 X_OTHER = [(x * NY + y, (x ^ 1) * NY + y) for x in range(NX) for y in range(NY)]
-HOPS = (2, 1, NG - 1)
-
-
-def onward(hop):
-    return [(x * NY + y, x * NY + (y + NL * hop) % NY) for x in range(NX) for y in range(NY)]
+Y_GROUPS = [[x * NY + y for y in range(NY)] for x in range(NX)]
 
 
 def placed(body, ins, outs, space, **extra):
@@ -203,21 +199,16 @@
     )(pairs, tiles, count, half, kept, came)
 
 
-def contract_kernel(flat, *refs):
-    parts, out = refs[:-1], refs[-1]
+def contract_kernel(flat, bp, out):
     y = member()[1]
-    group = y // NL
     nq = flat.shape[0]
     nall = nq * NG
     partial = lax.dot_general(
-        jnp.concatenate([p[...] for p in parts], axis=0),
-        flat[...],
-        (((1,), (1,)), ((), ())),
-        preferred_element_type=jnp.float32,
+        bp[...], flat[...], (((1,), (1,)), ((), ())), preferred_element_type=jnp.float32
     )
     n = lax.broadcasted_iota(jnp.int32, (nq, WIDTH), 0)
     c = lax.broadcasted_iota(jnp.int32, (nq, WIDTH), 1)
-    at = ((n // 2) % NX) * nq + group * (nq // NX) + (n // (2 * NX)) * 2 + n % 2
+    at = ((n // 2) % NX) * nq + (y // NL) * (nq // NX) + (n // (2 * NX)) * 2 + n % 2
     lines = [
         jnp.dot(
             partial,
@@ -227,25 +218,21 @@
         )
         for f in range(2)
     ]
-    for k, hop in enumerate((0,) + HOPS):
-        pair = (group + NG - hop) % NG
-        for o in range(NL):
-            for v in range(NX):
-                row = (k * NL + o) * 2 * NX + 2 * v
-                out[v * NY + NL * pair + ((y % NL) ^ o)] = (
-                    lines[0][row : row + 1, :] + lines[1][row + 1 : row + 2, :]
-                )
-
-
-def contract(flat, parts):
+    for v in range(NX):
+        for w in range(NY):
+            row = 2 * (w * NX + v)
+            out[v * NY + w] = lines[0][row : row + 1, :] + lines[1][row + 1 : row + 2, :]
+
+
+def contract(flat, bp):
     nall = flat.shape[0] * NG
     return placed(
         contract_kernel,
-        [pltpu.VMEM] * (1 + len(parts)),
+        [pltpu.VMEM] * 2,
         jax.ShapeDtypeStruct((nall // 2, 1, 2 * nall), jnp.float32),
         pltpu.VMEM,
         compiler_params=pltpu.CompilerParams(vmem_limit_bytes=4 << 20),
-    )(flat, *parts)
+    )(flat, bp)
 
 
 def total_kernel(parts, out):
@@ -294,23 +281,24 @@
     width = occ_tiles.shape[1]
     per_aux = three_index.shape[1]
     nterms = term_pairs.shape[1]
-    x, y = member()
+    x = member()[0]
 
     outgoing = pick(send_lists[0], occ_tiles, vir_tiles, regions)
+
+    outgoing, mine = lax.optimization_barrier((outgoing, three_index))
     recv = lax.all_to_all(outgoing, "region", 0, 0, tiled=True)
-
-    own = lax.all_gather(three_index, "aux", axis=0, tiled=False, axis_index_groups=X_GROUPS)
-    def sliced(b, side):
-        b = lax.dynamic_slice_in_dim(b, x * IB, IB, 3)
-        b = lax.dynamic_slice_in_dim(b, side * LB, LB, 4)
-        b = jnp.concatenate([b[:, 0], b[:, 1]], axis=3)
-        return b.reshape(NX * per_aux, IB * WIDTH)
-
-    theirs = lax.ppermute(sliced(own, 1 - y % NL), "aux", OTHER)
-    late, theirs = lax.optimization_barrier((own, theirs))
-    other = lax.ppermute(late, "aux", OTHER)
-    part = jnp.concatenate([sliced(own, y % NL), theirs])
-    parts = [part] + [lax.ppermute(part, "aux", onward(hop)) for hop in HOPS]
+    own = lax.all_gather(mine, "aux", axis=0, tiled=False, axis_index_groups=X_GROUPS)
+
+    part = lax.dynamic_slice_in_dim(own, x * IB, IB, 3)
+    cut = [
+        jnp.concatenate([part[:, 0, :, :, c : c + LB], part[:, 1, :, :, c : c + LB]], axis=3)
+        for c in range(0, width, LB)
+    ]
+    cut = jnp.stack(cut).reshape(NL, NX * per_aux, IB * WIDTH)
+    sent = jnp.concatenate([cut] * (NY // NL))
+    bp = lax.all_to_all(sent, "aux", 0, 0, tiled=True, axis_index_groups=Y_GROUPS)
+    bp = bp.reshape(NY * NX * per_aux, IB * WIDTH)
+    other = lax.ppermute(own, "aux", OTHER)
 
     mask_row = jnp.repeat(z_pattern[0], per_aux).astype(jnp.float32)
     weight = 0.5 + 0.125 * laplace_point[0].astype(jnp.float32)
@@ -321,7 +309,7 @@
     half = first(recv, own, other)
     half, factor = lax.optimization_barrier((half, factor))
     flat = second(term_pairs[0], term_tiles[0], term_count, half, recv, came)
-    partial = contract(flat, parts)
+    partial = contract(flat, bp)
 
     spread = lax.all_to_all(partial, "aux", 0, 0, tiled=True)
     every = lax.all_to_all(total(spread, regions), "region", 0, 0, tiled=True)

time: 113 us -> 115 us (1.018)
  starting transfers between devices: 39.6 us -> 29.8 us
  waiting for transfers between devices: 2.18 us -> 9.47 us
  local copies, waits for them, and re-layouts: 2.04 us -> 6.95 us
  blocking collectives: 53.5 us -> 49.2 us
  Pallas kernels: 12.5 us -> 16.3 us
    ppermute x5 -> x1, starting transfers between devices: 20.1 us -> 3.19 us  [per_device(): other = lax.ppermute(own, 'aux', OTHER)]
    all_to_all x1, blocking collectives: 28.3 us -> 20.1 us  [per_device(): every = lax.all_to_all(total(spread, regions), 'region', 0, 0, tiled=True)]
    all_to_all x1, waiting for transfers between devices: 0.01 us -> 6.95 us  [per_device(): recv = lax.all_to_all(outgoing, 'region', 0, 0, tiled=True)]
    all_to_all x0 -> x1, starting transfers between devices: none -> 6.82 us  [per_device(): lax.all_to_all(sent, 'aux', 0, 0, tiled=True, axis_index_groups=Y_GROUPS)]
    unnamed x4 -> x9, local copies, waits for them, and re-layouts: 1.63 us -> 5.93 us
    all_to_all x1, blocking collectives: 13.8 us -> 17.6 us  [per_device(): spread = lax.all_to_all(partial, 'aux', 0, 0, tiled=True)]
    pallas_call x1, Pallas kernels: 4.43 us -> 8.27 us  [second(): placed(second_kernel, [smem] * 3 + [vmem] * 3, jax.ShapeDtypeStruct((rows...]
  transfers between devices with their start and end apart: 7 -> 4, of which waited for: 1 -> 2; matrix products, arithmetic and copies ran while one was open for 3% -> 7% of each run, Pallas kernels for 7% -> 11%
where the time goes in v6:
time: 115 us; the launch traced here: 114 us
  blocking collectives  49.2 us (43%)
  starting transfers between devices  29.8 us (26%)
  Pallas kernels  16.3 us (14%)
  waiting for transfers between devices  9.47 us (8%)
  local copies, waits for them, and re-layouts  6.95 us (6%)
  between operations  1.44 us (1%)
    all_to_all x1, blocking collectives, per_device(): every = lax.all_to_all(total(spread, regions), 'region', 0, 0, tiled=True)  20.1 us
    all_to_all x1, blocking collectives, per_device(): spread = lax.all_to_all(partial, 'aux', 0, 0, tiled=True)  17.6 us
    all_to_all x1, starting transfers between devices, per_device(): recv = lax.all_to_all(outgoing, 'region', 0, 0, tiled=True)  16.7 us
    all_gather x1, blocking collectives, per_device(): lax.all_gather(mine, 'aux', axis=0, tiled=False, axis_index_groups=X_GROUPS)  11.5 us
    pallas_call x1, Pallas kernels, second(): placed(second_kernel, [smem] * 3 + [vmem] * 3, jax.ShapeDtypeStruct((rows...  8.27 us
    all_to_all x1, waiting for transfers between devices, per_device(): recv = lax.all_to_all(outgoing, 'region', 0, 0, tiled=True)  6.95 us
    all_to_all x1, starting transfers between devices, per_device(): lax.all_to_all(sent, 'aux', 0, 0, tiled=True, axis_index_groups=Y_GROUPS)  6.82 us
    unnamed x9, local copies, waits for them, and re-layouts  5.93 us
  transfers between devices with their start and end apart: 4, of which 2 were waited for; matrix products, arithmetic and copies ran while one was open for 7% of the time, Pallas kernels for 11%

profile of v6, /device:TPU:1, one launch (start us, length us, event | category | flops | bytes accessed | tf_op | source)
XLA Modules:
  0.0 114.0 jit_solution(11401044868794582896)
XLA Ops:
  0.0 2.9 %shard_map.91 = bf16[24,128,128]{2,1,0:T(8,128)(2,1)} custom-call(s32[2,48]{1,0:T(2,128)} %bitcast.30, bf16[16,128,128]{2,1,0:T(8,128)(2,1)} %occ.1, bf16[16,128,128]{2,1,0:T(8,128)(2,1)} %vir.1), custom_call_target="tpu_custom_call" | custom-call | flops 41943040 | bytes 2097152 | tf_op jit(solution)/shard_map/pallas_call | solution.py:81
  2.9 16.7 %all-to-all-start = ((bf16[24,128,128]{2,1,0:T(8,128)(2,1)}), bf16[24,128,128]{2,1,0:T(8,128)(2,1)S(1)}, u32[]{:S(2)}, u32[]{:S(2)}) async-start(bf16[24,128,128]{2,1,0:T(8,128)(2,1)} %shard_map.91), calls=%async_computation | async-start | bytes 1572864 | tf_op jit(solution)/shard_map/all_to_all | solution.py:289
  19.6 11.5 %all-gather = bf16[8,2,128,128]{3,2,1,0:T(8,128)(2,1)S(1)} all-gather(bf16[2,2,128,128]{3,2,1,0:T(8,128)(2,1)} %param.11), channel_id=2, replica_groups={{0,8,16,24},{1,9,17,25},{2,10,18,26},{3,11,19,27},{4,12,20,28},{5,13,21..., dimensions={0}, use_global_device_ids=true | all-gather | bytes 655360 | tf_op jit(solution)/shard_map/all_gather | solution.py:290
  31.0 3.2 %collective-permute-start = (bf16[4,2,2,128,128]{4,3,2,1,0:T(8,128)(2,1)S(1)}, bf16[4,2,2,128,128]{4,3,2,1,0:T(8,128)(2,1)S(1)}, u32[]{:S(2)}, u32[]{:S(2)}) collective-permute-start(bf16[4,2,2,128,128]{4,3,2,1,0:T(8,128)(2,1)S(1)} %bitcast.25), channel_id=1, source_target_pairs={{0,1},{1,0},{2,3},{3,2},{4,5},{5,4},{6,7},{7,6},{8,9},{9,8},{10,11... | collective-permute-start | bytes 1572872 | tf_op jit(solution)/shard_map/ppermute | solution.py:301
  34.3 0.1 dynamic-slice_bitcast_fusion.1
  34.4 0.1 pad_maximum_fusion
  34.5 0.6 constant_dynamic-update-slice_fusion.7
  35.2 0.6 constant_dynamic-update-slice_fusion.6
  35.8 0.6 constant_dynamic-update-slice_fusion.5
  36.5 0.7 convert_bitcast_fusion
  37.1 0.8 copy.18
  37.9 0.8 copy.19
  39.3 0.1 broadcast_in_dim.4
  39.4 0.1 concatenate.23
  40.2 0.6 constant_dynamic-update-slice_fusion.4
  40.8 0.6 constant_dynamic-update-slice_fusion.3
  41.4 0.6 constant_dynamic-update-slice_fusion.2
  42.0 0.6 constant_dynamic-update-slice_fusion.1
  42.7 0.6 constant_dynamic-update-slice_fusion
  43.3 6.9 %all-to-all-done.recv.kept = bf16[24,128,128]{2,1,0:T(8,128)(2,1)S(1)} async-done(((bf16[24,128,128]{2,1,0:T(8,128)(2,1)}), bf16[24,128,128]{2,1,0:T(8,128)(2,1)S(1)}, u32[]{:S(2)}, u32[]{:S(2)}) %all-to-all-start) | async-done | bytes 786464 | tf_op jit(solution)/shard_map/all_to_all | solution.py:289
  50.2 6.8 %all-to-all-start.1 = ((bf16[8,8,4096]{2,1,0:T(8,128)(2,1)}), bf16[8,8,4096]{2,1,0:T(8,128)(2,1)S(1)}, u32[]{:S(2)}, u32[]{:S(2)}) async-start(bf16[8,8,4096]{2,1,0:T(8,128)(2,1)} %constant_dynamic-update-slice_fusion), calls=%async_computation.1 | async-start | bytes 1048576 | tf_op jit(solution)/shard_map/all_to_all | solution.py:299
  57.1 0.1 maximum_multiply_fusion.factor
  57.2 3.1 %collective-permute-start.1 = (bf16[24,64,128]{2,1,0:T(8,128)(2,1)S(1)}, bf16[24,64,128]{2,1,0:T(8,128)(2,1)S(1)}, u32[]{:S(2)}, u32[]{:S(2)}) collective-permute-start(bf16[24,64,128]{2,1,0:T(8,128)(2,1)S(1)} %slice.20), channel_id=1, source_target_pairs={{0,8},{1,9},{2,10},{3,11},{4,12},{5,13},{6,14},{7,15},{8,0},{9,1},... | collective-permute-start | bytes 1179656 | tf_op jit(solution)/shard_map/ppermute | solution.py:308
  60.3 0.0 collective-permute-done.other
  60.3 3.9 %shard_map.92.half = bf16[96,512,128]{2,1,0:T(8,128)(2,1)S(1)} custom-call(bf16[24,128,128]{2,1,0:T(8,128)(2,1)S(1)} %all-to-all-done.recv.kept, bf16[4,2,2,128,128]{4,3,2,1,0:T(8,128)(2,1)S(1)} %bitcast.27, bf16[4,2,2,128,128]{4,3,2,1,0:T(8,128)(2,1)S(1)} %collective-permute-done.other), custom_call_target="tpu_custom_call" | custom-call | flops 4294967296 | bytes 4194304 | tf_op jit(solution)/shard_map/pallas_call | solution.py:132
  64.3 2.5 %collective-permute-done.1.came = bf16[24,64,128]{2,1,0:T(8,128)(2,1)S(1)} collective-permute-done((bf16[24,64,128]{2,1,0:T(8,128)(2,1)S(1)}, bf16[24,64,128]{2,1,0:T(8,128)(2,1)S(1)}, u32[]{:S(2)}, u32[]{:S(2)}) %collective-permute-start.1) | collective-permute-done | bytes 393248 | tf_op jit(solution)/shard_map/ppermute | solution.py:308
  66.8 8.3 %shard_map.93.flat = bf16[16,4096]{1,0:T(8,128)(2,1)S(1)} custom-call(s32[128,2]{1,0:T(8,128)S(1)} %bitcast.28, s32[128,2]{1,0:T(8,128)S(1)} %bitcast.29, s32[1]{0:T(128)S(6)} %copy.31.count, bf16[96,512,128]{2,1,0:T(8,128)(2,1)S(1)} %shard_map.92.half, bf16[24,128,128]{2,1,0:T(8,128)(2,1)S(1)} %all-to-all-done.recv.kept, ...), custom_call_target="tpu_custom_call" | custom-call | flops 4294967296 | bytes 4194304 | tf_op jit(solution)/shard_map/pallas_call | solution.py:187
  75.1 0.0 all-to-all-done.1
  75.1 0.5 shard_map.94
  75.6 17.6 %all_to_all.20.parts = f32[32,1,128]{2,1,0:T(1,128)S(1)} all-to-all(f32[32,1,128]{2,1,0:T(1,128)S(1)} %shard_map.94), channel_id=1, replica_groups=mesh['region'=24,'aux'=32] {'aux'}, dimensions={0} | all-to-all | bytes 32768 | tf_op jit(solution)/shard_map/all_to_all | solution.py:314
  93.3 20.1 %all_to_all.21.parts = f32[24,1,128]{2,1,0:T(1,128)S(1)} all-to-all(f32[24,1,128]{2,1,0:T(1,128)S(1)} %shard_map.95), channel_id=1, replica_groups=mesh['region'=24,'aux'=32] {'region'}, dimensions={0} | all-to-all | bytes 24576 | tf_op jit(solution)/shard_map/all_to_all | solution.py:315
  113.4 0.7 shard_map.96
  (4 shorter events, 0.1 us)
Async XLA Ops:
  2.9 47.4 %all-to-all-start = ((bf16[24,128,128]{2,1,0:T(8,128)(2,1)}), bf16[24,128,128]{2,1,0:T(8,128)(2,1)S(1)}, u32[]{:S(2)}, u32[]{:S(2)}) async-start(bf16[24,128,128]{2,1,0:T(8,128)(2,1)} %shard_map.91), calls=%async_computation | async-start | bytes 1572864 | tf_op jit(solution)/shard_map/all_to_all | solution.py:289
  31.0 29.3 %collective-permute-start = (bf16[4,2,2,128,128]{4,3,2,1,0:T(8,128)(2,1)S(1)}, bf16[4,2,2,128,128]{4,3,2,1,0:T(8,128)(2,1)S(1)}, u32[]{:S(2)}, u32[]{:S(2)}) collective-permute-start(bf16[4,2,2,128,128]{4,3,2,1,0:T(8,128)(2,1)S(1)} %bitcast.25), channel_id=1, source_target_pairs={{0,1},{1,0},{2,3},{3,2},{4,5},{5,4},{6,7},{7,6},{8,9},{9,8},{10,11... | collective-permute-start | bytes 1572872 | tf_op jit(solution)/shard_map/ppermute | solution.py:301
  50.2 24.8 %all-to-all-start.1 = ((bf16[8,8,4096]{2,1,0:T(8,128)(2,1)}), bf16[8,8,4096]{2,1,0:T(8,128)(2,1)S(1)}, u32[]{:S(2)}, u32[]{:S(2)}) async-start(bf16[8,8,4096]{2,1,0:T(8,128)(2,1)} %constant_dynamic-update-slice_fusion), calls=%async_computation.1 | async-start | bytes 1048576 | tf_op jit(solution)/shard_map/all_to_all | solution.py:299
  57.2 9.6 %collective-permute-start.1 = (bf16[24,64,128]{2,1,0:T(8,128)(2,1)S(1)}, bf16[24,64,128]{2,1,0:T(8,128)(2,1)S(1)}, u32[]{:S(2)}, u32[]{:S(2)}) collective-permute-start(bf16[24,64,128]{2,1,0:T(8,128)(2,1)S(1)} %slice.20), channel_id=1, source_target_pairs={{0,8},{1,9},{2,10},{3,11},{4,12},{5,13},{6,14},{7,15},{8,0},{9,1},... | collective-permute-start | bytes 1179656 | tf_op jit(solution)/shard_map/ppermute | solution.py:308

commit v7 on v5

--- a/solution.py
+++ b/solution.py
@@ -310,7 +310,7 @@
     late, theirs = lax.optimization_barrier((own, theirs))
     other = lax.ppermute(late, "aux", OTHER)
     part = jnp.concatenate([sliced(own, y % NL), theirs])
-    parts = [part] + [lax.ppermute(part, "aux", onward(hop)) for hop in HOPS]
+    parts = [part] + [lax.ppermute(part, "aux", onward(hop)) for hop in HOPS[:2]]
 
     mask_row = jnp.repeat(z_pattern[0], per_aux).astype(jnp.float32)
     weight = 0.5 + 0.125 * laplace_point[0].astype(jnp.float32)
@@ -319,7 +319,8 @@
 
     came = lax.ppermute(recv[:, 2 * IB :, :], "aux", X_OTHER)
     half = first(recv, own, other)
-    half, factor = lax.optimization_barrier((half, factor))
+    half, factor, late = lax.optimization_barrier((half, factor, part))
+    parts.append(lax.ppermute(late, "aux", onward(HOPS[2])))
     flat = second(term_pairs[0], term_tiles[0], term_count, half, recv, came)
     partial = contract(flat, parts)
 

time: 113 us -> 116 us (1.027)
  Pallas kernels: 12.5 us -> 16.3 us
  waiting for transfers between devices: 2.18 us -> 0.02 us
    pallas_call x1, Pallas kernels: 4.43 us -> 8.27 us  [second(): placed(second_kernel, [smem] * 3 + [vmem] * 3, jax.ShapeDtypeStruct((rows...]
    ppermute x1, waiting for transfers between devices: 2.17 us -> 0.01 us  [per_device(): came = lax.ppermute(recv[:, 2 * IB:, :], 'aux', X_OTHER)]
    all_to_all x1, blocking collectives: 13.8 us -> 15 us  [per_device(): spread = lax.all_to_all(partial, 'aux', 0, 0, tiled=True)]
  transfers between devices with their start and end apart: 7 -> 7, of which waited for: 1 -> 0; matrix products, arithmetic and copies ran while one was open for 3% -> 3% of each run, Pallas kernels for 7% -> 11%
where the time goes in v7:
time: 116 us; the launch traced here: 115 us
  blocking collectives  53.8 us (46%)
  starting transfers between devices  40.6 us (35%)
  Pallas kernels  16.3 us (14%)
  local copies, waits for them, and re-layouts  2.04 us (2%)
  between operations  1.56 us (1%)
    all_to_all x1, blocking collectives, per_device(): every = lax.all_to_all(total(spread, regions), 'region', 0, 0, tiled=True)  27.4 us
    all_to_all x1, starting transfers between devices, per_device(): recv = lax.all_to_all(outgoing, 'region', 0, 0, tiled=True)  16.7 us
    all_to_all x1, blocking collectives, per_device(): spread = lax.all_to_all(partial, 'aux', 0, 0, tiled=True)  15 us
    all_gather x1, blocking collectives, per_device(): lax.all_gather(three_index, 'aux', axis=0, tiled=False, axis_index_groups...  11.5 us
    ppermute x2, starting transfers between devices, per_device(): lax.ppermute(part, 'aux', onward(hop))  9.86 us
    pallas_call x1, Pallas kernels, second(): placed(second_kernel, [smem] * 3 + [vmem] * 3, jax.ShapeDtypeStruct((rows...  8.27 us
    ppermute x1, starting transfers between devices, per_device(): parts.append(lax.ppermute(late, 'aux', onward(HOPS[2])))  5.89 us
    pallas_call x1, Pallas kernels, first(): placed(first_kernel, [pltpu.VMEM] * 3, jax.ShapeDtypeStruct((4 * recv.sha...  3.96 us
  transfers between devices with their start and end apart: 7, of which 0 were waited for; matrix products, arithmetic and copies ran while one was open for 3% of the time, Pallas kernels for 11%

profile of v7, /device:TPU:1, one launch (start us, length us, event | category | flops | bytes accessed | tf_op | source)
XLA Modules:
  0.0 115.2 jit_solution(16235708944790394834)
XLA Ops:
  0.0 2.9 %shard_map.91 = bf16[24,128,128]{2,1,0:T(8,128)(2,1)} custom-call(s32[2,48]{1,0:T(2,128)} %bitcast.36, bf16[16,128,128]{2,1,0:T(8,128)(2,1)} %occ.1, bf16[16,128,128]{2,1,0:T(8,128)(2,1)} %vir.1), custom_call_target="tpu_custom_call" | custom-call | flops 41943040 | bytes 2097152 | tf_op jit(solution)/shard_map/pallas_call | solution.py:85
  2.9 16.7 %all-to-all-start = ((bf16[24,128,128]{2,1,0:T(8,128)(2,1)}), bf16[24,128,128]{2,1,0:T(8,128)(2,1)S(1)}, u32[]{:S(2)}, u32[]{:S(2)}) async-start(bf16[24,128,128]{2,1,0:T(8,128)(2,1)} %shard_map.91), calls=%async_computation | async-start | bytes 1572864 | tf_op jit(solution)/shard_map/all_to_all | solution.py:300
  19.6 11.5 %all-gather = bf16[8,2,128,128]{3,2,1,0:T(8,128)(2,1)S(1)} all-gather(bf16[2,2,128,128]{3,2,1,0:T(8,128)(2,1)} %param.11), channel_id=2, replica_groups={{0,8,16,24},{1,9,17,25},{2,10,18,26},{3,11,19,27},{4,12,20,28},{5,13,21..., dimensions={0}, use_global_device_ids=true | all-gather | bytes 655360 | tf_op jit(solution)/shard_map/all_gather | solution.py:302
  31.1 0.2 dynamic-slice_bitcast_fusion.1
  31.3 0.1 pad_maximum_fusion
  31.5 3.2 %collective-permute-start = (bf16[8,4096]{1,0:T(8,128)(2,1)S(1)}, bf16[8,4096]{1,0:T(8,128)(2,1)S(1)}, u32[]{:S(2)}, u32[]{:S(2)}) collective-permute-start(bf16[8,4096]{1,0:T(8,128)(2,1)S(1)} %bitcast.35), channel_id=1, source_target_pairs={{0,1},{1,0},{2,3},{3,2},{4,5},{5,4},{6,7},{7,6},{8,9},{9,8},{10,11... | collective-permute-start | bytes 196616 | tf_op jit(solution)/shard_map/ppermute | solution.py:309
  34.7 0.7 convert_bitcast_fusion
  35.4 0.1 broadcast_in_dim.4
  35.4 0.1 concatenate.22
  36.2 0.8 copy.18
  37.0 0.8 copy.19
  38.4 0.0 collective-permute-done
  38.4 2.1 %collective-permute-start.1 = (bf16[4,2,2,128,128]{4,3,2,1,0:T(8,128)(2,1)S(1)}, bf16[4,2,2,128,128]{4,3,2,1,0:T(8,128)(2,1)S(1)}, u32[]{:S(2)}, u32[]{:S(2)}) collective-permute-start(bf16[4,2,2,128,128]{4,3,2,1,0:T(8,128)(2,1)S(1)} %bitcast.29), channel_id=1, source_target_pairs={{0,1},{1,0},{2,3},{3,2},{4,5},{5,4},{6,7},{7,6},{8,9},{9,8},{10,11... | collective-permute-start | bytes 1572872 | tf_op jit(solution)/shard_map/ppermute | solution.py:311
  40.5 0.1 maximum_multiply_fusion.factor
  40.6 7.4 %collective-permute-start.3 = (bf16[16,4096]{1,0:T(8,128)(2,1)S(1)}, bf16[16,4096]{1,0:T(8,128)(2,1)S(1)}, u32[]{:S(2)}, u32[]{:S(2)}) collective-permute-start(bf16[16,4096]{1,0:T(8,128)(2,1)S(1)} %constant_dynamic-update-slice_fusion.refs_0_), channel_id=1, source_target_pairs={{0,4},{1,5},{2,6},{3,7},{4,0},{5,1},{6,2},{7,3},{8,12},{9,13},{10,... | collective-permute-start | bytes 393224 | tf_op jit(solution)/shard_map/ppermute | solution.py:313
  48.1 2.4 %collective-permute-start.4 = (bf16[16,4096]{1,0:T(8,128)(2,1)S(1)}, bf16[16,4096]{1,0:T(8,128)(2,1)S(1)}, u32[]{:S(2)}, u32[]{:S(2)}) collective-permute-start(bf16[16,4096]{1,0:T(8,128)(2,1)S(1)} %constant_dynamic-update-slice_fusion.refs_0_), channel_id=1, source_target_pairs={{0,2},{1,3},{2,4},{3,5},{4,6},{5,7},{6,0},{7,1},{8,10},{9,11},{10,... | collective-permute-start | bytes 393224 | tf_op jit(solution)/shard_map/ppermute | solution.py:313
  50.5 0.0 all-to-all-done.recv.kept
  50.5 2.9 %collective-permute-start.2 = (bf16[24,64,128]{2,1,0:T(8,128)(2,1)S(1)}, bf16[24,64,128]{2,1,0:T(8,128)(2,1)S(1)}, u32[]{:S(2)}, u32[]{:S(2)}) collective-permute-start(bf16[24,64,128]{2,1,0:T(8,128)(2,1)S(1)} %slice.20), channel_id=1, source_target_pairs={{0,8},{1,9},{2,10},{3,11},{4,12},{5,13},{6,14},{7,15},{8,0},{9,1},... | collective-permute-start | bytes 1179656 | tf_op jit(solution)/shard_map/ppermute | solution.py:320
  53.4 0.0 collective-permute-done.1.other
  53.4 4.0 %shard_map.92.half = bf16[96,512,128]{2,1,0:T(8,128)(2,1)S(1)} custom-call(bf16[24,128,128]{2,1,0:T(8,128)(2,1)S(1)} %all-to-all-done.recv.kept, bf16[4,2,2,128,128]{4,3,2,1,0:T(8,128)(2,1)S(1)} %bitcast.30, bf16[4,2,2,128,128]{4,3,2,1,0:T(8,128)(2,1)S(1)} %collective-permute-done.1.other), custom_call_target="tpu_custom_call" | custom-call | flops 4294967296 | bytes 4194304 | tf_op jit(solution)/shard_map/pallas_call | solution.py:136
  57.4 5.9 %collective-permute-start.5 = (bf16[16,4096]{1,0:T(8,128)(2,1)S(1)}, bf16[16,4096]{1,0:T(8,128)(2,1)S(1)}, u32[]{:S(2)}, u32[]{:S(2)}) collective-permute-start(bf16[16,4096]{1,0:T(8,128)(2,1)S(1)} %constant_dynamic-update-slice_fusion.refs_0_), channel_id=1, source_target_pairs={{0,6},{1,7},{2,0},{3,1},{4,2},{5,3},{6,4},{7,5},{8,14},{9,15},{10,... | collective-permute-start | bytes 393224 | tf_op jit(solution)/shard_map/ppermute | solution.py:323
  63.3 0.0 collective-permute-done.2.came
  63.3 8.3 %shard_map.93.flat = bf16[16,4096]{1,0:T(8,128)(2,1)S(1)} custom-call(s32[128,2]{1,0:T(8,128)S(1)} %bitcast.31, s32[128,2]{1,0:T(8,128)S(1)} %bitcast.32, s32[1]{0:T(128)S(6)} %copy.30.count, bf16[96,512,128]{2,1,0:T(8,128)(2,1)S(1)} %shard_map.92.half, bf16[24,128,128]{2,1,0:T(8,128)(2,1)S(1)} %all-to-all-done.recv.kept, ...), custom_call_target="tpu_custom_call" | custom-call | flops 4294967296 | bytes 4194304 | tf_op jit(solution)/shard_map/pallas_call | solution.py:191
  71.6 0.0 collective-permute-done.3.refs_1_
  71.6 0.0 collective-permute-done.4.refs_2_
  71.6 0.0 collective-permute-done.5.refs_3_
  71.6 0.5 shard_map.94
  72.1 15.0 %all_to_all.15.parts = f32[32,1,128]{2,1,0:T(1,128)S(1)} all-to-all(f32[32,1,128]{2,1,0:T(1,128)S(1)} %shard_map.94), channel_id=1, replica_groups=mesh['region'=24,'aux'=32] {'aux'}, dimensions={0} | all-to-all | bytes 32768 | tf_op jit(solution)/shard_map/all_to_all | solution.py:327
  87.2 27.4 %all_to_all.16.parts = f32[24,1,128]{2,1,0:T(1,128)S(1)} all-to-all(f32[24,1,128]{2,1,0:T(1,128)S(1)} %shard_map.95), channel_id=1, replica_groups=mesh['region'=24,'aux'=32] {'region'}, dimensions={0} | all-to-all | bytes 24576 | tf_op jit(solution)/shard_map/all_to_all | solution.py:328
  114.5 0.7 shard_map.96
  (5 shorter events, 0.1 us)
Async XLA Ops:
  2.9 47.6 %all-to-all-start = ((bf16[24,128,128]{2,1,0:T(8,128)(2,1)}), bf16[24,128,128]{2,1,0:T(8,128)(2,1)S(1)}, u32[]{:S(2)}, u32[]{:S(2)}) async-start(bf16[24,128,128]{2,1,0:T(8,128)(2,1)} %shard_map.91), calls=%async_computation | async-start | bytes 1572864 | tf_op jit(solution)/shard_map/all_to_all | solution.py:300
  31.5 7.0 %collective-permute-start = (bf16[8,4096]{1,0:T(8,128)(2,1)S(1)}, bf16[8,4096]{1,0:T(8,128)(2,1)S(1)}, u32[]{:S(2)}, u32[]{:S(2)}) collective-permute-start(bf16[8,4096]{1,0:T(8,128)(2,1)S(1)} %bitcast.35), channel_id=1, source_target_pairs={{0,1},{1,0},{2,3},{3,2},{4,5},{5,4},{6,7},{7,6},{8,9},{9,8},{10,11... | collective-permute-start | bytes 196616 | tf_op jit(solution)/shard_map/ppermute | solution.py:309
  38.4 15.0 %collective-permute-start.1 = (bf16[4,2,2,128,128]{4,3,2,1,0:T(8,128)(2,1)S(1)}, bf16[4,2,2,128,128]{4,3,2,1,0:T(8,128)(2,1)S(1)}, u32[]{:S(2)}, u32[]{:S(2)}) collective-permute-start(bf16[4,2,2,128,128]{4,3,2,1,0:T(8,128)(2,1)S(1)} %bitcast.29), channel_id=1, source_target_pairs={{0,1},{1,0},{2,3},{3,2},{4,5},{5,4},{6,7},{7,6},{8,9},{9,8},{10,11... | collective-permute-start | bytes 1572872 | tf_op jit(solution)/shard_map/ppermute | solution.py:311
  40.6 31.0 %collective-permute-start.3 = (bf16[16,4096]{1,0:T(8,128)(2,1)S(1)}, bf16[16,4096]{1,0:T(8,128)(2,1)S(1)}, u32[]{:S(2)}, u32[]{:S(2)}) collective-permute-start(bf16[16,4096]{1,0:T(8,128)(2,1)S(1)} %constant_dynamic-update-slice_fusion.refs_0_), channel_id=1, source_target_pairs={{0,4},{1,5},{2,6},{3,7},{4,0},{5,1},{6,2},{7,3},{8,12},{9,13},{10,... | collective-permute-start | bytes 393224 | tf_op jit(solution)/shard_map/ppermute | solution.py:313
  48.1 23.5 %collective-permute-start.4 = (bf16[16,4096]{1,0:T(8,128)(2,1)S(1)}, bf16[16,4096]{1,0:T(8,128)(2,1)S(1)}, u32[]{:S(2)}, u32[]{:S(2)}) collective-permute-start(bf16[16,4096]{1,0:T(8,128)(2,1)S(1)} %constant_dynamic-update-slice_fusion.refs_0_), channel_id=1, source_target_pairs={{0,2},{1,3},{2,4},{3,5},{4,6},{5,7},{6,0},{7,1},{8,10},{9,11},{10,... | collective-permute-start | bytes 393224 | tf_op jit(solution)/shard_map/ppermute | solution.py:313
  50.5 12.7 %collective-permute-start.2 = (bf16[24,64,128]{2,1,0:T(8,128)(2,1)S(1)}, bf16[24,64,128]{2,1,0:T(8,128)(2,1)S(1)}, u32[]{:S(2)}, u32[]{:S(2)}) collective-permute-start(bf16[24,64,128]{2,1,0:T(8,128)(2,1)S(1)} %slice.20), channel_id=1, source_target_pairs={{0,8},{1,9},{2,10},{3,11},{4,12},{5,13},{6,14},{7,15},{8,0},{9,1},... | collective-permute-start | bytes 1179656 | tf_op jit(solution)/shard_map/ppermute | solution.py:320
  57.4 14.2 %collective-permute-start.5 = (bf16[16,4096]{1,0:T(8,128)(2,1)S(1)}, bf16[16,4096]{1,0:T(8,128)(2,1)S(1)}, u32[]{:S(2)}, u32[]{:S(2)}) collective-permute-start(bf16[16,4096]{1,0:T(8,128)(2,1)S(1)} %constant_dynamic-update-slice_fusion.refs_0_), channel_id=1, source_target_pairs={{0,6},{1,7},{2,0},{3,1},{4,2},{5,3},{6,4},{7,5},{8,14},{9,15},{10,... | collective-permute-start | bytes 393224 | tf_op jit(solution)/shard_map/ppermute | solution.py:323

commit v8 on v5

--- a/solution.py
+++ b/solution.py
@@ -161,9 +161,9 @@
         for u in range(CHUNK):
             t = n * CHUNK + u
             at = jnp.minimum(t, live - 1)
-            b = tiles[at, 1]
-            side = jnp.where(t < live, pairs[at, 0] * NL + b % 2, -1)
-            lhs.append(half[pairs[at, 1] * (2 * regions) + tiles[at, 0]])
+            b = tiles[1, at]
+            side = jnp.where(t < live, pairs[0, at] * NL + b % 2, -1)
+            lhs.append(half[pairs[1, at] * (2 * regions) + tiles[0, at]])
             tile = vir[b // 2]
             tile = jnp.concatenate([tile, tile], axis=1)
             rhs.append(jnp.where(lane == side, tile, jnp.zeros_like(tile)))
@@ -320,7 +320,7 @@
     came = lax.ppermute(recv[:, 2 * IB :, :], "aux", X_OTHER)
     half = first(recv, own, other)
     half, factor = lax.optimization_barrier((half, factor))
-    flat = second(term_pairs[0], term_tiles[0], term_count, half, recv, came)
+    flat = second(term_pairs[0].T, term_tiles[0].T, term_count, half, recv, came)
     partial = contract(flat, parts)
 
     spread = lax.all_to_all(partial, "aux", 0, 0, tiled=True)

time: 113 us -> 109 us (0.965)
  Pallas kernels: 12.5 us -> 10.5 us
  local copies, waits for them, and re-layouts: 2.04 us -> 0.47 us
    pallas_call x1, Pallas kernels: 4.43 us -> 2.3 us  [second(): placed(second_kernel, [smem] * 3 + [vmem] * 3, jax.ShapeDtypeStruct((rows...]
    all_to_all x1, blocking collectives: 13.8 us -> 15.7 us  [per_device(): spread = lax.all_to_all(partial, 'aux', 0, 0, tiled=True)]
    unnamed x4 -> x6, local copies, waits for them, and re-layouts: 1.63 us -> 0.06 us
    all_to_all x1, blocking collectives: 28.3 us -> 26.9 us  [per_device(): every = lax.all_to_all(total(spread, regions), 'region', 0, 0, tiled=True)]
  transfers between devices with their start and end apart: 7 -> 7, of which waited for: 1 -> 1; matrix products, arithmetic and copies ran while one was open for 3% -> 1% of each run, Pallas kernels for 7% -> 6%
where the time goes in v8:
time: 109 us
  blocking collectives  54 us (50%)
  starting transfers between devices  39.8 us (37%)
  Pallas kernels  10.5 us (10%)
  waiting for transfers between devices  1.72 us (2%)
  between operations  1.54 us (1%)
    all_to_all x1, blocking collectives, per_device(): every = lax.all_to_all(total(spread, regions), 'region', 0, 0, tiled=True)  26.9 us
    all_to_all x1, starting transfers between devices, per_device(): recv = lax.all_to_all(outgoing, 'region', 0, 0, tiled=True)  16.7 us
    all_to_all x1, blocking collectives, per_device(): spread = lax.all_to_all(partial, 'aux', 0, 0, tiled=True)  15.7 us
    ppermute x3, starting transfers between devices, per_device(): parts = [part] + [lax.ppermute(part, 'aux', onward(hop)) for hop in HOPS]  13.9 us
    all_gather x1, blocking collectives, per_device(): lax.all_gather(three_index, 'aux', axis=0, tiled=False, axis_index_groups...  11.5 us
    pallas_call x1, Pallas kernels, first(): placed(first_kernel, [pltpu.VMEM] * 3, jax.ShapeDtypeStruct((4 * recv.sha...  3.96 us
    ppermute x1, starting transfers between devices, per_device(): theirs = lax.ppermute(sliced(own, 1 - y % NL), 'aux', OTHER)  3.2 us
    ppermute x1, starting transfers between devices, per_device(): other = lax.ppermute(late, 'aux', OTHER)  3.09 us
  transfers between devices with their start and end apart: 7, of which 1 were waited for; matrix products, arithmetic and copies ran while one was open for 1% of the time, Pallas kernels for 6%

profile of v8, /device:TPU:1, one launch (start us, length us, event | category | flops | bytes accessed | tf_op | source)
XLA Modules:
  0.0 108.9 jit_solution(15470940908919599766)
XLA Ops:
  0.0 0.0 copy-start
  0.0 0.0 copy-start.1
  0.0 3.0 %shard_map.91 = bf16[24,128,128]{2,1,0:T(8,128)(2,1)} custom-call(s32[2,48]{1,0:T(2,128)} %bitcast.40, bf16[16,128,128]{2,1,0:T(8,128)(2,1)} %occ.1, bf16[16,128,128]{2,1,0:T(8,128)(2,1)} %vir.1), custom_call_target="tpu_custom_call" | custom-call | flops 41943040 | bytes 2097152 | tf_op jit(solution)/shard_map/pallas_call | solution.py:85
  3.0 16.7 %all-to-all-start = ((bf16[24,128,128]{2,1,0:T(8,128)(2,1)}), bf16[24,128,128]{2,1,0:T(8,128)(2,1)S(1)}, u32[]{:S(2)}, u32[]{:S(2)}) async-start(bf16[24,128,128]{2,1,0:T(8,128)(2,1)} %shard_map.91), calls=%async_computation | async-start | bytes 1572864 | tf_op jit(solution)/shard_map/all_to_all | solution.py:300
  19.8 11.5 %all-gather = bf16[8,2,128,128]{3,2,1,0:T(8,128)(2,1)S(1)} all-gather(bf16[2,2,128,128]{3,2,1,0:T(8,128)(2,1)} %param.11), channel_id=2, replica_groups={{0,8,16,24},{1,9,17,25},{2,10,18,26},{3,11,19,27},{4,12,20,28},{5,13,21..., dimensions={0}, use_global_device_ids=true | all-gather | bytes 655360 | tf_op jit(solution)/shard_map/all_gather | solution.py:302
  31.2 0.2 dynamic-slice_bitcast_fusion.1
  31.4 0.1 pad_maximum_fusion
  31.6 3.2 %collective-permute-start = (bf16[8,4096]{1,0:T(8,128)(2,1)S(1)}, bf16[8,4096]{1,0:T(8,128)(2,1)S(1)}, u32[]{:S(2)}, u32[]{:S(2)}) collective-permute-start(bf16[8,4096]{1,0:T(8,128)(2,1)S(1)} %bitcast.39), channel_id=1, source_target_pairs={{0,1},{1,0},{2,3},{3,2},{4,5},{5,4},{6,7},{7,6},{8,9},{9,8},{10,11... | collective-permute-start | bytes 196616 | tf_op jit(solution)/shard_map/ppermute | solution.py:309
  34.8 0.7 convert_bitcast_fusion
  35.5 0.1 broadcast_in_dim.4
  35.6 0.1 concatenate.22
  37.0 0.0 collective-permute-done
  37.0 3.1 %collective-permute-start.1 = (bf16[4,2,2,128,128]{4,3,2,1,0:T(8,128)(2,1)S(1)}, bf16[4,2,2,128,128]{4,3,2,1,0:T(8,128)(2,1)S(1)}, u32[]{:S(2)}, u32[]{:S(2)}) collective-permute-start(bf16[4,2,2,128,128]{4,3,2,1,0:T(8,128)(2,1)S(1)} %bitcast.33), channel_id=1, source_target_pairs={{0,1},{1,0},{2,3},{3,2},{4,5},{5,4},{6,7},{7,6},{8,9},{9,8},{10,11... | collective-permute-start | bytes 1572872 | tf_op jit(solution)/shard_map/ppermute | solution.py:311
  40.1 0.1 maximum_multiply_fusion.factor
  40.2 6.5 %collective-permute-start.3 = (bf16[16,4096]{1,0:T(8,128)(2,1)S(1)}, bf16[16,4096]{1,0:T(8,128)(2,1)S(1)}, u32[]{:S(2)}, u32[]{:S(2)}) collective-permute-start(bf16[16,4096]{1,0:T(8,128)(2,1)S(1)} %constant_dynamic-update-slice_fusion.refs_0_), channel_id=1, source_target_pairs={{0,4},{1,5},{2,6},{3,7},{4,0},{5,1},{6,2},{7,3},{8,12},{9,13},{10,... | collective-permute-start | bytes 393224 | tf_op jit(solution)/shard_map/ppermute | solution.py:313
  46.7 2.4 %collective-permute-start.4 = (bf16[16,4096]{1,0:T(8,128)(2,1)S(1)}, bf16[16,4096]{1,0:T(8,128)(2,1)S(1)}, u32[]{:S(2)}, u32[]{:S(2)}) collective-permute-start(bf16[16,4096]{1,0:T(8,128)(2,1)S(1)} %constant_dynamic-update-slice_fusion.refs_0_), channel_id=1, source_target_pairs={{0,2},{1,3},{2,4},{3,5},{4,6},{5,7},{6,0},{7,1},{8,10},{9,11},{10,... | collective-permute-start | bytes 393224 | tf_op jit(solution)/shard_map/ppermute | solution.py:313
  49.2 5.0 %collective-permute-start.5 = (bf16[16,4096]{1,0:T(8,128)(2,1)S(1)}, bf16[16,4096]{1,0:T(8,128)(2,1)S(1)}, u32[]{:S(2)}, u32[]{:S(2)}) collective-permute-start(bf16[16,4096]{1,0:T(8,128)(2,1)S(1)} %constant_dynamic-update-slice_fusion.refs_0_), channel_id=1, source_target_pairs={{0,6},{1,7},{2,0},{3,1},{4,2},{5,3},{6,4},{7,5},{8,14},{9,15},{10,... | collective-permute-start | bytes 393224 | tf_op jit(solution)/shard_map/ppermute | solution.py:313
  54.1 0.0 all-to-all-done.recv.kept
  54.2 2.8 %collective-permute-start.2 = (bf16[24,64,128]{2,1,0:T(8,128)(2,1)S(1)}, bf16[24,64,128]{2,1,0:T(8,128)(2,1)S(1)}, u32[]{:S(2)}, u32[]{:S(2)}) collective-permute-start(bf16[24,64,128]{2,1,0:T(8,128)(2,1)S(1)} %slice.20), channel_id=1, source_target_pairs={{0,8},{1,9},{2,10},{3,11},{4,12},{5,13},{6,14},{7,15},{8,0},{9,1},... | collective-permute-start | bytes 1179656 | tf_op jit(solution)/shard_map/ppermute | solution.py:320
  57.0 0.0 collective-permute-done.1.other
  57.0 4.0 %shard_map.92.half = bf16[96,512,128]{2,1,0:T(8,128)(2,1)S(1)} custom-call(bf16[24,128,128]{2,1,0:T(8,128)(2,1)S(1)} %all-to-all-done.recv.kept, bf16[4,2,2,128,128]{4,3,2,1,0:T(8,128)(2,1)S(1)} %bitcast.34, bf16[4,2,2,128,128]{4,3,2,1,0:T(8,128)(2,1)S(1)} %collective-permute-done.1.other), custom_call_target="tpu_custom_call" | custom-call | flops 4294967296 | bytes 4194304 | tf_op jit(solution)/shard_map/pallas_call | solution.py:136
  61.0 1.7 %collective-permute-done.2.came = bf16[24,64,128]{2,1,0:T(8,128)(2,1)S(1)} collective-permute-done((bf16[24,64,128]{2,1,0:T(8,128)(2,1)S(1)}, bf16[24,64,128]{2,1,0:T(8,128)(2,1)S(1)}, u32[]{:S(2)}, u32[]{:S(2)}) %collective-permute-start.2) | collective-permute-done | bytes 393248 | tf_op jit(solution)/shard_map/ppermute | solution.py:320
  62.7 0.0 copy-done
  62.7 0.0 copy-done.1
  62.7 2.3 %shard_map.93.flat = bf16[16,4096]{1,0:T(8,128)(2,1)S(1)} custom-call(s32[2,128]{1,0:T(2,128)S(1)} %bitcast.35, s32[2,128]{1,0:T(2,128)S(1)} %bitcast.36, s32[1]{0:T(128)S(6)} %copy.24.count, bf16[96,512,128]{2,1,0:T(8,128)(2,1)S(1)} %shard_map.92.half, bf16[24,128,128]{2,1,0:T(8,128)(2,1)S(1)} %all-to-all-done.recv.kept, ...), custom_call_target="tpu_custom_call" | custom-call | flops 4294967296 | bytes 4194304 | tf_op jit(solution)/shard_map/pallas_call | solution.py:191
  65.0 0.0 collective-permute-done.3.refs_1_
  65.0 0.0 collective-permute-done.4.refs_2_
  65.0 0.0 collective-permute-done.5.refs_3_
  65.1 0.5 shard_map.94
  65.6 15.7 %all_to_all.15.parts = f32[32,1,128]{2,1,0:T(1,128)S(1)} all-to-all(f32[32,1,128]{2,1,0:T(1,128)S(1)} %shard_map.94), channel_id=1, replica_groups=mesh['region'=24,'aux'=32] {'aux'}, dimensions={0} | all-to-all | bytes 32768 | tf_op jit(solution)/shard_map/all_to_all | solution.py:326
  81.3 26.9 %all_to_all.16.parts = f32[24,1,128]{2,1,0:T(1,128)S(1)} all-to-all(f32[24,1,128]{2,1,0:T(1,128)S(1)} %shard_map.95), channel_id=1, replica_groups=mesh['region'=24,'aux'=32] {'region'}, dimensions={0} | all-to-all | bytes 24576 | tf_op jit(solution)/shard_map/all_to_all | solution.py:327
  108.2 0.7 shard_map.96
  (5 shorter events, 0.1 us)
Async XLA Ops:
  0.0 62.7 %copy-start = (s32[1,128,2]{1,2,0:T(2,128)S(1)}, s32[1,128,2]{1,2,0:T(2,128)}, u32[]{:S(2)}) copy-start(s32[1,128,2]{1,2,0:T(2,128)} %param.13) | copy-start | bytes 3076
  0.0 62.7 %copy-start.1 = (s32[1,128,2]{1,2,0:T(2,128)S(1)}, s32[1,128,2]{1,2,0:T(2,128)}, u32[]{:S(2)}) copy-start(s32[1,128,2]{1,2,0:T(2,128)} %param.14) | copy-start | bytes 3076
  3.0 51.1 %all-to-all-start = ((bf16[24,128,128]{2,1,0:T(8,128)(2,1)}), bf16[24,128,128]{2,1,0:T(8,128)(2,1)S(1)}, u32[]{:S(2)}, u32[]{:S(2)}) async-start(bf16[24,128,128]{2,1,0:T(8,128)(2,1)} %shard_map.91), calls=%async_computation | async-start | bytes 1572864 | tf_op jit(solution)/shard_map/all_to_all | solution.py:300
  31.6 5.4 %collective-permute-start = (bf16[8,4096]{1,0:T(8,128)(2,1)S(1)}, bf16[8,4096]{1,0:T(8,128)(2,1)S(1)}, u32[]{:S(2)}, u32[]{:S(2)}) collective-permute-start(bf16[8,4096]{1,0:T(8,128)(2,1)S(1)} %bitcast.39), channel_id=1, source_target_pairs={{0,1},{1,0},{2,3},{3,2},{4,5},{5,4},{6,7},{7,6},{8,9},{9,8},{10,11... | collective-permute-start | bytes 196616 | tf_op jit(solution)/shard_map/ppermute | solution.py:309
  37.0 20.0 %collective-permute-start.1 = (bf16[4,2,2,128,128]{4,3,2,1,0:T(8,128)(2,1)S(1)}, bf16[4,2,2,128,128]{4,3,2,1,0:T(8,128)(2,1)S(1)}, u32[]{:S(2)}, u32[]{:S(2)}) collective-permute-start(bf16[4,2,2,128,128]{4,3,2,1,0:T(8,128)(2,1)S(1)} %bitcast.33), channel_id=1, source_target_pairs={{0,1},{1,0},{2,3},{3,2},{4,5},{5,4},{6,7},{7,6},{8,9},{9,8},{10,11... | collective-permute-start | bytes 1572872 | tf_op jit(solution)/shard_map/ppermute | solution.py:311
  40.2 24.8 %collective-permute-start.3 = (bf16[16,4096]{1,0:T(8,128)(2,1)S(1)}, bf16[16,4096]{1,0:T(8,128)(2,1)S(1)}, u32[]{:S(2)}, u32[]{:S(2)}) collective-permute-start(bf16[16,4096]{1,0:T(8,128)(2,1)S(1)} %constant_dynamic-update-slice_fusion.refs_0_), channel_id=1, source_target_pairs={{0,4},{1,5},{2,6},{3,7},{4,0},{5,1},{6,2},{7,3},{8,12},{9,13},{10,... | collective-permute-start | bytes 393224 | tf_op jit(solution)/shard_map/ppermute | solution.py:313
  46.7 18.3 %collective-permute-start.4 = (bf16[16,4096]{1,0:T(8,128)(2,1)S(1)}, bf16[16,4096]{1,0:T(8,128)(2,1)S(1)}, u32[]{:S(2)}, u32[]{:S(2)}) collective-permute-start(bf16[16,4096]{1,0:T(8,128)(2,1)S(1)} %constant_dynamic-update-slice_fusion.refs_0_), channel_id=1, source_target_pairs={{0,2},{1,3},{2,4},{3,5},{4,6},{5,7},{6,0},{7,1},{8,10},{9,11},{10,... | collective-permute-start | bytes 393224 | tf_op jit(solution)/shard_map/ppermute | solution.py:313
  49.2 15.9 %collective-permute-start.5 = (bf16[16,4096]{1,0:T(8,128)(2,1)S(1)}, bf16[16,4096]{1,0:T(8,128)(2,1)S(1)}, u32[]{:S(2)}, u32[]{:S(2)}) collective-permute-start(bf16[16,4096]{1,0:T(8,128)(2,1)S(1)} %constant_dynamic-update-slice_fusion.refs_0_), channel_id=1, source_target_pairs={{0,6},{1,7},{2,0},{3,1},{4,2},{5,3},{6,4},{7,5},{8,14},{9,15},{10,... | collective-permute-start | bytes 393224 | tf_op jit(solution)/shard_map/ppermute | solution.py:313
  54.2 8.5 %collective-permute-start.2 = (bf16[24,64,128]{2,1,0:T(8,128)(2,1)S(1)}, bf16[24,64,128]{2,1,0:T(8,128)(2,1)S(1)}, u32[]{:S(2)}, u32[]{:S(2)}) collective-permute-start(bf16[24,64,128]{2,1,0:T(8,128)(2,1)S(1)} %slice.20), channel_id=1, source_target_pairs={{0,8},{1,9},{2,10},{3,11},{4,12},{5,13},{6,14},{7,15},{8,0},{9,1},... | collective-permute-start | bytes 1179656 | tf_op jit(solution)/shard_map/ppermute | solution.py:320

commit v9 on v8

--- a/solution.py
+++ b/solution.py
@@ -199,7 +199,7 @@
             pltpu.VMEM((rows, WIDTH), jnp.float32),
         ],
         compiler_params=pltpu.CompilerParams(vmem_limit_bytes=16 << 20),
-        cost_estimate=pl.CostEstimate(flops=4 << 30, bytes_accessed=4 << 20, transcendentals=0),
+        cost_estimate=pl.CostEstimate(flops=1 << 28, bytes_accessed=1 << 20, transcendentals=0),
     )(pairs, tiles, count, half, kept, came)
 
 
@@ -310,14 +310,16 @@
     late, theirs = lax.optimization_barrier((own, theirs))
     other = lax.ppermute(late, "aux", OTHER)
     part = jnp.concatenate([sliced(own, y % NL), theirs])
-    parts = [part] + [lax.ppermute(part, "aux", onward(hop)) for hop in HOPS]
+    came, late = lax.optimization_barrier((recv[:, 2 * IB :, :], part))
+    came = lax.ppermute(came, "aux", X_OTHER)
+    parts = [part] + [lax.ppermute(part, "aux", onward(hop)) for hop in HOPS[:2]]
+    parts.append(lax.ppermute(late, "aux", onward(HOPS[2])))
 
     mask_row = jnp.repeat(z_pattern[0], per_aux).astype(jnp.float32)
     weight = 0.5 + 0.125 * laplace_point[0].astype(jnp.float32)
     scale = weight / (width * jnp.sqrt(jnp.float32(regions * nterms)))
     factor = jnp.concatenate([mask_row, mask_row])[None] * scale
 
-    came = lax.ppermute(recv[:, 2 * IB :, :], "aux", X_OTHER)
     half = first(recv, own, other)
     half, factor = lax.optimization_barrier((half, factor))
     flat = second(term_pairs[0].T, term_tiles[0].T, term_count, half, recv, came)

time: 109 us -> 106 us (0.972)
  blocking collectives: 54 us -> 46.3 us
  Pallas kernels: 10.5 us -> 14.3 us
  starting transfers between devices: 39.8 us -> 41 us
    all_to_all x1, blocking collectives: 26.9 us -> 19.9 us  [per_device(): every = lax.all_to_all(total(spread, regions), 'region', 0, 0, tiled=True)]
    pallas_call x1, Pallas kernels: 2.3 us -> 6.11 us  [second(): placed(second_kernel, [smem] * 3 + [vmem] * 3, jax.ShapeDtypeStruct((rows...]
    ppermute x4, waiting for transfers between devices: 1.72 us -> 0.01 us  [the longest x2 0.01 us: per_device(): lax.ppermute(part, 'aux', onward(hop))]
    all_to_all x1, waiting for transfers between devices: 0.01 us -> 1.21 us  [per_device(): recv = lax.all_to_all(outgoing, 'region', 0, 0, tiled=True)]
    ppermute x4, starting transfers between devices: 16.8 us -> 18 us  [the longest x2 8.96 us: per_device(): lax.ppermute(part, 'aux', onward(hop))]
  transfers between devices with their start and end apart: 7 -> 7, of which waited for: 1 -> 1; matrix products, arithmetic and copies ran while one was open for 1% -> 1% of each run, Pallas kernels for 6% -> 10%
where the time goes in v9:
time: 106 us
  blocking collectives  46.3 us (44%)
  starting transfers between devices  41 us (39%)
  Pallas kernels  14.3 us (13%)
  between operations  1.55 us (1%)
  waiting for transfers between devices  1.23 us (1%)
    all_to_all x1, blocking collectives, per_device(): every = lax.all_to_all(total(spread, regions), 'region', 0, 0, tiled=True)  19.9 us
    all_to_all x1, starting transfers between devices, per_device(): recv = lax.all_to_all(outgoing, 'region', 0, 0, tiled=True)  16.7 us
    all_to_all x1, blocking collectives, per_device(): spread = lax.all_to_all(partial, 'aux', 0, 0, tiled=True)  15 us
    all_gather x1, blocking collectives, per_device(): lax.all_gather(three_index, 'aux', axis=0, tiled=False, axis_index_groups...  11.5 us
    ppermute x2, starting transfers between devices, per_device(): lax.ppermute(part, 'aux', onward(hop))  8.96 us
    pallas_call x1, Pallas kernels, second(): placed(second_kernel, [smem] * 3 + [vmem] * 3, jax.ShapeDtypeStruct((rows...  6.11 us
    ppermute x1, starting transfers between devices, per_device(): parts.append(lax.ppermute(late, 'aux', onward(HOPS[2])))  5.88 us
    pallas_call x1, Pallas kernels, first(): placed(first_kernel, [pltpu.VMEM] * 3, jax.ShapeDtypeStruct((4 * recv.sha...  3.96 us
  transfers between devices with their start and end apart: 7, of which 1 were waited for; matrix products, arithmetic and copies ran while one was open for 1% of the time, Pallas kernels for 10%

profile of v9, /device:TPU:1, one launch (start us, length us, event | category | flops | bytes accessed | tf_op | source)
XLA Modules:
  0.0 105.7 jit_solution(8445016289433006704)
XLA Ops:
  0.0 0.0 copy-start
  0.0 0.0 copy-start.1
  0.0 3.0 %shard_map.91 = bf16[24,128,128]{2,1,0:T(8,128)(2,1)} custom-call(s32[2,48]{1,0:T(2,128)} %bitcast.40, bf16[16,128,128]{2,1,0:T(8,128)(2,1)} %occ.1, bf16[16,128,128]{2,1,0:T(8,128)(2,1)} %vir.1), custom_call_target="tpu_custom_call" | custom-call | flops 41943040 | bytes 2097152 | tf_op jit(solution)/shard_map/pallas_call | solution.py:85
  3.0 16.7 %all-to-all-start = ((bf16[24,128,128]{2,1,0:T(8,128)(2,1)}), bf16[24,128,128]{2,1,0:T(8,128)(2,1)S(1)}, u32[]{:S(2)}, u32[]{:S(2)}) async-start(bf16[24,128,128]{2,1,0:T(8,128)(2,1)} %shard_map.91), calls=%async_computation | async-start | bytes 1572864 | tf_op jit(solution)/shard_map/all_to_all | solution.py:300
  19.8 11.5 %all-gather = bf16[8,2,128,128]{3,2,1,0:T(8,128)(2,1)S(1)} all-gather(bf16[2,2,128,128]{3,2,1,0:T(8,128)(2,1)} %param.11), channel_id=2, replica_groups={{0,8,16,24},{1,9,17,25},{2,10,18,26},{3,11,19,27},{4,12,20,28},{5,13,21..., dimensions={0}, use_global_device_ids=true | all-gather | bytes 655360 | tf_op jit(solution)/shard_map/all_gather | solution.py:302
  31.2 0.2 dynamic-slice_bitcast_fusion.1
  31.4 0.1 pad_maximum_fusion
  31.6 3.2 %collective-permute-start = (bf16[8,4096]{1,0:T(8,128)(2,1)S(1)}, bf16[8,4096]{1,0:T(8,128)(2,1)S(1)}, u32[]{:S(2)}, u32[]{:S(2)}) collective-permute-start(bf16[8,4096]{1,0:T(8,128)(2,1)S(1)} %bitcast.39), channel_id=1, source_target_pairs={{0,1},{1,0},{2,3},{3,2},{4,5},{5,4},{6,7},{7,6},{8,9},{9,8},{10,11... | collective-permute-start | bytes 196616 | tf_op jit(solution)/shard_map/ppermute | solution.py:309
  34.8 0.7 convert_bitcast_fusion
  35.5 0.1 broadcast_in_dim.4
  35.6 0.1 concatenate.22
  37.0 0.0 collective-permute-done
  37.0 3.1 %collective-permute-start.1 = (bf16[4,2,2,128,128]{4,3,2,1,0:T(8,128)(2,1)S(1)}, bf16[4,2,2,128,128]{4,3,2,1,0:T(8,128)(2,1)S(1)}, u32[]{:S(2)}, u32[]{:S(2)}) collective-permute-start(bf16[4,2,2,128,128]{4,3,2,1,0:T(8,128)(2,1)S(1)} %bitcast.33), channel_id=1, source_target_pairs={{0,1},{1,0},{2,3},{3,2},{4,5},{5,4},{6,7},{7,6},{8,9},{9,8},{10,11... | collective-permute-start | bytes 1572872 | tf_op jit(solution)/shard_map/ppermute | solution.py:311
  40.1 0.1 maximum_multiply_fusion.factor
  40.2 6.5 %collective-permute-start.3 = (bf16[16,4096]{1,0:T(8,128)(2,1)S(1)}, bf16[16,4096]{1,0:T(8,128)(2,1)S(1)}, u32[]{:S(2)}, u32[]{:S(2)}) collective-permute-start(bf16[16,4096]{1,0:T(8,128)(2,1)S(1)} %constant_dynamic-update-slice_fusion.refs_0_), channel_id=1, source_target_pairs={{0,4},{1,5},{2,6},{3,7},{4,0},{5,1},{6,2},{7,3},{8,12},{9,13},{10,... | collective-permute-start | bytes 393224 | tf_op jit(solution)/shard_map/ppermute | solution.py:315
  46.7 2.4 %collective-permute-start.4 = (bf16[16,4096]{1,0:T(8,128)(2,1)S(1)}, bf16[16,4096]{1,0:T(8,128)(2,1)S(1)}, u32[]{:S(2)}, u32[]{:S(2)}) collective-permute-start(bf16[16,4096]{1,0:T(8,128)(2,1)S(1)} %constant_dynamic-update-slice_fusion.refs_0_), channel_id=1, source_target_pairs={{0,2},{1,3},{2,4},{3,5},{4,6},{5,7},{6,0},{7,1},{8,10},{9,11},{10,... | collective-permute-start | bytes 393224 | tf_op jit(solution)/shard_map/ppermute | solution.py:315
  49.2 1.2 %all-to-all-done.recv.kept = bf16[24,128,128]{2,1,0:T(8,128)(2,1)S(1)} async-done(((bf16[24,128,128]{2,1,0:T(8,128)(2,1)}), bf16[24,128,128]{2,1,0:T(8,128)(2,1)S(1)}, u32[]{:S(2)}, u32[]{:S(2)}) %all-to-all-start) | async-done | bytes 786464 | tf_op jit(solution)/shard_map/all_to_all | solution.py:300
  50.4 3.1 %collective-permute-start.2 = (bf16[24,64,128]{2,1,0:T(8,128)(2,1)S(1)}, bf16[24,64,128]{2,1,0:T(8,128)(2,1)S(1)}, u32[]{:S(2)}, u32[]{:S(2)}) collective-permute-start(bf16[24,64,128]{2,1,0:T(8,128)(2,1)S(1)} %slice.20), channel_id=1, source_target_pairs={{0,8},{1,9},{2,10},{3,11},{4,12},{5,13},{6,14},{7,15},{8,0},{9,1},... | collective-permute-start | bytes 1179656 | tf_op jit(solution)/shard_map/ppermute | solution.py:314
  53.5 5.9 %collective-permute-start.5 = (bf16[16,4096]{1,0:T(8,128)(2,1)S(1)}, bf16[16,4096]{1,0:T(8,128)(2,1)S(1)}, u32[]{:S(2)}, u32[]{:S(2)}) collective-permute-start(bf16[16,4096]{1,0:T(8,128)(2,1)S(1)} %constant_dynamic-update-slice_fusion.refs_0_), channel_id=1, source_target_pairs={{0,6},{1,7},{2,0},{3,1},{4,2},{5,3},{6,4},{7,5},{8,14},{9,15},{10,... | collective-permute-start | bytes 393224 | tf_op jit(solution)/shard_map/ppermute | solution.py:316
  59.4 0.0 collective-permute-done.1.other
  59.4 4.0 %shard_map.92.half = bf16[96,512,128]{2,1,0:T(8,128)(2,1)S(1)} custom-call(bf16[24,128,128]{2,1,0:T(8,128)(2,1)S(1)} %all-to-all-done.recv.kept, bf16[4,2,2,128,128]{4,3,2,1,0:T(8,128)(2,1)S(1)} %bitcast.34, bf16[4,2,2,128,128]{4,3,2,1,0:T(8,128)(2,1)S(1)} %collective-permute-done.1.other), custom_call_target="tpu_custom_call" | custom-call | flops 4294967296 | bytes 4194304 | tf_op jit(solution)/shard_map/pallas_call | solution.py:136
  63.4 0.0 collective-permute-done.2.came
  63.4 0.0 copy-done
  63.4 0.0 copy-done.1
  63.4 6.1 %shard_map.93.flat = bf16[16,4096]{1,0:T(8,128)(2,1)S(1)} custom-call(s32[2,128]{1,0:T(2,128)S(1)} %bitcast.35, s32[2,128]{1,0:T(2,128)S(1)} %bitcast.36, s32[1]{0:T(128)S(6)} %copy.24.count, bf16[96,512,128]{2,1,0:T(8,128)(2,1)S(1)} %shard_map.92.half, bf16[24,128,128]{2,1,0:T(8,128)(2,1)S(1)} %all-to-all-done.recv.kept, ...), custom_call_target="tpu_custom_call" | custom-call | flops 268435456 | bytes 1048576 | tf_op jit(solution)/shard_map/pallas_call | solution.py:191
  69.6 0.0 collective-permute-done.3.refs_1_
  69.6 0.0 collective-permute-done.4.refs_2_
  69.6 0.0 collective-permute-done.5.refs_3_
  69.6 0.5 shard_map.94
  70.1 15.0 %all_to_all.15.parts = f32[32,1,128]{2,1,0:T(1,128)S(1)} all-to-all(f32[32,1,128]{2,1,0:T(1,128)S(1)} %shard_map.94), channel_id=1, replica_groups=mesh['region'=24,'aux'=32] {'aux'}, dimensions={0} | all-to-all | bytes 32768 | tf_op jit(solution)/shard_map/all_to_all | solution.py:328
  85.2 19.9 %all_to_all.16.parts = f32[24,1,128]{2,1,0:T(1,128)S(1)} all-to-all(f32[24,1,128]{2,1,0:T(1,128)S(1)} %shard_map.95), channel_id=1, replica_groups=mesh['region'=24,'aux'=32] {'region'}, dimensions={0} | all-to-all | bytes 24576 | tf_op jit(solution)/shard_map/all_to_all | solution.py:329
  105.0 0.7 shard_map.96
  (5 shorter events, 0.1 us)
Async XLA Ops:
  0.0 63.4 %copy-start = (s32[1,128,2]{1,2,0:T(2,128)S(1)}, s32[1,128,2]{1,2,0:T(2,128)}, u32[]{:S(2)}) copy-start(s32[1,128,2]{1,2,0:T(2,128)} %param.13) | copy-start | bytes 3076
  0.0 63.4 %copy-start.1 = (s32[1,128,2]{1,2,0:T(2,128)S(1)}, s32[1,128,2]{1,2,0:T(2,128)}, u32[]{:S(2)}) copy-start(s32[1,128,2]{1,2,0:T(2,128)} %param.14) | copy-start | bytes 3076
  3.0 47.4 %all-to-all-start = ((bf16[24,128,128]{2,1,0:T(8,128)(2,1)}), bf16[24,128,128]{2,1,0:T(8,128)(2,1)S(1)}, u32[]{:S(2)}, u32[]{:S(2)}) async-start(bf16[24,128,128]{2,1,0:T(8,128)(2,1)} %shard_map.91), calls=%async_computation | async-start | bytes 1572864 | tf_op jit(solution)/shard_map/all_to_all | solution.py:300
  31.6 5.4 %collective-permute-start = (bf16[8,4096]{1,0:T(8,128)(2,1)S(1)}, bf16[8,4096]{1,0:T(8,128)(2,1)S(1)}, u32[]{:S(2)}, u32[]{:S(2)}) collective-permute-start(bf16[8,4096]{1,0:T(8,128)(2,1)S(1)} %bitcast.39), channel_id=1, source_target_pairs={{0,1},{1,0},{2,3},{3,2},{4,5},{5,4},{6,7},{7,6},{8,9},{9,8},{10,11... | collective-permute-start | bytes 196616 | tf_op jit(solution)/shard_map/ppermute | solution.py:309
  37.0 22.4 %collective-permute-start.1 = (bf16[4,2,2,128,128]{4,3,2,1,0:T(8,128)(2,1)S(1)}, bf16[4,2,2,128,128]{4,3,2,1,0:T(8,128)(2,1)S(1)}, u32[]{:S(2)}, u32[]{:S(2)}) collective-permute-start(bf16[4,2,2,128,128]{4,3,2,1,0:T(8,128)(2,1)S(1)} %bitcast.33), channel_id=1, source_target_pairs={{0,1},{1,0},{2,3},{3,2},{4,5},{5,4},{6,7},{7,6},{8,9},{9,8},{10,11... | collective-permute-start | bytes 1572872 | tf_op jit(solution)/shard_map/ppermute | solution.py:311
  40.2 29.4 %collective-permute-start.3 = (bf16[16,4096]{1,0:T(8,128)(2,1)S(1)}, bf16[16,4096]{1,0:T(8,128)(2,1)S(1)}, u32[]{:S(2)}, u32[]{:S(2)}) collective-permute-start(bf16[16,4096]{1,0:T(8,128)(2,1)S(1)} %constant_dynamic-update-slice_fusion.refs_0_), channel_id=1, source_target_pairs={{0,4},{1,5},{2,6},{3,7},{4,0},{5,1},{6,2},{7,3},{8,12},{9,13},{10,... | collective-permute-start | bytes 393224 | tf_op jit(solution)/shard_map/ppermute | solution.py:315
  46.7 22.8 %collective-permute-start.4 = (bf16[16,4096]{1,0:T(8,128)(2,1)S(1)}, bf16[16,4096]{1,0:T(8,128)(2,1)S(1)}, u32[]{:S(2)}, u32[]{:S(2)}) collective-permute-start(bf16[16,4096]{1,0:T(8,128)(2,1)S(1)} %constant_dynamic-update-slice_fusion.refs_0_), channel_id=1, source_target_pairs={{0,2},{1,3},{2,4},{3,5},{4,6},{5,7},{6,0},{7,1},{8,10},{9,11},{10,... | collective-permute-start | bytes 393224 | tf_op jit(solution)/shard_map/ppermute | solution.py:315
  50.4 13.0 %collective-permute-start.2 = (bf16[24,64,128]{2,1,0:T(8,128)(2,1)S(1)}, bf16[24,64,128]{2,1,0:T(8,128)(2,1)S(1)}, u32[]{:S(2)}, u32[]{:S(2)}) collective-permute-start(bf16[24,64,128]{2,1,0:T(8,128)(2,1)S(1)} %slice.20), channel_id=1, source_target_pairs={{0,8},{1,9},{2,10},{3,11},{4,12},{5,13},{6,14},{7,15},{8,0},{9,1},... | collective-permute-start | bytes 1179656 | tf_op jit(solution)/shard_map/ppermute | solution.py:314
  53.5 16.0 %collective-permute-start.5 = (bf16[16,4096]{1,0:T(8,128)(2,1)S(1)}, bf16[16,4096]{1,0:T(8,128)(2,1)S(1)}, u32[]{:S(2)}, u32[]{:S(2)}) collective-permute-start(bf16[16,4096]{1,0:T(8,128)(2,1)S(1)} %constant_dynamic-update-slice_fusion.refs_0_), channel_id=1, source_target_pairs={{0,6},{1,7},{2,0},{3,1},{4,2},{5,3},{6,4},{7,5},{8,14},{9,15},{10,... | collective-permute-start | bytes 393224 | tf_op jit(solution)/shard_map/ppermute | solution.py:316
